TPU v7x, 128 devices: a whole 4x4x4 slice. The times are simulated.
128 devices in a mesh: mesh: 128 (over y, z, x, core).
Axes of the slice: x: 4, y: 4, z: 4, core: 2. Of those that a mesh axis runs over, the one named last changes fastest.
Arguments:
- states: float32 [786432, 256], P('mesh'), may hold values from -30 to 30
- inv_sqrt_mass: float32 [786432], P('mesh'), may hold values from 0.25 to 1.75
- element_blocks: bfloat16 [2048, 512, 512], P('mesh'), may hold values from -0.25 to 0.25
- element_nodes: int32 [2048, 512], P('mesh'), may hold values from 0 to 6143, as said below
- element_counts: int32 [128], P('mesh'), may hold values from 1 to 16, as said below
- node_counts: int32 [128], replicated, may hold values from 4608 to 6144, as said below
- boundary_rows: int32 [128, 2, 384], P('mesh'), may hold values from 0 to 4607, as said below
Outputs:
- rotated: float32 [786432, 256], P('mesh')
Inputs may be any that keep to these rules, and one draw needn't show every extreme that they name: `node_counts`: live node rows of each device; some device has 6144. `element_counts`: live element slots of each device (the first slots are live); some device has 16. `element_nodes`: every entry is below its device's node count. `boundary_rows`: for each device the 768 entries are distinct rows below 4608.
All inputs are finite; a program needn't handle non-finite values.
Results may differ from a plain program's by a relative error of at most 0.0077.
Values sent between devices are 32-bit elements; how exact they have to be, the bound alone decides.
No kernel may reach another device: no remote copies, remote signals or barrier semaphores. Data moves between devices by JAX's collectives and lax.ppermute only.
A program may use at most 128 MiB of HBM per device.

v0:
```python
import jax
import jax.numpy as jnp
from jax import lax
from jax.sharding import PartitionSpec as P


def passed_along(block, axis, distance):
    devices = range(lax.axis_size(axis))
    route = [(i - distance, i) for i in devices if i - distance in devices]
    return lax.ppermute(block, axis, route)


def total_of_pieces(value, axis):
    return lax.all_gather(value, axis).sum(0)


def body(
    states, inv_sqrt_mass, element_blocks, element_nodes, element_counts, node_counts, boundary_rows
):
    position = lax.axis_index("mesh")
    devices = lax.axis_size("mesh")
    row_total = states.shape[0]
    width = states.shape[1]
    slots = element_blocks.shape[0]
    lower_rows = boundary_rows[0, 0]
    upper_rows = boundary_rows[0, 1]
    shared = lower_rows.shape[0]
    has_below = position >= 1
    owner_vals, owner_mass = passed_along(
        (states[upper_rows], inv_sqrt_mass[upper_rows]), "mesh", 1
    )
    field = states.at[lower_rows].set(jnp.where(has_below, owner_vals, states[lower_rows]))
    mass = inv_sqrt_mass.at[lower_rows].set(
        jnp.where(has_below, owner_mass, inv_sqrt_mass[lower_rows])
    )
    live_slots = element_counts[0]
    row_index = jnp.arange(row_total)
    slot_index = jnp.arange(slots)
    slot_live = slot_index < live_slots

    def ham(values):
        scaled = (mass[:, None] * values).astype(jnp.bfloat16)
        empty = jnp.zeros((row_total, width), jnp.float32)

        def add_element(slot, total):
            rows = element_nodes[slot]

            def compute(acc):
                part = jnp.dot(
                    element_blocks[slot], scaled[rows], preferred_element_type=jnp.float32
                )
                return acc.at[rows].add(part)

            return lax.cond(slot_live[slot], compute, lambda acc: acc, total)

        local = lax.fori_loop(0, slots, add_element, empty)
        coming_up = passed_along(local[upper_rows], "mesh", 1)
        coming_down = passed_along(local[lower_rows], "mesh", -1)
        assembled = local.at[lower_rows].add(coming_up).at[upper_rows].add(coming_down)
        return mass[:, None] * assembled

    center = 0.5
    half_width = 1.5
    first = (ham(field) - center * field) / half_width
    second = 2.0 * (ham(first) - center * first) / half_width - field
    filtered = 2.0 * (ham(second) - center * second) / half_width - first
    live = row_index < node_counts[position]
    in_lower = jnp.any(row_index[:, None] == lower_rows[None, :], axis=1)
    owned = live & jnp.logical_not(in_lower & has_below)
    weighted = jnp.where(owned[:, None], filtered, 0.0)
    half = width // 2
    left_cols = weighted[:, :half]
    right_cols = weighted[:, half:]
    numbers = (((0,), (0,)), ((), ()))
    top_left = lax.dot_general(
        left_cols,
        left_cols,
        numbers,
        precision=lax.Precision.HIGHEST,
        preferred_element_type=jnp.float32,
    )
    top_right = lax.dot_general(
        left_cols,
        right_cols,
        numbers,
        precision=lax.Precision.HIGHEST,
        preferred_element_type=jnp.float32,
    )
    low_right = lax.dot_general(
        right_cols,
        right_cols,
        numbers,
        precision=lax.Precision.HIGHEST,
        preferred_element_type=jnp.float32,
    )
    summed = total_of_pieces(jnp.stack([top_left, top_right, low_right]), "mesh")
    gram = jnp.concatenate(
        [
            jnp.concatenate([summed[0], summed[1]], axis=1),
            jnp.concatenate([summed[1].T, summed[2]], axis=1),
        ],
        axis=0,
    )
    total = (jnp.sum(node_counts) - shared * (devices - 1)).astype(jnp.float32)
    gram = gram / total
    factor = jnp.linalg.cholesky(gram)
    inverse = jax.scipy.linalg.solve_triangular(
        factor, jnp.eye(width, dtype=jnp.float32), lower=True
    )
    rotated = jnp.dot(
        filtered, inverse.T, precision=lax.Precision.HIGHEST, preferred_element_type=jnp.float32
    )
    return jnp.where(live[:, None], rotated, 0.0)


def solution(mesh):
    in_specs = (
        P("mesh", None),
        P("mesh"),
        P("mesh", None, None),
        P("mesh", None),
        P("mesh"),
        P(),
        P("mesh", None, None),
    )
    out_specs = P("mesh", None)
    return jax.shard_map(body, mesh=mesh, in_specs=in_specs, out_specs=out_specs, check_vma=False)
```

profile of v0, /device:TPU:1, one launch (start us, length us, event | category | flops | bytes accessed | tf_op | source)
XLA Modules:
  0.0 1106.0 jit_solution(11642952865085979069)
XLA Ops:
  32.9 9.9 scatter_custom_fusion.4
  49.3 88.1 %while.49 = (s32[]{:T(128)}, f32[6144,256]{1,0:T(8,128)}, pred[16]{0:T(512)(128)(4,1)S(1)}, s32[16,512]{1,0:T(8,128)}, bf16[16,512,512]{2,1,0:T(8,128)(2,1)}, /*index=5*/bf16[6144,256]{1,0:T(8,128)(2,1)S(1)}, s32[]{:T(128)}) while((s32[]{:T(128)}, f32[6144,256]{1,0:T(8,128)}, pred[16]{0:T(512)(128)(4,1)S(1)}, s32[16,512]{1,0:T(8,128)}, ...), condition=%wide.region_6.7_spmd, body=%wide.region_2.6_spmd.sunk | while | flops 134351360 | bytes 3422386 | solution.py:56
  50.4 13.8 %conditional.6 = (f32[6144,256]{1,0:T(8,128)}) conditional(s32[]{:T(128)} %bitcast.77, f32[6144,256]{1,0:T(8,128)} %get-tuple-element.670, (s32[16,512]{1,0:T(8,128)}, s32[]{:T(128)}, bf16[16,512,512]{2,1,0:T(8,128)(2,1)}, bf16[6144,256]{1,0:T(8,128)(2,1)S(1)}, f32[6144,256]{1,0:T(8,128)}) %tuple.132), branch_computations={%region_3.3_spmd, %region_4.5_spmd} | conditional | flops 134351360 | bytes 3422258 | solution.py:54
  55.3 8.9 scatter_fusion
  65.4 13.8 %conditional.6 = (f32[6144,256]{1,0:T(8,128)}) conditional(s32[]{:T(128)} %bitcast.77, f32[6144,256]{1,0:T(8,128)} %get-tuple-element.670, (s32[16,512]{1,0:T(8,128)}, s32[]{:T(128)}, bf16[16,512,512]{2,1,0:T(8,128)(2,1)}, bf16[6144,256]{1,0:T(8,128)(2,1)S(1)}, f32[6144,256]{1,0:T(8,128)}) %tuple.132), branch_computations={%region_3.3_spmd, %region_4.5_spmd} | conditional | flops 134351360 | bytes 3422258 | solution.py:54
  70.3 8.9 scatter_fusion
  80.4 13.8 %conditional.6 = (f32[6144,256]{1,0:T(8,128)}) conditional(s32[]{:T(128)} %bitcast.77, f32[6144,256]{1,0:T(8,128)} %get-tuple-element.670, (s32[16,512]{1,0:T(8,128)}, s32[]{:T(128)}, bf16[16,512,512]{2,1,0:T(8,128)(2,1)}, bf16[6144,256]{1,0:T(8,128)(2,1)S(1)}, f32[6144,256]{1,0:T(8,128)}) %tuple.132), branch_computations={%region_3.3_spmd, %region_4.5_spmd} | conditional | flops 134351360 | bytes 3422258 | solution.py:54
  95.3 13.8 %conditional.6 = (f32[6144,256]{1,0:T(8,128)}) conditional(s32[]{:T(128)} %bitcast.77, f32[6144,256]{1,0:T(8,128)} %get-tuple-element.670, (s32[16,512]{1,0:T(8,128)}, s32[]{:T(128)}, bf16[16,512,512]{2,1,0:T(8,128)(2,1)}, bf16[6144,256]{1,0:T(8,128)(2,1)S(1)}, f32[6144,256]{1,0:T(8,128)}) %tuple.132), branch_computations={%region_3.3_spmd, %region_4.5_spmd} | conditional | flops 134351360 | bytes 3422258 | solution.py:54
  100.2 8.9 scatter_fusion
  110.3 13.8 %conditional.6 = (f32[6144,256]{1,0:T(8,128)}) conditional(s32[]{:T(128)} %bitcast.77, f32[6144,256]{1,0:T(8,128)} %get-tuple-element.670, (s32[16,512]{1,0:T(8,128)}, s32[]{:T(128)}, bf16[16,512,512]{2,1,0:T(8,128)(2,1)}, bf16[6144,256]{1,0:T(8,128)(2,1)S(1)}, f32[6144,256]{1,0:T(8,128)}) %tuple.132), branch_computations={%region_3.3_spmd, %region_4.5_spmd} | conditional | flops 134351360 | bytes 3422258 | solution.py:54
  159.8 148.7 %collective-permute-done.3 = f32[384,256]{1,0:T(8,128)S(1)} collective-permute-done((f32[384,256]{1,0:T(8,128)S(1)}, f32[384,256]{1,0:T(8,128)S(1)}, u32[]{:S(2)}, u32[]{:S(2)}) %collective-permute-start.3) | collective-permute-done | bytes 393248 | tf_op jit(solution)/shard_map/ppermute | solution.py:10
  325.2 89.1 %while.50 = (s32[]{:T(128)}, f32[6144,256]{1,0:T(8,128)}, pred[16]{0:T(512)(128)(4,1)S(1)}, s32[16,512]{1,0:T(8,128)}, bf16[16,512,512]{2,1,0:T(8,128)(2,1)}, /*index=5*/bf16[6144,256]{1,0:T(8,128)(2,1)S(1)}, s32[]{:T(128)}) while((s32[]{:T(128)}, f32[6144,256]{1,0:T(8,128)}, pred[16]{0:T(512)(128)(4,1)S(1)}, s32[16,512]{1,0:T(8,128)}, ...), condition=%wide.region_13.14_spmd, body=%wide.region_9.13_spmd.sunk | while | flops 134351360 | bytes 3422386 | solution.py:56
  326.4 13.8 %conditional.7 = (f32[6144,256]{1,0:T(8,128)}) conditional(s32[]{:T(128)} %bitcast.78, f32[6144,256]{1,0:T(8,128)} %get-tuple-element.691, (s32[16,512]{1,0:T(8,128)}, s32[]{:T(128)}, bf16[16,512,512]{2,1,0:T(8,128)(2,1)}, bf16[6144,256]{1,0:T(8,128)(2,1)S(1)}, f32[6144,256]{1,0:T(8,128)}) %tuple.134), branch_computations={%region_10.10_spmd, %region_11.12_spmd} | conditional | flops 134351360 | bytes 3422258 | solution.py:54
  341.5 13.8 %conditional.7 = (f32[6144,256]{1,0:T(8,128)}) conditional(s32[]{:T(128)} %bitcast.78, f32[6144,256]{1,0:T(8,128)} %get-tuple-element.691, (s32[16,512]{1,0:T(8,128)}, s32[]{:T(128)}, bf16[16,512,512]{2,1,0:T(8,128)(2,1)}, bf16[6144,256]{1,0:T(8,128)(2,1)S(1)}, f32[6144,256]{1,0:T(8,128)}) %tuple.134), branch_computations={%region_10.10_spmd, %region_11.12_spmd} | conditional | flops 134351360 | bytes 3422258 | solution.py:54
  356.5 13.8 %conditional.7 = (f32[6144,256]{1,0:T(8,128)}) conditional(s32[]{:T(128)} %bitcast.78, f32[6144,256]{1,0:T(8,128)} %get-tuple-element.691, (s32[16,512]{1,0:T(8,128)}, s32[]{:T(128)}, bf16[16,512,512]{2,1,0:T(8,128)(2,1)}, bf16[6144,256]{1,0:T(8,128)(2,1)S(1)}, f32[6144,256]{1,0:T(8,128)}) %tuple.134), branch_computations={%region_10.10_spmd, %region_11.12_spmd} | conditional | flops 134351360 | bytes 3422258 | solution.py:54
  371.5 13.8 %conditional.7 = (f32[6144,256]{1,0:T(8,128)}) conditional(s32[]{:T(128)} %bitcast.78, f32[6144,256]{1,0:T(8,128)} %get-tuple-element.691, (s32[16,512]{1,0:T(8,128)}, s32[]{:T(128)}, bf16[16,512,512]{2,1,0:T(8,128)(2,1)}, bf16[6144,256]{1,0:T(8,128)(2,1)S(1)}, f32[6144,256]{1,0:T(8,128)}) %tuple.134), branch_computations={%region_10.10_spmd, %region_11.12_spmd} | conditional | flops 134351360 | bytes 3422258 | solution.py:54
  386.6 13.8 %conditional.7 = (f32[6144,256]{1,0:T(8,128)}) conditional(s32[]{:T(128)} %bitcast.78, f32[6144,256]{1,0:T(8,128)} %get-tuple-element.691, (s32[16,512]{1,0:T(8,128)}, s32[]{:T(128)}, bf16[16,512,512]{2,1,0:T(8,128)(2,1)}, bf16[6144,256]{1,0:T(8,128)(2,1)S(1)}, f32[6144,256]{1,0:T(8,128)}) %tuple.134), branch_computations={%region_10.10_spmd, %region_11.12_spmd} | conditional | flops 134351360 | bytes 3422258 | solution.py:54
  438.6 148.4 %collective-permute-done.5 = f32[384,256]{1,0:T(8,128)S(1)} collective-permute-done((f32[384,256]{1,0:T(8,128)S(1)}, f32[384,256]{1,0:T(8,128)S(1)}, u32[]{:S(2)}, u32[]{:S(2)}) %collective-permute-start.5) | collective-permute-done | bytes 393248 | tf_op jit(solution)/shard_map/ppermute | solution.py:10
  605.4 88.8 %while.51 = (s32[]{:T(128)}, f32[6144,256]{1,0:T(8,128)}, pred[16]{0:T(512)(128)(4,1)S(1)}, s32[16,512]{1,0:T(8,128)}, bf16[16,512,512]{2,1,0:T(8,128)(2,1)}, /*index=5*/bf16[6144,256]{1,0:T(8,128)(2,1)S(1)}, s32[]{:T(128)}) while((s32[]{:T(128)}, f32[6144,256]{1,0:T(8,128)}, pred[16]{0:T(512)(128)(4,1)S(1)}, s32[16,512]{1,0:T(8,128)}, ...), condition=%wide.region_20.21_spmd, body=%wide.region_16.20_spmd.sunk | while | flops 134351360 | bytes 3422386 | solution.py:56
  606.6 13.7 %conditional.8 = (f32[6144,256]{1,0:T(8,128)}) conditional(s32[]{:T(128)} %bitcast.79, f32[6144,256]{1,0:T(8,128)} %get-tuple-element.712, (s32[16,512]{1,0:T(8,128)}, s32[]{:T(128)}, bf16[16,512,512]{2,1,0:T(8,128)(2,1)}, bf16[6144,256]{1,0:T(8,128)(2,1)S(1)}, f32[6144,256]{1,0:T(8,128)}) %tuple.136), branch_computations={%region_17.17_spmd, %region_18.19_spmd} | conditional | flops 134351360 | bytes 3422258 | solution.py:54
  621.6 13.7 %conditional.8 = (f32[6144,256]{1,0:T(8,128)}) conditional(s32[]{:T(128)} %bitcast.79, f32[6144,256]{1,0:T(8,128)} %get-tuple-element.712, (s32[16,512]{1,0:T(8,128)}, s32[]{:T(128)}, bf16[16,512,512]{2,1,0:T(8,128)(2,1)}, bf16[6144,256]{1,0:T(8,128)(2,1)S(1)}, f32[6144,256]{1,0:T(8,128)}) %tuple.136), branch_computations={%region_17.17_spmd, %region_18.19_spmd} | conditional | flops 134351360 | bytes 3422258 | solution.py:54
  636.5 13.7 %conditional.8 = (f32[6144,256]{1,0:T(8,128)}) conditional(s32[]{:T(128)} %bitcast.79, f32[6144,256]{1,0:T(8,128)} %get-tuple-element.712, (s32[16,512]{1,0:T(8,128)}, s32[]{:T(128)}, bf16[16,512,512]{2,1,0:T(8,128)(2,1)}, bf16[6144,256]{1,0:T(8,128)(2,1)S(1)}, f32[6144,256]{1,0:T(8,128)}) %tuple.136), branch_computations={%region_17.17_spmd, %region_18.19_spmd} | conditional | flops 134351360 | bytes 3422258 | solution.py:54
  651.5 13.7 %conditional.8 = (f32[6144,256]{1,0:T(8,128)}) conditional(s32[]{:T(128)} %bitcast.79, f32[6144,256]{1,0:T(8,128)} %get-tuple-element.712, (s32[16,512]{1,0:T(8,128)}, s32[]{:T(128)}, bf16[16,512,512]{2,1,0:T(8,128)(2,1)}, bf16[6144,256]{1,0:T(8,128)(2,1)S(1)}, f32[6144,256]{1,0:T(8,128)}) %tuple.136), branch_computations={%region_17.17_spmd, %region_18.19_spmd} | conditional | flops 134351360 | bytes 3422258 | solution.py:54
  666.4 13.7 %conditional.8 = (f32[6144,256]{1,0:T(8,128)}) conditional(s32[]{:T(128)} %bitcast.79, f32[6144,256]{1,0:T(8,128)} %get-tuple-element.712, (s32[16,512]{1,0:T(8,128)}, s32[]{:T(128)}, bf16[16,512,512]{2,1,0:T(8,128)(2,1)}, bf16[6144,256]{1,0:T(8,128)(2,1)S(1)}, f32[6144,256]{1,0:T(8,128)}) %tuple.136), branch_computations={%region_17.17_spmd, %region_18.19_spmd} | conditional | flops 134351360 | bytes 3422258 | solution.py:54
  721.0 145.8 %collective-permute-done.7 = f32[384,256]{1,0:T(8,128)S(1)} collective-permute-done((f32[384,256]{1,0:T(8,128)S(1)}, f32[384,256]{1,0:T(8,128)S(1)}, u32[]{:S(2)}, u32[]{:S(2)}) %collective-permute-start.7) | collective-permute-done | bytes 393248 | tf_op jit(solution)/shard_map/ppermute | solution.py:10
  874.6 13.2 %broadcast_select_fusion = (f32[6144,256]{1,0:T(8,128)S(1)}, f32[6144,256]{1,0:T(8,128)}) fusion(pred[6144]{0:T(1024)(128)(4,1)S(1)} %not_and_fusion, f32[6144,256]{1,0:T(8,128)} %scatter_custom_fusion.4, f32[6144,256]{1,0:T(8,128)} %scatter_fusion.5, f32[6144,256]{1,0:T(8,128)} %scatter_fusion.7, f32[6144,256]{1,0:T(8,128)} %scatter_fusion.9, ...), kind=kLoop, calls=%fused_computation.53 | loop fusion | flops 23592960 | bytes 37779456 | tf_op jit(solution)/shard_map/jit(_where)/select_n | solution.py:70
  906.6 112.6 %all-gather.3.cloned.1.call-done = f32[384,128,128]{2,1,0:T(8,128)} async-done(((f32[3,128,128]{2,1,0:T(8,128)}), f32[384,128,128]{2,1,0:T(8,128)}) %all-gather.3.cloned.1.call-update) | async-done | bytes 25165840 | tf_op jit(solution)/shard_map/all_gather | solution.py:14
  1019.2 9.2 reduce_sum.18
  1029.0 11.7 %cholesky.50 = f32[128,128]{1,0:T(8,128)S(1)} custom-call(f32[128,128]{1,0:T(8,128)S(1)} %cholesky.118), custom_call_target="Cholesky" | custom-call | tf_op jit(solution)/shard_map/jit(cholesky)/cholesky | solution.py:106
  1040.7 9.8 custom-call.15
  1051.0 11.7 %cholesky.105 = f32[128,128]{1,0:T(8,128)S(1)} custom-call(f32[128,128]{1,0:T(8,128)S(1)} %convolution_subtract_fusion.1), custom_call_target="Cholesky" | custom-call | tf_op jit(solution)/shard_map/jit(cholesky)/cholesky | solution.py:106
  1069.1 19.9 %custom-call.16 = f32[2,128,128]{1,2,0:T(8,128)S(1)} custom-call(f32[2,128,128]{2,1,0:T(8,128)S(1)} %get-tuple-element.459), custom_call_target="InvertDiagBlocksLowerTriangular" | custom-call | tf_op jit(solution)/shard_map/jit(_solve_triangular)/triangular_solve | solution.py:107
  (242 shorter events, 395.1 us)
Async XLA Ops:
  6.5 1012.7 %all-gather.3.cloned.1.call-start = ((), (), s32[]{:S(2)}) async-start(), calls=%async_computation | async-start | bytes 25362432 | tf_op jit(solution)/shard_map/all_gather | solution.py:14
  7.3 5.9 copy-start
  15.8 14.1 %collective-permute-start = (f32[384]{0:T(512)S(1)}, f32[384]{0:T(512)S(1)}, u32[]{:S(2)}, u32[]{:S(2)}) collective-permute-start(f32[384]{0:T(512)S(1)} %gather_fusion.3), channel_id=1, source_target_pairs={{0,1},{1,2},{2,3},{3,4},{4,5},{5,6},{6,7},{7,8},{8,9},{9,10},{10,1... | collective-permute-start | bytes 4616 | tf_op jit(solution)/shard_map/ppermute | solution.py:10
  24.7 8.2 collective-permute-start.1
  141.9 10.1 collective-permute-start.2
  149.8 158.6 %collective-permute-start.3 = (f32[384,256]{1,0:T(8,128)S(1)}, f32[384,256]{1,0:T(8,128)S(1)}, u32[]{:S(2)}, u32[]{:S(2)}) collective-permute-start(f32[384,256]{1,0:T(8,128)S(1)} %gather_fusion.7), channel_id=1, source_target_pairs={{1,0},{2,1},{3,2},{4,3},{5,4},{6,5},{7,6},{8,7},{9,8},{10,9},{11,1... | collective-permute-start | bytes 1179656 | tf_op jit(solution)/shard_map/ppermute | solution.py:10
  414.3 15.4 %copy-start.1 = (s32[128]{0:T(128)S(1)}, s32[128]{0:T(128)}, u32[]{:S(2)}) copy-start(s32[128]{0:T(128)} %param.24) | copy-start | bytes 1540
  418.8 11.6 %collective-permute-start.4 = (f32[384,256]{1,0:T(8,128)S(1)}, f32[384,256]{1,0:T(8,128)S(1)}, u32[]{:S(2)}, u32[]{:S(2)}) collective-permute-start(f32[384,256]{1,0:T(8,128)S(1)} %gather_fusion.8), channel_id=1, source_target_pairs={{0,1},{1,2},{2,3},{3,4},{4,5},{5,6},{6,7},{7,8},{8,9},{9,10},{10,1... | collective-permute-start | bytes 1179656 | tf_op jit(solution)/shard_map/ppermute | solution.py:10
  427.7 159.3 %collective-permute-start.5 = (f32[384,256]{1,0:T(8,128)S(1)}, f32[384,256]{1,0:T(8,128)S(1)}, u32[]{:S(2)}, u32[]{:S(2)}) collective-permute-start(f32[384,256]{1,0:T(8,128)S(1)} %gather_fusion.9), channel_id=1, source_target_pairs={{1,0},{2,1},{3,2},{4,3},{5,4},{6,5},{7,6},{8,7},{9,8},{10,9},{11,1... | collective-permute-start | bytes 1179656 | tf_op jit(solution)/shard_map/ppermute | solution.py:10
  703.1 10.1 collective-permute-start.6
  708.5 158.3 %collective-permute-start.7 = (f32[384,256]{1,0:T(8,128)S(1)}, f32[384,256]{1,0:T(8,128)S(1)}, u32[]{:S(2)}, u32[]{:S(2)}) collective-permute-start(f32[384,256]{1,0:T(8,128)S(1)} %gather_fusion.11), channel_id=1, source_target_pairs={{1,0},{2,1},{3,2},{4,3},{5,4},{6,5},{7,6},{8,7},{9,8},{10,9},{11,1... | collective-permute-start | bytes 1179656 | tf_op jit(solution)/shard_map/ppermute | solution.py:10
Sparse Core Ops, SparseCore 0:
  904.7 114.5 all-gather.2
where the time goes:
time: 1120 us; the launch traced here: 1110 us
  waiting for transfers between devices  557 us (50%)
  other arithmetic  299 us (27%)
  local copies, waits for them, and re-layouts  119 us (11%)
  matrix products  58.4 us (5%)
  loops' own time  30.6 us (3%)
  starting transfers between devices  25.8 us (2%)
  between operations  17 us (2%)
    ppermute x8, waiting for transfers between devices, passed_along(): return lax.ppermute(block, axis, route)  444 us
    scatter-add x15, other arithmetic, compute(): return acc.at[rows].add(part)  134 us
    all_gather x1, waiting for transfers between devices, total_of_pieces(): return lax.all_gather(value, axis).sum(0)  113 us
    scatter-add x6, other arithmetic, ham(): local.at[lower_rows].add(coming_up).at[upper_rows].add(coming_down)  47.2 us
    another operation x6, other arithmetic, body(): factor = jnp.linalg.cholesky(gram)  34 us
    dot_general x15, matrix products, compute(): jnp.dot(element_blocks[slot], scaled[rows], preferred_element_type=jnp.fl...  32.3 us
    another operation x3, loops' own time, ham(): local = lax.fori_loop(0, slots, add_element, empty)  29.6 us
    dynamic_slice x48, local copies, waits for them, and re-layouts, add_element(): return lax.cond(slot_live[slot], compute, lambda acc: acc, total)  29.3 us
  transfers between devices with their start and end apart: 9, of which 5 were waited for; matrix products, arithmetic and copies ran while one was open for 4% of the time, Pallas kernels for 0%

commit v1 on v0

v1 whole, which is shorter than its diff:
```python
import functools

import jax
import jax.numpy as jnp
from jax import lax
from jax.experimental import pallas as pl
from jax.experimental.pallas import tpu as pltpu
from jax.sharding import PartitionSpec as P

CENTER = 0.5
HALF_WIDTH = 1.5
LANES = 128
ACCS = 4
F32 = jnp.float32
SMEM = pl.BlockSpec(memory_space=pltpu.SMEM)
VMEM = pl.BlockSpec(memory_space=pltpu.VMEM)
HBM = pl.BlockSpec(memory_space=pl.ANY)


def passed_along(block, axis, distance):
    devices = range(lax.axis_size(axis))
    route = [(i - distance, i) for i in devices if i - distance in devices]
    return lax.ppermute(block, axis, route)


def pair(offset):
    return pl.ds(pl.multiple_of(offset, 2), 2)


def span(start, size):
    return pl.ds(pl.multiple_of(start, size), size)


def params(mib=60):
    return pltpu.CompilerParams(vmem_limit_bytes=mib * 2**20)


def mass_pick(rows, mass, out):
    shared = out.shape[0]

    def step(j, carry):
        out[j] = mass[rows[shared + j] // 2]
        return carry

    lax.fori_loop(0, shared, step, 0, unroll=8)


def split_rows(states, mass48, w_out, m_out):
    for i in range(states.shape[0] // LANES):
        m = jnp.broadcast_to(mass48[i : i + 1, :], (LANES, LANES)).T
        block = states[i * LANES : (i + 1) * LANES, :]
        for h in range(2):
            at = pl.ds(2 * i * LANES + h, LANES, stride=2)
            m_out[at, :] = m
            w_out[at, :] = m * block[:, h * LANES : (h + 1) * LANES]


def add_rows(target, rows, base, source):
    group = 8

    def step(g, carry):
        at = [rows[base + g * group + k] for k in range(group)]
        new = [target[pair(at[k]), :] + source[pair(2 * (g * group + k)), :] for k in range(group)]
        for k in range(group):
            target[pair(at[k]), :] = new[k]
        return carry

    lax.fori_loop(0, source.shape[0] // (2 * group), step, 0, unroll=2)


def take_rows(out, rows, base, source):
    def step(j, carry):
        out[pair(2 * j), :] = source[pair(rows[base + j]), :]
        return carry

    lax.fori_loop(0, out.shape[0] // 2, step, 0, unroll=16)


def ham_kernel(stage, *refs):
    it = iter(refs)
    info, nodes, rows = next(it), next(it), next(it)
    if stage == 1:
        mass_in, value_in = next(it), next(it)
    else:
        from_below, from_above = next(it), next(it)
    x_hbm, m_hbm = next(it), next(it)
    prev_hbm = next(it) if stage > 1 else None
    blocks_hbm = next(it)
    next_hbm, send_up, send_down = next(it), next(it), next(it)
    w_hbm = next(it) if stage < 3 else None
    m_out_hbm = next(it) if stage == 1 else None
    w, m = next(it), next(it)
    prev = next(it) if stage > 1 else None
    accs = [next(it) for _ in range(ACCS)]
    blocks, picked, parts = next(it), next(it), next(it)
    sems, block_sems = next(it), next(it)

    shared = send_up.shape[0] // 2
    size = picked.shape[0] // 2
    live = info[0]

    load_w = pltpu.make_async_copy(x_hbm, w, sems.at[0])
    load_m = pltpu.make_async_copy(m_hbm, m, sems.at[1])
    load_w.start()
    load_m.start()

    def block_copy(e):
        return pltpu.make_async_copy(blocks_hbm.at[e], blocks.at[e], block_sems.at[e])

    def start_block(e, carry):
        block_copy(e).start()
        return carry

    lax.fori_loop(0, live, start_block, 0)
    if stage > 1:
        load_prev = pltpu.make_async_copy(prev_hbm, prev, sems.at[2])
        load_prev.start()

    chunk = 512
    chunks = w.shape[0] // chunk

    def clear(c, carry):
        for acc in accs:
            acc[span(c * chunk, chunk), :] = jnp.zeros((chunk, LANES), F32)
        return carry

    lax.fori_loop(0, chunks, clear, 0)
    load_w.wait()
    if stage == 1:
        load_m.wait()

        @pl.when(info[2] > 0)
        def _():
            for h in range(2):
                picked[pl.ds(h, shared, stride=2), :] = value_in[:, h * LANES : (h + 1) * LANES]

            def step(j, carry):
                at = pair(rows[j])
                m_j = jnp.full((2, LANES), mass_in[j], F32)
                m[at, :] = m_j
                w[at, :] = m_j * picked[pair(2 * j), :]
                return carry

            lax.fori_loop(0, shared, step, 0, unroll=8)

        save_m = pltpu.make_async_copy(m, m_out_hbm, sems.at[1])
        save_m.start()
    else:
        add_rows(w, rows, 0, from_below)
        add_rows(w, rows, shared, from_above)
    if stage < 3:
        save_w = pltpu.make_async_copy(w, w_hbm, sems.at[0])
        save_w.start()

    def product(e):
        block_copy(e).wait()
        x = jnp.concatenate(
            [picked[pl.ds(h, size, stride=2), :].astype(jnp.bfloat16) for h in range(2)], axis=1
        )
        part = jnp.dot(blocks[e], x, preferred_element_type=F32)
        for h in range(2):
            parts[pl.ds(h, size, stride=2), :] = part[:, h * LANES : (h + 1) * LANES]

    def first_pick(j, carry):
        picked[pair(2 * j), :] = w[pair(nodes[j]), :]
        return carry

    lax.fori_loop(0, size, first_pick, 0, unroll=32)
    product(0)

    def element(e, carry):
        later = jnp.minimum(e + 1, live - 1)

        def move(g, inner):
            for k in range(ACCS):
                j = g * ACCS + k
                picked[pair(2 * j), :] = w[pair(nodes[later * size + j]), :]
                at = pair(nodes[e * size + j])
                accs[k][at, :] = accs[k][at, :] + parts[pair(2 * j), :]
            return inner

        lax.fori_loop(0, size // ACCS, move, 0, unroll=8)

        @pl.when(e + 1 < live)
        def _():
            product(later)

        return carry

    lax.fori_loop(0, live, element, 0)

    if stage > 1:
        load_m.wait()
        load_prev.wait()
    factor = 1.0 if stage == 1 else 2.0
    scale_h = factor / HALF_WIDTH
    scale_w = -factor * CENTER / HALF_WIDTH

    def combine(c, carry):
        at = span(c * chunk, chunk)
        total = accs[0][at, :]
        for acc in accs[1:]:
            total = total + acc[at, :]
        mass = m[at, :]
        total = scale_h * (mass * mass) * total
        accs[0][at, :] = total
        new = total + scale_w * w[at, :]
        if stage > 1:
            new = new - prev[at, :]
        accs[1][at, :] = new
        pltpu.make_async_copy(accs[1].at[at, :], next_hbm.at[at, :], sems.at[3]).start()
        return carry

    lax.fori_loop(0, chunks, combine, 0)
    take_rows(send_up, rows, shared, accs[0])
    take_rows(send_down, rows, 0, accs[0])
    pltpu.make_async_copy(accs[1], next_hbm, sems.at[3]).wait()
    if stage < 3:
        save_w.wait()
    if stage == 1:
        save_m.wait()


def ham(stage, operands, field, blocks, shared):
    tall = jax.ShapeDtypeStruct(field, F32)
    send = jax.ShapeDtypeStruct((2 * shared, LANES), F32)
    size = blocks.shape[1]
    n_out = 3 + (stage < 3) + (stage == 1)
    outs = [tall, send, send] + [tall] * (n_out - 3)
    out_specs = [HBM, VMEM, VMEM] + [HBM] * (n_out - 3)
    in_specs = [SMEM, SMEM, SMEM] + ([SMEM, VMEM] if stage == 1 else [VMEM, VMEM])
    in_specs += [HBM, HBM] + ([HBM] if stage > 1 else []) + [HBM]
    fields = [pltpu.VMEM(field, F32)] * (ACCS + 2 + (stage > 1))
    scratch = fields + [
        pltpu.VMEM(blocks.shape, blocks.dtype),
        pltpu.VMEM((2 * size, LANES), F32),
        pltpu.VMEM((2 * size, LANES), F32),
        pltpu.SemaphoreType.DMA((4,)),
        pltpu.SemaphoreType.DMA((blocks.shape[0],)),
    ]
    return pl.pallas_call(
        functools.partial(ham_kernel, stage),
        out_shape=outs,
        in_specs=in_specs,
        out_specs=out_specs,
        scratch_shapes=scratch,
        compiler_params=params(),
        name="ham%d" % stage,
    )(*operands)


def split3(x):
    high = x.astype(jnp.bfloat16)
    return high, (x - high.astype(F32)).astype(jnp.bfloat16)


def finish_kernel(info, rows, from_below, from_above, x_hbm, m_hbm, out, gram, w, m, sems):
    load_w = pltpu.make_async_copy(x_hbm, w, sems.at[0])
    load_m = pltpu.make_async_copy(m_hbm, m, sems.at[1])
    load_w.start()
    load_m.start()
    shared = from_below.shape[0] // 2
    load_w.wait()
    add_rows(w, rows, 0, from_below)
    add_rows(w, rows, shared, from_above)
    load_m.wait()
    n = 256
    chunks = out.shape[0] // n

    def divide(c, carry):
        for h in range(2):
            at = pl.ds(2 * n * c + h, n, stride=2)
            value = w[at, :] / m[at, :]
            out[span(c * n, n), h * LANES : (h + 1) * LANES] = value
            w[at, :] = value
        return carry

    lax.fori_loop(0, chunks, divide, 0)

    @pl.when(info[2] > 0)
    def _():
        def blank(j, carry):
            w[pair(rows[j]), :] = jnp.zeros((2, LANES), F32)
            return carry

        lax.fori_loop(0, shared, blank, 0, unroll=16)

    gram[...] = jnp.zeros_like(gram)
    limit = info[1]

    def add_chunk(c, carry):
        live = c * n + lax.broadcasted_iota(jnp.int32, (n, LANES), 0) < limit
        g = jnp.concatenate(
            [jnp.where(live, w[pl.ds(2 * n * c + h, n, stride=2), :], 0.0) for h in range(2)], axis=1
        )
        high, low = split3(g)
        dims = (((0,), (0,)), ((), ()))
        square = lax.dot_general(high, high, dims, preferred_element_type=F32)
        cross = lax.dot_general(high, low, dims, preferred_element_type=F32)
        gram[...] += square + (cross + cross.T)
        return carry

    lax.fori_loop(0, chunks, add_chunk, 0)


def body(
    states, inv_sqrt_mass, element_blocks, element_nodes, element_counts, node_counts, boundary_rows
):
    position = lax.axis_index("mesh")
    devices = lax.axis_size("mesh")
    row_total, width = states.shape
    shared = boundary_rows.shape[2]
    field = (2 * row_total, LANES)
    info = jnp.stack([element_counts[0], node_counts[position], position]).astype(jnp.int32)
    rows = 2 * boundary_rows.reshape(-1)
    nodes = 2 * element_nodes.reshape(-1)

    mass_send = pl.pallas_call(
        mass_pick,
        out_shape=jax.ShapeDtypeStruct((shared,), F32),
        in_specs=[SMEM, SMEM],
        out_specs=SMEM,
        name="mass_pick",
    )(rows, inv_sqrt_mass)
    owner_mass = passed_along(mass_send, "mesh", 1)
    owner_vals = passed_along(states[boundary_rows[0, 1]], "mesh", 1)
    tall = jax.ShapeDtypeStruct(field, F32)
    w0, m = pl.pallas_call(
        split_rows,
        out_shape=[tall, tall],
        in_specs=[VMEM, VMEM],
        out_specs=[VMEM, VMEM],
        compiler_params=params(),
        name="split_rows",
    )(states, inv_sqrt_mass.reshape(-1, LANES))

    w1, up, down, w0, m = ham(
        1,
        (info, nodes, rows, owner_mass, owner_vals, w0, m, element_blocks),
        field,
        element_blocks,
        shared,
    )
    up, down = passed_along(up, "mesh", 1), passed_along(down, "mesh", -1)
    w2, up, down, w1 = ham(
        2, (info, nodes, rows, up, down, w1, m, w0, element_blocks), field, element_blocks, shared
    )
    up, down = passed_along(up, "mesh", 1), passed_along(down, "mesh", -1)
    w3, up, down = ham(
        3, (info, nodes, rows, up, down, w2, m, w1, element_blocks), field, element_blocks, shared
    )
    up, down = passed_along(up, "mesh", 1), passed_along(down, "mesh", -1)
    filtered, gram = pl.pallas_call(
        finish_kernel,
        out_shape=[
            jax.ShapeDtypeStruct(states.shape, F32),
            jax.ShapeDtypeStruct((width, width), F32),
        ],
        in_specs=[SMEM, SMEM, VMEM, VMEM, HBM, HBM],
        out_specs=[VMEM, VMEM],
        scratch_shapes=[pltpu.VMEM(field, F32), pltpu.VMEM(field, F32), pltpu.SemaphoreType.DMA((2,))],
        compiler_params=params(),
        name="finish",
    )(info, rows, up, down, w3, m)

    gram = lax.psum(gram, "mesh")
    total = (jnp.sum(node_counts) - shared * (devices - 1)).astype(F32)
    gram = gram / total
    factor = jnp.linalg.cholesky(gram)
    inverse = jax.scipy.linalg.solve_triangular(factor, jnp.eye(width, dtype=F32), lower=True)
    rotated = jnp.dot(
        filtered, inverse.T, precision=lax.Precision.HIGHEST, preferred_element_type=F32
    )
    live = jnp.arange(row_total) < node_counts[position]
    return jnp.where(live[:, None], rotated, 0.0)


def solution(mesh):
    in_specs = (
        P("mesh", None),
        P("mesh"),
        P("mesh", None, None),
        P("mesh", None),
        P("mesh"),
        P(),
        P("mesh", None, None),
    )
    out_specs = P("mesh", None)
    return jax.shard_map(body, mesh=mesh, in_specs=in_specs, out_specs=out_specs, check_vma=False)
```

time: 1120 us -> 423 us (0.38); the launches traced: 1110 us -> 422 us
  waiting for transfers between devices: 557 us -> 210 us
  other arithmetic: 299 us -> 60.6 us
  local copies, waits for them, and re-layouts: 119 us -> 15.9 us
  Pallas kernels: 0 us -> 90.4 us
  matrix products: 58.4 us -> 10.2 us
  loops' own time: 30.6 us -> 0.03 us
    ppermute x8, waiting for transfers between devices: 444 us -> 28.1 us  [passed_along(): return lax.ppermute(block, axis, route)]
    psum x0 -> x1, waiting for transfers between devices: none -> 181 us  [body(): gram = lax.psum(gram, 'mesh')]
    scatter-add x21 -> x0, other arithmetic: 181 us -> none  [the longest x15 134 us: compute(): return acc.at[rows].add(part)]
    all_gather x1 -> x0, waiting for transfers between devices: 113 us -> none  [total_of_pieces(): return lax.all_gather(value, axis).sum(0)]
    pallas_call x0 -> x6, Pallas kernels: none -> 90.4 us  [the longest x3 59.9 us: ham(): pl.pallas_call(functools.partial(ham_kernel, stage), out_shape=outs, in_s...]
    gather x24 -> x1, local copies, waits for them, and re-layouts: 65.5 us -> 4.45 us  [body(): owner_vals = passed_along(states[boundary_rows[0, 1]], 'mesh', 1)]
    dot_general x18 -> x0, matrix products: 48.3 us -> none  [the longest x15 32.3 us: compute(): jnp.dot(element_blocks[slot], scaled[rows], preferred_element_type=jnp.fl...]
    another operation x52 -> x1, loops' own time: 30.6 us -> 0.03 us  [body(): jax.scipy.linalg.solve_triangular(factor, jnp.eye(width, dtype=F32), lowe...]
  transfers between devices with their start and end apart: 9 -> 9, of which waited for: 5 -> 7; matrix products, arithmetic and copies ran while one was open for 4% -> 2% of each run, Pallas kernels for 0% -> 3%
where the time goes in v1:
time: 423 us; the launch traced here: 422 us
  waiting for transfers between devices  210 us (50%)
  Pallas kernels  90.4 us (21%)
  other arithmetic  60.6 us (14%)
  starting transfers between devices  19.5 us (5%)
  between operations  16.2 us (4%)
  local copies, waits for them, and re-layouts  15.9 us (4%)
  matrix products  10.2 us (2%)
    psum x1, waiting for transfers between devices, body(): gram = lax.psum(gram, 'mesh')  181 us
    pallas_call x3, Pallas kernels, ham(): pl.pallas_call(functools.partial(ham_kernel, stage), out_shape=outs, in_s...  59.9 us
    another operation x6, other arithmetic, body(): factor = jnp.linalg.cholesky(gram)  34 us
    ppermute x8, waiting for transfers between devices, passed_along(): return lax.ppermute(block, axis, route)  28.1 us
    another operation x3, other arithmetic, body(): jax.scipy.linalg.solve_triangular(factor, jnp.eye(width, dtype=F32), lowe...  19.9 us
    ppermute x8, starting transfers between devices, passed_along(): return lax.ppermute(block, axis, route)  19.5 us
    pallas_call x1, Pallas kernels, body(): pl.pallas_call(finish_kernel, out_shape=[jax.ShapeDtypeStruct(states.shap...  18 us
    dot_general x1, matrix products, body(): jnp.dot(filtered, inverse.T, precision=lax.Precision.HIGHEST, preferred_e...  8.87 us
  transfers between devices with their start and end apart: 9, of which 7 were waited for; matrix products, arithmetic and copies ran while one was open for 2% of the time, Pallas kernels for 3%

profile of v1, /device:TPU:1, one launch (start us, length us, event | category | flops | bytes accessed | tf_op | source)
XLA Modules:
  0.0 422.4 jit_solution(628026451321260075)
XLA Ops:
  7.3 4.5 %gather_fusion = f32[384,256]{1,0:T(8,128)S(1)} fusion(f32[6144,256]{1,0:T(8,128)} %states.1, s32[1024]{0:T(1024)S(1)} %pad_clamp_fusion), kind=kCustom, calls=%fused_computation | custom fusion | bytes 787968 | tf_op jit(solution)/shard_map/gather | solution.py:326
  11.7 4.5 %collective-permute-start.1 = (f32[384,256]{1,0:T(8,128)S(1)}, f32[384,256]{1,0:T(8,128)S(1)}, u32[]{:S(2)}, u32[]{:S(2)}) collective-permute-start(f32[384,256]{1,0:T(8,128)S(1)} %gather_fusion), channel_id=1, source_target_pairs={{0,1},{1,2},{2,3},{3,4},{4,5},{5,6},{6,7},{7,8},{8,9},{9,10},{10,1... | collective-permute-start | bytes 1179656 | tf_op jit(solution)/shard_map/ppermute | solution.py:23
  17.5 4.2 mass_pick.1
  21.7 1.9 collective-permute-start
  26.3 1.3 pad_add_fusion.refs_0_.info
  28.2 8.4 %split_rows.1 = (f32[12288,128]{1,0:T(8,128)}, f32[12288,128]{1,0:T(8,128)}) custom-call(f32[6144,256]{1,0:T(8,128)} %states.1, f32[48,128]{1,0:T(8,128)} %bitcast.43), custom_call_target="tpu_custom_call" | custom-call | tf_op jit(solution)/shard_map/split_rows/pallas_call | solution.py:328
  37.4 20.6 %ham1.1 = (f32[12288,128]{1,0:T(8,128)}, f32[768,128]{1,0:T(8,128)}, f32[768,128]{1,0:T(8,128)}, f32[12288,128]{1,0:T(8,128)}, f32[12288,128]{1,0:T(8,128)}) custom-call(s32[3]{0:T(128)} %pad_add_fusion.refs_0_.info, s32[8192]{0:T(1024)} %bitcast.40, s32[768]{0:T(1024)} %mul.18.rows.refs_2_, f32[384]{0:T(512)} %copy-done.7, f32[384,256]{1,0:T(8,128)} %copy-done.2, ...), custom_call_target="tpu_custom_call" | custom-call | tf_op jit(solution)/shard_map/ham1/pallas_call | solution.py:241
  58.0 1.9 collective-permute-start.2
  59.9 2.4 collective-permute-start.3
  62.4 2.6 collective-permute-done.2.refs_3_
  65.0 4.3 %collective-permute-done.3.refs_4_ = f32[768,128]{1,0:T(8,128)S(1)} collective-permute-done((f32[768,128]{1,0:T(8,128)}, f32[768,128]{1,0:T(8,128)S(1)}, u32[]{:S(2)}, u32[]{:S(2)}) %collective-permute-start.3) | collective-permute-done | bytes 393248 | tf_op jit(solution)/shard_map/ppermute | solution.py:23
  70.0 19.7 %ham2.1 = (f32[12288,128]{1,0:T(8,128)}, f32[768,128]{1,0:T(8,128)}, f32[768,128]{1,0:T(8,128)}, f32[12288,128]{1,0:T(8,128)}) custom-call(s32[3]{0:T(128)} %pad_add_fusion.refs_0_.info, s32[8192]{0:T(1024)} %bitcast.41, s32[768]{0:T(1024)} %mul.18.rows.refs_2_, f32[768,128]{1,0:T(8,128)} %copy-done.3, f32[768,128]{1,0:T(8,128)} %copy-done.5, ...), custom_call_target="tpu_custom_call" | custom-call | tf_op jit(solution)/shard_map/ham2/pallas_call | solution.py:241
  89.7 1.9 collective-permute-start.4
  91.6 2.4 collective-permute-start.5
  94.1 2.6 collective-permute-done.4.refs_3_
  96.7 4.3 %collective-permute-done.5.refs_4_ = f32[768,128]{1,0:T(8,128)S(1)} collective-permute-done((f32[768,128]{1,0:T(8,128)}, f32[768,128]{1,0:T(8,128)S(1)}, u32[]{:S(2)}, u32[]{:S(2)}) %collective-permute-start.5) | collective-permute-done | bytes 393248 | tf_op jit(solution)/shard_map/ppermute | solution.py:23
  101.7 19.6 %ham3.1 = (f32[12288,128]{1,0:T(8,128)}, f32[768,128]{1,0:T(8,128)}, f32[768,128]{1,0:T(8,128)}) custom-call(s32[3]{0:T(128)} %pad_add_fusion.refs_0_.info, s32[8192]{0:T(1024)} %bitcast.42, s32[768]{0:T(1024)} %mul.18.rows.refs_2_, f32[768,128]{1,0:T(8,128)} %copy-done.4, f32[768,128]{1,0:T(8,128)} %copy-done.6, f32[12288,128]{1,0:T(8,128)} %get-tuple-element.30.refs_5_, ...), custom_call_target="tpu_custom_call" | custom-call | tf_op jit(solution)/shard_map/ham3/pallas_call | solution.py:241
  121.3 1.9 collective-permute-start.6
  123.2 2.4 collective-permute-start.7
  126.3 1.9 collective-permute-done.6.from_below
  128.3 12.4 %collective-permute-done.7.from_above = f32[768,128]{1,0:T(8,128)S(1)} collective-permute-done((f32[768,128]{1,0:T(8,128)}, f32[768,128]{1,0:T(8,128)S(1)}, u32[]{:S(2)}, u32[]{:S(2)}) %collective-permute-start.7) | collective-permute-done | bytes 393248 | tf_op jit(solution)/shard_map/ppermute | solution.py:23
  141.4 18.0 %finish.1 = (f32[6144,256]{1,0:T(8,128)}, f32[256,256]{1,0:T(8,128)}) custom-call(s32[3]{0:T(128)} %pad_add_fusion.refs_0_.info, s32[768]{0:T(1024)} %mul.18.rows.refs_2_, f32[768,128]{1,0:T(8,128)} %copy-done, f32[768,128]{1,0:T(8,128)} %copy-done.1, f32[12288,128]{1,0:T(8,128)} %get-tuple-element.34.x_hbm, f32[12288,128]{1,0:T(8,128)} %get-tuple-element.26.refs_6_.m_hbm), custom_call_target="tpu_custom_call" | custom-call | tf_op jit(solution)/shard_map/finish/pallas_call | solution.py:353
  159.4 1.8 copy.10
  162.5 181.5 %all-reduce.3.cloned.1.call-done = f32[256,256]{0,1:T(8,128)} async-done(((f32[256,256]{0,1:T(8,128)}), f32[256,256]{0,1:T(8,128)}) %all-reduce.3.cloned.1.call-update) | async-done | bytes 262160 | tf_op jit(solution)/shard_map/psum | solution.py:366
  346.1 11.7 %cholesky.50 = f32[128,128]{1,0:T(8,128)S(1)} custom-call(f32[128,128]{1,0:T(8,128)S(1)} %cholesky.118), custom_call_target="Cholesky" | custom-call | tf_op jit(solution)/shard_map/jit(cholesky)/cholesky | solution.py:369
  357.8 9.8 %custom-call.15 = f32[1,128,128]{1,2,0:T(8,128)S(1)} custom-call(f32[1,128,128]{2,1,0:T(8,128)S(1)} %get-tuple-element.58), custom_call_target="InvertDiagBlocksLowerTriangular" | custom-call | tf_op jit(solution)/shard_map/jit(cholesky)/cholesky | solution.py:369
  368.1 11.7 %cholesky.105 = f32[128,128]{1,0:T(8,128)S(1)} custom-call(f32[128,128]{1,0:T(8,128)S(1)} %convolution_subtract_fusion.1), custom_call_target="Cholesky" | custom-call | tf_op jit(solution)/shard_map/jit(cholesky)/cholesky | solution.py:369
  381.9 4.0 while.1
  382.5 1.4 bitcast_dynamic-update-slice_fusion.2
  384.5 1.4 bitcast_dynamic-update-slice_fusion.2
  385.9 19.9 %custom-call.16 = f32[2,128,128]{1,2,0:T(8,128)S(1)} custom-call(f32[2,128,128]{2,1,0:T(8,128)S(1)} %get-tuple-element.44), custom_call_target="InvertDiagBlocksLowerTriangular" | custom-call | tf_op jit(solution)/shard_map/jit(_solve_triangular)/triangular_solve | solution.py:370
  406.7 8.9 %convolution_select_fusion = f32[6144,256]{1,0:T(8,128)} fusion(f32[6144,256]{1,0:T(8,128)} %get-tuple-element.35, pred[6144]{0:T(1024)(128)(4,1)S(1)} %iota_compare_fusion.4, f32[128,256]{1,0:T(8,128)S(1)} %fusion.7, f32[128,256]{1,0:T(8,128)S(1)} %fusion.4), kind=kOutput, calls=%fused_computation.3 | convolution fusion | flops 4833476608 | bytes 12851200 | tf_op jit(solution)/shard_map/dot_general | solution.py:371
  (53 shorter events, 14.5 us)
Async XLA Ops:
  6.5 337.4 %all-reduce.3.cloned.1.call-start = ((), (), s32[]{:S(2)}) async-start(), calls=%async_computation | async-start | bytes 524288 | tf_op jit(solution)/shard_map/psum | solution.py:366
  11.7 24.9 %collective-permute-start.1 = (f32[384,256]{1,0:T(8,128)S(1)}, f32[384,256]{1,0:T(8,128)S(1)}, u32[]{:S(2)}, u32[]{:S(2)}) collective-permute-start(f32[384,256]{1,0:T(8,128)S(1)} %gather_fusion), channel_id=1, source_target_pairs={{0,1},{1,2},{2,3},{3,4},{4,5},{5,6},{6,7},{7,8},{8,9},{9,10},{10,1... | collective-permute-start | bytes 1179656 | tf_op jit(solution)/shard_map/ppermute | solution.py:23
  21.7 15.0 %collective-permute-start = (f32[384]{0:T(512)}, f32[384]{0:T(512)S(1)}, u32[]{:S(2)}, u32[]{:S(2)}) collective-permute-start(f32[384]{0:T(512)} %mass_pick.1), channel_id=1, source_target_pairs={{0,1},{1,2},{2,3},{3,4},{4,5},{5,6},{6,7},{7,8},{8,9},{9,10},{10,1... | collective-permute-start | bytes 4616 | tf_op jit(solution)/shard_map/ppermute | solution.py:23
  36.6 0.6 copy-start.7
  36.7 0.8 copy-start.2
  58.0 6.9 %collective-permute-start.2 = (f32[768,128]{1,0:T(8,128)}, f32[768,128]{1,0:T(8,128)S(1)}, u32[]{:S(2)}, u32[]{:S(2)}) collective-permute-start(f32[768,128]{1,0:T(8,128)} %get-tuple-element.23), channel_id=1, source_target_pairs={{0,1},{1,2},{2,3},{3,4},{4,5},{5,6},{6,7},{7,8},{8,9},{9,10},{10,1... | collective-permute-start | bytes 1179656 | tf_op jit(solution)/shard_map/ppermute | solution.py:23
  59.9 9.3 %collective-permute-start.3 = (f32[768,128]{1,0:T(8,128)}, f32[768,128]{1,0:T(8,128)S(1)}, u32[]{:S(2)}, u32[]{:S(2)}) collective-permute-start(f32[768,128]{1,0:T(8,128)} %get-tuple-element.24), channel_id=1, source_target_pairs={{1,0},{2,1},{3,2},{4,3},{5,4},{6,5},{7,6},{8,7},{9,8},{10,9},{11,1... | collective-permute-start | bytes 1179656 | tf_op jit(solution)/shard_map/ppermute | solution.py:23
  65.0 4.3 %copy-start.3 = (f32[768,128]{1,0:T(8,128)}, f32[768,128]{1,0:T(8,128)S(1)}, u32[]{:S(2)}) copy-start(f32[768,128]{1,0:T(8,128)S(1)} %collective-permute-done.2.refs_3_) | copy-start | bytes 1179652
  69.3 0.8 copy-start.5
  89.7 6.9 %collective-permute-start.4 = (f32[768,128]{1,0:T(8,128)}, f32[768,128]{1,0:T(8,128)S(1)}, u32[]{:S(2)}, u32[]{:S(2)}) collective-permute-start(f32[768,128]{1,0:T(8,128)} %get-tuple-element.28), channel_id=1, source_target_pairs={{0,1},{1,2},{2,3},{3,4},{4,5},{5,6},{6,7},{7,8},{8,9},{9,10},{10,1... | collective-permute-start | bytes 1179656 | tf_op jit(solution)/shard_map/ppermute | solution.py:23
  91.6 9.3 %collective-permute-start.5 = (f32[768,128]{1,0:T(8,128)}, f32[768,128]{1,0:T(8,128)S(1)}, u32[]{:S(2)}, u32[]{:S(2)}) collective-permute-start(f32[768,128]{1,0:T(8,128)} %get-tuple-element.29), channel_id=1, source_target_pairs={{1,0},{2,1},{3,2},{4,3},{5,4},{6,5},{7,6},{8,7},{9,8},{10,9},{11,1... | collective-permute-start | bytes 1179656 | tf_op jit(solution)/shard_map/ppermute | solution.py:23
  96.7 4.3 %copy-start.4 = (f32[768,128]{1,0:T(8,128)}, f32[768,128]{1,0:T(8,128)S(1)}, u32[]{:S(2)}) copy-start(f32[768,128]{1,0:T(8,128)S(1)} %collective-permute-done.4.refs_3_) | copy-start | bytes 1179652
  100.9 0.8 copy-start.6
  121.3 6.9 %collective-permute-start.6 = (f32[768,128]{1,0:T(8,128)}, f32[768,128]{1,0:T(8,128)S(1)}, u32[]{:S(2)}, u32[]{:S(2)}) collective-permute-start(f32[768,128]{1,0:T(8,128)} %get-tuple-element.32), channel_id=1, source_target_pairs={{0,1},{1,2},{2,3},{3,4},{4,5},{5,6},{6,7},{7,8},{8,9},{9,10},{10,1... | collective-permute-start | bytes 1179656 | tf_op jit(solution)/shard_map/ppermute | solution.py:23
  123.2 17.4 %collective-permute-start.7 = (f32[768,128]{1,0:T(8,128)}, f32[768,128]{1,0:T(8,128)S(1)}, u32[]{:S(2)}, u32[]{:S(2)}) collective-permute-start(f32[768,128]{1,0:T(8,128)} %get-tuple-element.33), channel_id=1, source_target_pairs={{1,0},{2,1},{3,2},{4,3},{5,4},{6,5},{7,6},{8,7},{9,8},{10,9},{11,1... | collective-permute-start | bytes 1179656 | tf_op jit(solution)/shard_map/ppermute | solution.py:23
  128.3 12.4 %copy-start = (f32[768,128]{1,0:T(8,128)}, f32[768,128]{1,0:T(8,128)S(1)}, u32[]{:S(2)}) copy-start(f32[768,128]{1,0:T(8,128)S(1)} %collective-permute-done.6.from_below) | copy-start | bytes 1179652
  140.6 0.7 copy-start.1
  141.4 19.8 %copy-start.8 = (s32[128]{0:T(128)S(1)}, s32[128]{0:T(128)}, u32[]{:S(2)}) copy-start(s32[128]{0:T(128)} %param.12) | copy-start | bytes 1540
Sparse Core Ops, SparseCore 0:
  161.3 182.5 all-reduce.2

commit v2 on v1

v2 whole, which is shorter than its diff:
```python
import functools

import jax
import jax.numpy as jnp
from jax import lax
from jax.experimental import pallas as pl
from jax.experimental.pallas import tpu as pltpu
from jax.sharding import PartitionSpec as P

CENTER = 0.5
HALF_WIDTH = 1.5
LANES = 128
ACCS = 4
UNROLL = 64
F32 = jnp.float32
SMEM = pl.BlockSpec(memory_space=pltpu.SMEM)
VMEM = pl.BlockSpec(memory_space=pltpu.VMEM)
HBM = pl.BlockSpec(memory_space=pl.ANY)


def passed_along(block, axis, distance):
    devices = range(lax.axis_size(axis))
    route = [(i - distance, i) for i in devices if i - distance in devices]
    return lax.ppermute(block, axis, route)


def pair(offset):
    return pl.ds(pl.multiple_of(offset, 2), 2)


def span(start, size):
    return pl.ds(pl.multiple_of(start, size), size)


def params(mib=60):
    return pltpu.CompilerParams(vmem_limit_bytes=mib * 2**20)


def send_rows(rows, mass, states_hbm, values_out, mass_out, left, right, sems):
    sides = (left, right)
    loads = [
        pltpu.make_async_copy(states_hbm.at[:, h * LANES : (h + 1) * LANES], sides[h], sems.at[h])
        for h in range(2)
    ]
    for load in loads:
        load.start()
    shared = mass_out.shape[0]
    unroll = 16

    def mass_step(g, carry):
        some = rows.at[pl.ds(shared + g * unroll, unroll)]
        for k in range(unroll):
            mass_out[g * unroll + k] = mass[some[k] // 2]
        return carry

    lax.fori_loop(0, shared // unroll, mass_step, 0)
    for load in loads:
        load.wait()

    def step(g, carry):
        some = rows.at[pl.ds(shared + g * unroll, unroll)]
        base = pl.multiple_of(2 * g * unroll, 2 * unroll)
        for k in range(unroll):
            row = some[k] // 2
            for h in range(2):
                values_out[pl.ds(base + 2 * k + h, 1), :] = sides[h][pl.ds(row, 1), :]
        return carry

    lax.fori_loop(0, shared // unroll, step, 0)


def split_rows(mass_all, states, w_out, m_out):
    step = pl.program_id(0)
    per = states.shape[0] // LANES
    for i in range(per):
        m = jnp.broadcast_to(mass_all[pl.ds(step * per + i, 1), :], (LANES, LANES)).T
        block = states[i * LANES : (i + 1) * LANES, :]
        for h in range(2):
            at = pl.ds(2 * i * LANES + h, LANES, stride=2)
            m_out[at, :] = m
            w_out[at, :] = m * block[:, h * LANES : (h + 1) * LANES]


def add_rows(target, rows, base, source):
    group = 16

    def step(g, carry):
        some = rows.at[pl.ds(base + g * group, group)]
        first = pl.multiple_of(2 * g * group, 2 * group)
        at = [pair(some[k]) for k in range(group)]
        new = [target[at[k], :] + source[pl.ds(first + 2 * k, 2), :] for k in range(group)]
        for k in range(group):
            target[at[k], :] = new[k]
        return carry

    lax.fori_loop(0, source.shape[0] // (2 * group), step, 0)


def take_rows(out, rows, base, source):
    group = 32

    def step(g, carry):
        some = rows.at[pl.ds(base + g * group, group)]
        first = pl.multiple_of(2 * g * group, 2 * group)
        for k in range(group):
            out[pl.ds(first + 2 * k, 2), :] = source[pair(some[k]), :]
        return carry

    lax.fori_loop(0, out.shape[0] // (2 * group), step, 0)


def ham_kernel(stage, *refs):
    it = iter(refs)
    count, position, nodes, rows = next(it), next(it), next(it), next(it)
    if stage == 1:
        mass_in, value_in = next(it), next(it)
    else:
        from_below, from_above = next(it), next(it)
    x_hbm, m_hbm = next(it), next(it)
    prev_hbm = next(it) if stage > 1 else None
    blocks_hbm = next(it)
    next_hbm, send_up, send_down = next(it), next(it), next(it)
    w_hbm = next(it) if stage < 3 else None
    m_out_hbm = next(it) if stage == 1 else None
    w, m = next(it), next(it)
    prev = next(it) if stage > 1 else None
    accs = [next(it) for _ in range(ACCS)]
    blocks, picked, parts = next(it), next(it), next(it)
    sems, block_sems = next(it), next(it)

    shared = send_up.shape[0] // 2
    size = picked.shape[0] // 2
    live = count[0]

    load_w = pltpu.make_async_copy(x_hbm, w, sems.at[0])
    load_m = pltpu.make_async_copy(m_hbm, m, sems.at[1])
    load_w.start()
    if stage == 1:
        load_m.start()

    def block_copy(e):
        return pltpu.make_async_copy(blocks_hbm.at[e], blocks.at[e], block_sems.at[e])

    def start_block(e, carry):
        block_copy(e).start()
        return carry

    block_copy(0).start()
    chunk = 512
    chunks = w.shape[0] // chunk

    def clear(c, carry):
        for acc in accs:
            acc[span(c * chunk, chunk), :] = jnp.zeros((chunk, LANES), F32)
        return carry

    lax.fori_loop(0, chunks, clear, 0)
    load_w.wait()
    lax.fori_loop(1, live, start_block, 0)
    if stage == 1:
        load_m.wait()

        @pl.when(position[0] > 0)
        def _():
            def step(j, carry):
                at = pair(rows[j])
                m_j = jnp.full((2, LANES), mass_in[j], F32)
                m[at, :] = m_j
                w[at, :] = m_j * value_in[pair(2 * j), :]
                return carry

            lax.fori_loop(0, shared, step, 0, unroll=8)

        save_m = pltpu.make_async_copy(m, m_out_hbm, sems.at[1])
        save_m.start()
    else:
        load_m.start()
        load_prev = pltpu.make_async_copy(prev_hbm, prev, sems.at[2])
        load_prev.start()
        add_rows(w, rows, 0, from_below)
        add_rows(w, rows, shared, from_above)
    if stage < 3:
        save_w = pltpu.make_async_copy(w, w_hbm, sems.at[0])
        save_w.start()

    def product(e):
        block_copy(e).wait()
        x = jnp.concatenate(
            [picked[pl.ds(h, size, stride=2), :].astype(jnp.bfloat16) for h in range(2)], axis=1
        )
        part = jnp.dot(blocks[e], x, preferred_element_type=F32)
        for h in range(2):
            parts[pl.ds(h, size, stride=2), :] = part[:, h * LANES : (h + 1) * LANES]

    take_rows(picked, nodes, 0, w)
    product(0)

    def element(e, carry):
        later = jnp.minimum(e + 1, live - 1)

        def move(g, inner):
            here = nodes.at[pl.ds(e * size + g * UNROLL, UNROLL)]
            ahead = nodes.at[pl.ds(later * size + g * UNROLL, UNROLL)]
            first = pl.multiple_of(2 * g * UNROLL, 2 * UNROLL)
            for k in range(UNROLL):
                line = pl.ds(first + 2 * k, 2)
                picked[line, :] = w[pair(ahead[k]), :]
                at = pair(here[k])
                acc = accs[k % ACCS]
                acc[at, :] = acc[at, :] + parts[line, :]
            return inner

        lax.fori_loop(0, size // UNROLL, move, 0)

        @pl.when(e + 1 < live)
        def _():
            product(later)

        return carry

    lax.fori_loop(0, live, element, 0)

    if stage > 1:
        load_m.wait()
        load_prev.wait()
    factor = 1.0 if stage == 1 else 2.0
    scale_h = factor / HALF_WIDTH
    scale_w = -factor * CENTER / HALF_WIDTH

    def combine(c, carry):
        at = span(c * chunk, chunk)
        total = accs[0][at, :]
        for acc in accs[1:]:
            total = total + acc[at, :]
        mass = m[at, :]
        rest = scale_w * w[at, :]
        if stage > 1:
            rest = rest - prev[at, :]
        if stage < 3:
            total = scale_h * (mass * mass) * total
        else:
            total = scale_h * mass * total
            rest = rest / mass
        accs[0][at, :] = total
        accs[1][at, :] = total + rest
        pltpu.make_async_copy(accs[1].at[at, :], next_hbm.at[at, :], sems.at[3]).start()
        return carry

    lax.fori_loop(0, chunks, combine, 0)
    take_rows(send_up, rows, shared, accs[0])
    take_rows(send_down, rows, 0, accs[0])
    pltpu.make_async_copy(accs[1], next_hbm, sems.at[3]).wait()
    if stage < 3:
        save_w.wait()
    if stage == 1:
        save_m.wait()


def ham(stage, operands, field, blocks, shared):
    tall = jax.ShapeDtypeStruct(field, F32)
    send = jax.ShapeDtypeStruct((2 * shared, LANES), F32)
    size = blocks.shape[1]
    n_out = 3 + (stage < 3) + (stage == 1)
    outs = [tall, send, send] + [tall] * (n_out - 3)
    out_specs = [HBM, VMEM, VMEM] + [HBM] * (n_out - 3)
    in_specs = [SMEM, SMEM, SMEM, SMEM] + ([SMEM, VMEM] if stage == 1 else [VMEM, VMEM])
    in_specs += [HBM, HBM] + ([HBM] if stage > 1 else []) + [HBM]
    fields = [pltpu.VMEM(field, F32)] * (ACCS + 2 + (stage > 1))
    scratch = fields + [
        pltpu.VMEM(blocks.shape, blocks.dtype),
        pltpu.VMEM((2 * size, LANES), F32),
        pltpu.VMEM((2 * size, LANES), F32),
        pltpu.SemaphoreType.DMA((4,)),
        pltpu.SemaphoreType.DMA((blocks.shape[0],)),
    ]
    return pl.pallas_call(
        functools.partial(ham_kernel, stage),
        out_shape=outs,
        in_specs=in_specs,
        out_specs=out_specs,
        scratch_shapes=scratch,
        compiler_params=params(),
        name="ham%d" % stage,
    )(*operands)


def high_low(x):
    high = x.astype(jnp.bfloat16)
    return high, (x - high.astype(F32)).astype(jnp.bfloat16)


def halves(ref, start, size):
    return jnp.concatenate([ref[pl.ds(start + h, size, stride=2), :] for h in range(2)], axis=1)


def finish_kernel(
    counts, position, rows, from_below, from_above, x_hbm, f_hbm, keep, give, w, shared_rows, gram, sems
):
    load = pltpu.make_async_copy(x_hbm, w, sems.at[0])
    load.start()
    shared = from_below.shape[0] // 2
    width = 2 * LANES
    gram[...] = jnp.zeros_like(gram)
    load.wait()
    add_rows(w, rows, 0, from_below)
    add_rows(w, rows, shared, from_above)
    save = pltpu.make_async_copy(w, f_hbm, sems.at[1])
    save.start()
    take_rows(shared_rows, rows, 0, w)
    limit = counts[position[0]]
    n = 256
    dims = (((0,), (0,)), ((), ()))

    def add_chunk(c, carry):
        live = c * n + lax.broadcasted_iota(jnp.int32, (n, width), 0) < limit
        high, low = high_low(jnp.where(live, halves(w, 2 * n * c, n), 0.0))
        gram[...] += lax.dot_general(
            high, jnp.concatenate([high, low], axis=1), dims, preferred_element_type=F32
        )
        return carry

    lax.fori_loop(0, pl.cdiv(limit, n), add_chunk, 0)

    @pl.when(position[0] > 0)
    def _():
        high, low = high_low(halves(shared_rows, 0, shared))
        gram[...] -= lax.dot_general(
            high, jnp.concatenate([high, low], axis=1), dims, preferred_element_type=F32
        )

    cross = gram[:, width:]
    full = gram[:, :width] + (cross + cross.T)
    row = lax.broadcasted_iota(jnp.int32, (LANES, LANES), 0)
    lane = lax.broadcasted_iota(jnp.int32, (LANES, LANES), 1)
    last = full[LANES:, LANES:]
    both = jnp.where(row >= lane, full[:LANES, :LANES], last)
    diagonal = jnp.sum(jnp.where(row == lane, last, 0.0), axis=0, keepdims=True)
    pieces = (
        (both, jnp.broadcast_to(diagonal, (8, LANES))),
        (full[:LANES, LANES:], jnp.zeros((8, LANES), F32)),
    )
    for core in range(2):

        @pl.when(position[0] % 2 == core)
        def _():
            for out, (block, tail) in ((keep, pieces[core]), (give, pieces[1 - core])):
                out[0:LANES, :] = block
                out[LANES : LANES + 8, :] = tail

    save.wait()


def shifted(value, stride, radix, by):
    route = []
    for i in range(lax.axis_size("mesh")):
        digit = i // stride % radix
        route.append((i, i + ((digit + by) % radix - digit) * stride))
    return lax.ppermute(value, "mesh", route)


def sum_over_devices(keep, give):
    total = keep + shifted(give, 1, 2, 1)
    stride, devices = 2, lax.axis_size("mesh")
    while stride < devices:
        radix = min(4, devices // stride)
        got = [shifted(total, stride, radix, by) for by in range(1, radix)]
        for piece in got:
            total = total + piece
        stride *= radix
    return total, shifted(total, 1, 2, 1)


def eliminate(block):
    n = block.shape[0]
    lane = lax.broadcasted_iota(jnp.int32, (8, n), 1)
    sub = lax.broadcasted_iota(jnp.int32, (8, n), 0)
    parts = [block[8 * i : 8 * i + 8, :] for i in range(n // 8)]
    for k in range(n):
        q, s = divmod(k, 8)
        row = parts[q][s : s + 1, :]
        rec = 1.0 / jnp.broadcast_to(row[:, k : k + 1], (1, n))
        row = jnp.broadcast_to(jnp.where(lane[:1] == k, 1.0, row) * rec, (8, n))
        for i in range(q, n // 8):
            col = jnp.broadcast_to(parts[i][:, k : k + 1], (8, n))
            new = jnp.where(lane == k, 0.0, parts[i]) - col * row
            parts[i] = jnp.where(sub > s, new, parts[i]) if i == q else new
    done = []
    for i in range(n // 8):
        here = sub + 8 * i
        pivot = jnp.sum(jnp.where(lane == here, parts[i], 0.0), axis=1, keepdims=True)
        unit = jnp.where(lane < here, parts[i], jnp.where(lane == here, 1.0, 0.0))
        done.append(unit * lax.rsqrt(pivot))
    return jnp.concatenate(done, axis=0)


def dot32(a, b, ca, cb):
    return lax.dot_general(
        a,
        b,
        (((ca,), (cb,)), ((), ())),
        precision=lax.Precision.HIGHEST,
        preferred_element_type=F32,
    )


def rotate_kernel(
    counts, position, mine, other, f_hbm, out_hbm, w, out, block, factors, basis, sems, *, total_of
):
    load = pltpu.make_async_copy(f_hbm, w, sems.at[0])
    load.start()
    total = lax.fori_loop(0, counts.shape[0], lambda i, t: t + counts[i], jnp.int32(0))
    scale = 1.0 / (jnp.full((LANES, LANES), total_of(total), jnp.int32).astype(F32))
    core = jnp.full((LANES + 8, LANES), position[0] % 2, jnp.int32)
    first = jnp.where(core == 0, mine[...], other[...])
    second = jnp.where(core == 0, other[...], mine[...])
    row = lax.broadcasted_iota(jnp.int32, (LANES, LANES), 0)
    lane = lax.broadcasted_iota(jnp.int32, (LANES, LANES), 1)
    both = first[:LANES, :]
    turned = both.T
    block[...] = jnp.where(row >= lane, both, turned) * scale
    right = second[:LANES, :] * scale
    last = jnp.where(row < lane, both, turned)
    last = jnp.where(row == lane, jnp.broadcast_to(first[LANES : LANES + 1, :], (LANES, LANES)), last)
    factors[2] = last * scale

    def panel(p, carry):
        factors[p] = eliminate(block[...])

        @pl.when(p == 0)
        def _():
            side = dot32(factors[0], right, 1, 0)
            block[...] = factors[2] - dot32(side, side, 0, 0)
            factors[2] = side

        return carry

    lax.fori_loop(0, 2, panel, 0)
    n = 2 * LANES
    top = factors[0].T
    low_right = factors[1].T
    corner = -dot32(top, dot32(factors[2], low_right, 1, 0), 1, 0)
    inverse_t = jnp.concatenate(
        [
            jnp.concatenate([top, corner], axis=1),
            jnp.concatenate([jnp.zeros((LANES, LANES), F32), low_right], axis=1),
        ],
        axis=0,
    )
    basis[0:n, :], basis[n : 2 * n, :] = high_low(inverse_t)
    limit = counts[position[0]]
    load.wait()
    size = 512

    def chunk(c, carry):
        at = span(c * size, size)
        high, low = high_low(halves(w, 2 * size * c, size))
        value = jnp.dot(high, basis[0:n, :], preferred_element_type=F32)
        value += jnp.dot(high, basis[n : 2 * n, :], preferred_element_type=F32)
        value += jnp.dot(low, basis[0:n, :], preferred_element_type=F32)
        live = c * size + lax.broadcasted_iota(jnp.int32, (size, n), 0) < limit
        out[at, :] = jnp.where(live, value, 0.0)
        pltpu.make_async_copy(out.at[at, :], out_hbm.at[at, :], sems.at[1]).start()
        return carry

    lax.fori_loop(0, out.shape[0] // size, chunk, 0)
    pltpu.make_async_copy(out, out_hbm, sems.at[1]).wait()


def body(
    states, inv_sqrt_mass, element_blocks, element_nodes, element_counts, node_counts, boundary_rows
):
    position = lax.axis_index("mesh").astype(jnp.int32).reshape(1)
    devices = lax.axis_size("mesh")
    row_total, width = states.shape
    shared = boundary_rows.shape[2]
    field = (2 * row_total, LANES)
    rows = 2 * boundary_rows.reshape(-1)
    nodes = 2 * element_nodes.reshape(-1)
    tall = jax.ShapeDtypeStruct(field, F32)
    send = jax.ShapeDtypeStruct((2 * shared, LANES), F32)

    values, masses = pl.pallas_call(
        send_rows,
        out_shape=[send, jax.ShapeDtypeStruct((shared,), F32)],
        in_specs=[SMEM, SMEM, HBM],
        out_specs=[VMEM, SMEM],
        scratch_shapes=[
            pltpu.VMEM((row_total, LANES), F32),
            pltpu.VMEM((row_total, LANES), F32),
            pltpu.SemaphoreType.DMA((2,)),
        ],
        compiler_params=params(),
        name="send_rows",
    )(rows, inv_sqrt_mass, states)
    owner_mass = passed_along(masses, "mesh", 1)
    owner_vals = passed_along(values, "mesh", 1)
    step = 1024
    w0, m = pl.pallas_call(
        split_rows,
        grid=(row_total // step,),
        out_shape=[tall, tall],
        in_specs=[VMEM, pl.BlockSpec((step, width), lambda i: (i, 0))],
        out_specs=[pl.BlockSpec((2 * step, LANES), lambda i: (i, 0))] * 2,
        compiler_params=params(),
        cost_estimate=pl.CostEstimate(
            flops=row_total * width, bytes_accessed=12 * row_total * width, transcendentals=0
        ),
        name="split_rows",
    )(inv_sqrt_mass.reshape(-1, LANES), states)

    head = (element_counts, position, nodes, rows)
    args = (field, element_blocks, shared)
    w1, up, down, w0, m = ham(1, head + (owner_mass, owner_vals, w0, m, element_blocks), *args)
    up, down = passed_along(up, "mesh", 1), passed_along(down, "mesh", -1)
    w2, up, down, w1 = ham(2, head + (up, down, w1, m, w0, element_blocks), *args)
    up, down = passed_along(up, "mesh", 1), passed_along(down, "mesh", -1)
    w3, up, down = ham(3, head + (up, down, w2, m, w1, element_blocks), *args)
    up, down = passed_along(up, "mesh", 1), passed_along(down, "mesh", -1)
    half = jax.ShapeDtypeStruct((LANES + 8, LANES), F32)
    filtered, keep, give = pl.pallas_call(
        finish_kernel,
        out_shape=[tall, half, half],
        in_specs=[SMEM, SMEM, SMEM, VMEM, VMEM, HBM],
        out_specs=[HBM, VMEM, VMEM],
        scratch_shapes=[
            pltpu.VMEM(field, F32),
            pltpu.VMEM((2 * shared, LANES), F32),
            pltpu.VMEM((width, 2 * width), F32),
            pltpu.SemaphoreType.DMA((2,)),
        ],
        compiler_params=params(),
        name="finish",
    )(node_counts, position, rows, up, down, w3)

    mine, other = sum_over_devices(keep, give)
    return pl.pallas_call(
        functools.partial(rotate_kernel, total_of=lambda t: t - shared * (devices - 1)),
        out_shape=jax.ShapeDtypeStruct(states.shape, F32),
        in_specs=[SMEM, SMEM, VMEM, VMEM, HBM],
        out_specs=HBM,
        scratch_shapes=[
            pltpu.VMEM(field, F32),
            pltpu.VMEM(states.shape, F32),
            pltpu.VMEM((LANES, LANES), F32),
            pltpu.VMEM((3, LANES, LANES), F32),
            pltpu.VMEM((2 * width, width), jnp.bfloat16),
            pltpu.SemaphoreType.DMA((2,)),
        ],
        compiler_params=params(),
        name="rotate",
    )(node_counts, position, mine, other, filtered)


def solution(mesh):
    in_specs = (
        P("mesh", None),
        P("mesh"),
        P("mesh", None, None),
        P("mesh", None),
        P("mesh"),
        P(),
        P("mesh", None, None),
    )
    out_specs = P("mesh", None)
    return jax.shard_map(body, mesh=mesh, in_specs=in_specs, out_specs=out_specs, check_vma=False)
```

time: 423 us -> 230 us (0.54)
  waiting for transfers between devices: 210 us -> 35 us
  other arithmetic: 60.6 us -> 1.66 us
  Pallas kernels: 90.4 us -> 138 us
  starting transfers between devices: 19.5 us -> 47.9 us
  between operations: 16.2 us -> 1 us
  local copies, waits for them, and re-layouts: 15.9 us -> 4.87 us
  matrix products: 10.2 us -> 0 us
    psum x1 -> x0, waiting for transfers between devices: 181 us -> none  [body(): gram = lax.psum(gram, 'mesh')]
    another operation x10 -> x0, other arithmetic: 55.2 us -> none  [the longest x6 34 us: body(): factor = jnp.linalg.cholesky(gram)]
    ppermute x0 -> x11, starting transfers between devices: none -> 28.4 us  [shifted(): return lax.ppermute(value, 'mesh', route)]
    pallas_call x3 -> x4, Pallas kernels: 30.6 us -> 58 us  [the longest x1 29.8 us: body(): pl.pallas_call(functools.partial(rotate_kernel, total_of=lambda t: t - sh...]
    pallas_call x3, Pallas kernels: 59.9 us -> 80.3 us  [ham(): pl.pallas_call(functools.partial(ham_kernel, stage), out_shape=outs, in_s...]
    ppermute x0 -> x11, waiting for transfers between devices: none -> 14.4 us  [shifted(): return lax.ppermute(value, 'mesh', route)]
    dot_general x1 -> x0, matrix products: 8.87 us -> none  [body(): jnp.dot(filtered, inverse.T, precision=lax.Precision.HIGHEST, preferred_e...]
    ppermute x8, waiting for transfers between devices: 28.1 us -> 20.6 us  [passed_along(): return lax.ppermute(block, axis, route)]
  transfers between devices with their start and end apart: 9 -> 19, of which waited for: 7 -> 15; matrix products, arithmetic and copies ran while one was open for 2% -> 0% of each run, Pallas kernels for 3% -> 4%
where the time goes in v2:
time: 230 us; the launch traced here: 229 us
  Pallas kernels  138 us (60%)
  starting transfers between devices  47.9 us (21%)
  waiting for transfers between devices  35 us (15%)
  local copies, waits for them, and re-layouts  4.87 us (2%)
    pallas_call x3, Pallas kernels, ham(): pl.pallas_call(functools.partial(ham_kernel, stage), out_shape=outs, in_s...  80.3 us
    pallas_call x1, Pallas kernels, body(): pl.pallas_call(functools.partial(rotate_kernel, total_of=lambda t: t - sh...  29.8 us
    ppermute x11, starting transfers between devices, shifted(): return lax.ppermute(value, 'mesh', route)  28.4 us
    ppermute x8, waiting for transfers between devices, passed_along(): return lax.ppermute(block, axis, route)  20.6 us
    ppermute x8, starting transfers between devices, passed_along(): return lax.ppermute(block, axis, route)  19.5 us
    ppermute x11, waiting for transfers between devices, shifted(): return lax.ppermute(value, 'mesh', route)  14.4 us
    pallas_call x1, Pallas kernels, body(): pl.pallas_call(finish_kernel, out_shape=[tall, half, half], in_specs=[SME...  13 us
    pallas_call x1, Pallas kernels, body(): pl.pallas_call(split_rows, grid=(row_total // step,), out_shape=[tall, ta...  8.31 us
  transfers between devices with their start and end apart: 19, of which 15 were waited for; matrix products, arithmetic and copies ran while one was open for 0% of the time, Pallas kernels for 4%

profile of v2, /device:TPU:1, one launch (start us, length us, event | category | flops | bytes accessed | tf_op | source)
XLA Modules:
  0.0 228.7 jit_solution(16016346054674641440)
XLA Ops:
  1.3 6.9 %send_rows.1 = (f32[768,128]{1,0:T(8,128)}, f32[384]{0:T(512)}) custom-call(s32[768]{0:T(1024)} %mul.18.rows.refs_3_, f32[6144]{0:T(1024)} %mass.1, f32[6144,256]{1,0:T(8,128)} %states.1), custom_call_target="tpu_custom_call" | custom-call | tf_op jit(solution)/shard_map/send_rows/pallas_call | solution.py:482
  8.2 4.5 %collective-permute-start.1 = (f32[768,128]{1,0:T(8,128)}, f32[768,128]{1,0:T(8,128)S(1)}, u32[]{:S(2)}, u32[]{:S(2)}) collective-permute-start(f32[768,128]{1,0:T(8,128)} %get-tuple-element.25), channel_id=1, source_target_pairs={{0,1},{1,2},{2,3},{3,4},{4,5},{5,6},{6,7},{7,8},{8,9},{9,10},{10,1... | collective-permute-start | bytes 1179656 | tf_op jit(solution)/shard_map/ppermute | solution.py:24
  12.7 1.9 collective-permute-start
  15.9 8.3 %split_rows.1 = (f32[12288,128]{1,0:T(8,128)}, f32[12288,128]{1,0:T(8,128)}) custom-call(f32[48,128]{1,0:T(8,128)} %bitcast.8, f32[6144,256]{1,0:T(8,128)} %states.1), custom_call_target="tpu_custom_call" | custom-call | flops 1572864 | bytes 18874368 | tf_op jit(solution)/shard_map/split_rows/pallas_call | solution.py:498
  25.0 27.5 %ham1.1 = (f32[12288,128]{1,0:T(8,128)}, f32[768,128]{1,0:T(8,128)}, f32[768,128]{1,0:T(8,128)}, f32[12288,128]{1,0:T(8,128)}, f32[12288,128]{1,0:T(8,128)}) custom-call(s32[1]{0:T(128)S(6)} %copy.9.refs_0_, s32[1]{0:T(128)} %bitcast.refs_1_.position, s32[8192]{0:T(1024)} %bitcast.5, s32[768]{0:T(1024)} %mul.18.rows.refs_3_, f32[384]{0:T(512)} %copy-done.10, ...), custom_call_target="tpu_custom_call" | custom-call | tf_op jit(solution)/shard_map/ham1/pallas_call | solution.py:276
  52.4 1.9 collective-permute-start.2
  54.4 2.4 %collective-permute-start.3 = (f32[768,128]{1,0:T(8,128)}, f32[768,128]{1,0:T(8,128)S(1)}, u32[]{:S(2)}, u32[]{:S(2)}) collective-permute-start(f32[768,128]{1,0:T(8,128)} %get-tuple-element.29), channel_id=1, source_target_pairs={{1,0},{2,1},{3,2},{4,3},{5,4},{6,5},{7,6},{8,7},{9,8},{10,9},{11,1... | collective-permute-start | bytes 1179656 | tf_op jit(solution)/shard_map/ppermute | solution.py:24
  56.8 2.6 %collective-permute-done.2.refs_4_ = f32[768,128]{1,0:T(8,128)S(1)} collective-permute-done((f32[768,128]{1,0:T(8,128)}, f32[768,128]{1,0:T(8,128)S(1)}, u32[]{:S(2)}, u32[]{:S(2)}) %collective-permute-start.2) | collective-permute-done | bytes 393248 | tf_op jit(solution)/shard_map/ppermute | solution.py:24
  59.4 4.3 %collective-permute-done.3.refs_5_ = f32[768,128]{1,0:T(8,128)S(1)} collective-permute-done((f32[768,128]{1,0:T(8,128)}, f32[768,128]{1,0:T(8,128)S(1)}, u32[]{:S(2)}, u32[]{:S(2)}) %collective-permute-start.3) | collective-permute-done | bytes 393248 | tf_op jit(solution)/shard_map/ppermute | solution.py:24
  64.4 26.4 %ham2.1 = (f32[12288,128]{1,0:T(8,128)}, f32[768,128]{1,0:T(8,128)}, f32[768,128]{1,0:T(8,128)}, f32[12288,128]{1,0:T(8,128)}) custom-call(s32[1]{0:T(128)S(6)} %copy.9.refs_0_, s32[1]{0:T(128)} %bitcast.refs_1_.position, s32[8192]{0:T(1024)} %bitcast.6, s32[768]{0:T(1024)} %mul.18.rows.refs_3_, f32[768,128]{1,0:T(8,128)} %copy-done.4, ...), custom_call_target="tpu_custom_call" | custom-call | tf_op jit(solution)/shard_map/ham2/pallas_call | solution.py:276
  90.9 1.9 collective-permute-start.4
  92.8 2.4 %collective-permute-start.5 = (f32[768,128]{1,0:T(8,128)}, f32[768,128]{1,0:T(8,128)S(1)}, u32[]{:S(2)}, u32[]{:S(2)}) collective-permute-start(f32[768,128]{1,0:T(8,128)} %get-tuple-element.34), channel_id=1, source_target_pairs={{1,0},{2,1},{3,2},{4,3},{5,4},{6,5},{7,6},{8,7},{9,8},{10,9},{11,1... | collective-permute-start | bytes 1179656 | tf_op jit(solution)/shard_map/ppermute | solution.py:24
  95.2 2.6 %collective-permute-done.4.refs_4_ = f32[768,128]{1,0:T(8,128)S(1)} collective-permute-done((f32[768,128]{1,0:T(8,128)}, f32[768,128]{1,0:T(8,128)S(1)}, u32[]{:S(2)}, u32[]{:S(2)}) %collective-permute-start.4) | collective-permute-done | bytes 393248 | tf_op jit(solution)/shard_map/ppermute | solution.py:24
  97.8 4.3 %collective-permute-done.5.refs_5_ = f32[768,128]{1,0:T(8,128)S(1)} collective-permute-done((f32[768,128]{1,0:T(8,128)}, f32[768,128]{1,0:T(8,128)S(1)}, u32[]{:S(2)}, u32[]{:S(2)}) %collective-permute-start.5) | collective-permute-done | bytes 393248 | tf_op jit(solution)/shard_map/ppermute | solution.py:24
  102.9 26.4 %ham3.1 = (f32[12288,128]{1,0:T(8,128)}, f32[768,128]{1,0:T(8,128)}, f32[768,128]{1,0:T(8,128)}) custom-call(s32[1]{0:T(128)S(6)} %copy.9.refs_0_, s32[1]{0:T(128)} %bitcast.refs_1_.position, s32[8192]{0:T(1024)} %bitcast.7, s32[768]{0:T(1024)} %mul.18.rows.refs_3_, f32[768,128]{1,0:T(8,128)} %copy-done.3, f32[768,128]{1,0:T(8,128)} %copy-done.5, ...), custom_call_target="tpu_custom_call" | custom-call | tf_op jit(solution)/shard_map/ham3/pallas_call | solution.py:276
  129.3 1.9 collective-permute-start.6
  131.2 2.4 %collective-permute-start.7 = (f32[768,128]{1,0:T(8,128)}, f32[768,128]{1,0:T(8,128)S(1)}, u32[]{:S(2)}, u32[]{:S(2)}) collective-permute-start(f32[768,128]{1,0:T(8,128)} %get-tuple-element.38), channel_id=1, source_target_pairs={{1,0},{2,1},{3,2},{4,3},{5,4},{6,5},{7,6},{8,7},{9,8},{10,9},{11,1... | collective-permute-start | bytes 1179656 | tf_op jit(solution)/shard_map/ppermute | solution.py:24
  133.6 2.6 %collective-permute-done.6.from_below = f32[768,128]{1,0:T(8,128)S(1)} collective-permute-done((f32[768,128]{1,0:T(8,128)}, f32[768,128]{1,0:T(8,128)S(1)}, u32[]{:S(2)}, u32[]{:S(2)}) %collective-permute-start.6) | collective-permute-done | bytes 393248 | tf_op jit(solution)/shard_map/ppermute | solution.py:24
  136.2 4.3 %collective-permute-done.7.from_above = f32[768,128]{1,0:T(8,128)S(1)} collective-permute-done((f32[768,128]{1,0:T(8,128)}, f32[768,128]{1,0:T(8,128)S(1)}, u32[]{:S(2)}, u32[]{:S(2)}) %collective-permute-start.7) | collective-permute-done | bytes 393248 | tf_op jit(solution)/shard_map/ppermute | solution.py:24
  141.3 13.0 %finish.1 = (f32[12288,128]{1,0:T(8,128)}, f32[136,128]{1,0:T(8,128)}, f32[136,128]{1,0:T(8,128)}) custom-call(s32[128]{0:T(128)} %counts.3, s32[1]{0:T(128)} %bitcast.refs_1_.position, s32[768]{0:T(1024)} %mul.18.rows.refs_3_, f32[768,128]{1,0:T(8,128)} %copy-done, f32[768,128]{1,0:T(8,128)} %copy-done.1, f32[12288,128]{1,0:T(8,128)} %get-tuple-element.39.x_hbm), custom_call_target="tpu_custom_call" | custom-call | tf_op jit(solution)/shard_map/finish/pallas_call | solution.py:520
  154.4 1.5 collective-permute-done.8
  156.8 3.6 %collective-permute-start.10 = (f32[136,128]{1,0:T(8,128)S(1)}, f32[136,128]{1,0:T(8,128)S(1)}, u32[]{:S(2)}, u32[]{:S(2)}) collective-permute-start(f32[136,128]{1,0:T(8,128)S(1)} %add.30), channel_id=1, source_target_pairs={{0,4},{1,5},{2,6},{3,7},{4,0},{5,1},{6,2},{7,3},{8,12},{9,13},{10,... | collective-permute-start | bytes 208904 | tf_op jit(solution)/shard_map/ppermute | solution.py:358
  161.0 1.6 collective-permute-done.10
  162.6 2.2 collective-permute-done.9
  164.8 9.1 %collective-permute-start.14 = (f32[136,128]{1,0:T(8,128)S(1)}, f32[136,128]{1,0:T(8,128)S(1)}, u32[]{:S(2)}, u32[]{:S(2)}) collective-permute-start(f32[136,128]{1,0:T(8,128)S(1)} %add_add_fusion.2), channel_id=1, source_target_pairs={{0,24},{1,25},{2,26},{3,27},{4,28},{5,29},{6,30},{7,31},{8,0},{9,1... | collective-permute-start | bytes 208904 | tf_op jit(solution)/shard_map/ppermute | solution.py:358
  173.9 3.3 %collective-permute-start.13 = (f32[136,128]{1,0:T(8,128)S(1)}, f32[136,128]{1,0:T(8,128)S(1)}, u32[]{:S(2)}, u32[]{:S(2)}) collective-permute-start(f32[136,128]{1,0:T(8,128)S(1)} %add_add_fusion.2), channel_id=1, source_target_pairs={{0,16},{1,17},{2,18},{3,19},{4,20},{5,21},{6,22},{7,23},{8,24},{9,... | collective-permute-start | bytes 208904 | tf_op jit(solution)/shard_map/ppermute | solution.py:358
  178.8 2.7 %collective-permute-done.12 = f32[136,128]{1,0:T(8,128)S(1)} collective-permute-done((f32[136,128]{1,0:T(8,128)S(1)}, f32[136,128]{1,0:T(8,128)S(1)}, u32[]{:S(2)}, u32[]{:S(2)}) %collective-permute-start.12) | collective-permute-done | bytes 69664 | tf_op jit(solution)/shard_map/ppermute | solution.py:358
  181.5 2.8 %collective-permute-start.17 = (f32[136,128]{1,0:T(8,128)S(1)}, f32[136,128]{1,0:T(8,128)S(1)}, u32[]{:S(2)}, u32[]{:S(2)}) collective-permute-start(f32[136,128]{1,0:T(8,128)S(1)} %add_add_fusion.1), channel_id=1, source_target_pairs={{0,96},{1,97},{2,98},{3,99},{4,100},{5,101},{6,102},{7,103},{8,104... | collective-permute-start | bytes 208904 | tf_op jit(solution)/shard_map/ppermute | solution.py:358
  184.3 4.5 %collective-permute-start.16 = (f32[136,128]{1,0:T(8,128)S(1)}, f32[136,128]{1,0:T(8,128)S(1)}, u32[]{:S(2)}, u32[]{:S(2)}) collective-permute-start(f32[136,128]{1,0:T(8,128)S(1)} %add_add_fusion.1), channel_id=1, source_target_pairs={{0,64},{1,65},{2,66},{3,67},{4,68},{5,69},{6,70},{7,71},{8,72},{9,... | collective-permute-start | bytes 208904 | tf_op jit(solution)/shard_map/ppermute | solution.py:358
  190.6 3.1 %collective-permute-done.15 = f32[136,128]{1,0:T(8,128)S(1)} collective-permute-done((f32[136,128]{1,0:T(8,128)S(1)}, f32[136,128]{1,0:T(8,128)S(1)}, u32[]{:S(2)}, u32[]{:S(2)}) %collective-permute-start.15) | collective-permute-done | bytes 69664 | tf_op jit(solution)/shard_map/ppermute | solution.py:358
  193.7 3.4 %collective-permute-start.18 = (f32[136,128]{1,0:T(8,128)S(1)}, f32[136,128]{1,0:T(8,128)S(1)}, u32[]{:S(2)}, u32[]{:S(2)}) collective-permute-start(f32[136,128]{1,0:T(8,128)S(1)} %add_add_fusion.mine), channel_id=1, source_target_pairs={{0,1},{1,0},{2,3},{3,2},{4,5},{5,4},{6,7},{7,6},{8,9},{9,8},{10,11... | collective-permute-start | bytes 208904 | tf_op jit(solution)/shard_map/ppermute | solution.py:358
  198.7 29.8 %rotate.1 = f32[6144,256]{1,0:T(8,128)} custom-call(s32[128]{0:T(128)} %counts.3, s32[1]{0:T(128)} %bitcast.refs_1_.position, f32[136,128]{1,0:T(8,128)} %copy-done.7, f32[136,128]{1,0:T(8,128)} %copy-done.8, f32[12288,128]{1,0:T(8,128)} %get-tuple-element.42.f_hbm), custom_call_target="tpu_custom_call" | custom-call | tf_op jit(solution)/shard_map/rotate/pallas_call | solution.py:536
  (43 shorter events, 11.6 us)
Async XLA Ops:
  0.0 14.6 %copy-start.9 = (s32[16,512]{1,0:T(8,128)S(1)}, s32[16,512]{1,0:T(8,128)}, u32[]{:S(2)}) copy-start(s32[16,512]{1,0:T(8,128)} %param.10) | copy-start | bytes 98308
  8.2 16.1 %collective-permute-start.1 = (f32[768,128]{1,0:T(8,128)}, f32[768,128]{1,0:T(8,128)S(1)}, u32[]{:S(2)}, u32[]{:S(2)}) collective-permute-start(f32[768,128]{1,0:T(8,128)} %get-tuple-element.25), channel_id=1, source_target_pairs={{0,1},{1,2},{2,3},{3,4},{4,5},{5,6},{6,7},{7,8},{8,9},{9,10},{10,1... | collective-permute-start | bytes 1179656 | tf_op jit(solution)/shard_map/ppermute | solution.py:24
  12.7 11.5 %collective-permute-start = (f32[384]{0:T(512)}, f32[384]{0:T(512)S(1)}, u32[]{:S(2)}, u32[]{:S(2)}) collective-permute-start(f32[384]{0:T(512)} %get-tuple-element.24), channel_id=1, source_target_pairs={{0,1},{1,2},{2,3},{3,4},{4,5},{5,6},{6,7},{7,8},{8,9},{9,10},{10,1... | collective-permute-start | bytes 4616 | tf_op jit(solution)/shard_map/ppermute | solution.py:24
  24.2 0.6 copy-start.10
  24.2 0.8 copy-start.2
  52.4 6.9 %collective-permute-start.2 = (f32[768,128]{1,0:T(8,128)}, f32[768,128]{1,0:T(8,128)S(1)}, u32[]{:S(2)}, u32[]{:S(2)}) collective-permute-start(f32[768,128]{1,0:T(8,128)} %get-tuple-element.28), channel_id=1, source_target_pairs={{0,1},{1,2},{2,3},{3,4},{4,5},{5,6},{6,7},{7,8},{8,9},{9,10},{10,1... | collective-permute-start | bytes 1179656 | tf_op jit(solution)/shard_map/ppermute | solution.py:24
  54.4 9.3 %collective-permute-start.3 = (f32[768,128]{1,0:T(8,128)}, f32[768,128]{1,0:T(8,128)S(1)}, u32[]{:S(2)}, u32[]{:S(2)}) collective-permute-start(f32[768,128]{1,0:T(8,128)} %get-tuple-element.29), channel_id=1, source_target_pairs={{1,0},{2,1},{3,2},{4,3},{5,4},{6,5},{7,6},{8,7},{9,8},{10,9},{11,1... | collective-permute-start | bytes 1179656 | tf_op jit(solution)/shard_map/ppermute | solution.py:24
  59.4 4.3 %copy-start.4 = (f32[768,128]{1,0:T(8,128)}, f32[768,128]{1,0:T(8,128)S(1)}, u32[]{:S(2)}) copy-start(f32[768,128]{1,0:T(8,128)S(1)} %collective-permute-done.2.refs_4_) | copy-start | bytes 1179652
  63.7 0.8 copy-start.6
  90.9 6.9 %collective-permute-start.4 = (f32[768,128]{1,0:T(8,128)}, f32[768,128]{1,0:T(8,128)S(1)}, u32[]{:S(2)}, u32[]{:S(2)}) collective-permute-start(f32[768,128]{1,0:T(8,128)} %get-tuple-element.33), channel_id=1, source_target_pairs={{0,1},{1,2},{2,3},{3,4},{4,5},{5,6},{6,7},{7,8},{8,9},{9,10},{10,1... | collective-permute-start | bytes 1179656 | tf_op jit(solution)/shard_map/ppermute | solution.py:24
  92.8 9.3 %collective-permute-start.5 = (f32[768,128]{1,0:T(8,128)}, f32[768,128]{1,0:T(8,128)S(1)}, u32[]{:S(2)}, u32[]{:S(2)}) collective-permute-start(f32[768,128]{1,0:T(8,128)} %get-tuple-element.34), channel_id=1, source_target_pairs={{1,0},{2,1},{3,2},{4,3},{5,4},{6,5},{7,6},{8,7},{9,8},{10,9},{11,1... | collective-permute-start | bytes 1179656 | tf_op jit(solution)/shard_map/ppermute | solution.py:24
  97.8 4.3 %copy-start.3 = (f32[768,128]{1,0:T(8,128)}, f32[768,128]{1,0:T(8,128)S(1)}, u32[]{:S(2)}) copy-start(f32[768,128]{1,0:T(8,128)S(1)} %collective-permute-done.4.refs_4_) | copy-start | bytes 1179652
  102.1 0.8 copy-start.5
  129.3 6.9 %collective-permute-start.6 = (f32[768,128]{1,0:T(8,128)}, f32[768,128]{1,0:T(8,128)S(1)}, u32[]{:S(2)}, u32[]{:S(2)}) collective-permute-start(f32[768,128]{1,0:T(8,128)} %get-tuple-element.37), channel_id=1, source_target_pairs={{0,1},{1,2},{2,3},{3,4},{4,5},{5,6},{6,7},{7,8},{8,9},{9,10},{10,1... | collective-permute-start | bytes 1179656 | tf_op jit(solution)/shard_map/ppermute | solution.py:24
  131.2 9.3 %collective-permute-start.7 = (f32[768,128]{1,0:T(8,128)}, f32[768,128]{1,0:T(8,128)S(1)}, u32[]{:S(2)}, u32[]{:S(2)}) collective-permute-start(f32[768,128]{1,0:T(8,128)} %get-tuple-element.38), channel_id=1, source_target_pairs={{1,0},{2,1},{3,2},{4,3},{5,4},{6,5},{7,6},{8,7},{9,8},{10,9},{11,1... | collective-permute-start | bytes 1179656 | tf_op jit(solution)/shard_map/ppermute | solution.py:24
  136.2 4.3 %copy-start = (f32[768,128]{1,0:T(8,128)}, f32[768,128]{1,0:T(8,128)S(1)}, u32[]{:S(2)}) copy-start(f32[768,128]{1,0:T(8,128)S(1)} %collective-permute-done.6.from_below) | copy-start | bytes 1179652
  140.5 0.8 copy-start.1
  154.3 1.6 collective-permute-start.8
  156.7 4.3 %collective-permute-start.11 = (f32[136,128]{1,0:T(8,128)S(1)}, f32[136,128]{1,0:T(8,128)S(1)}, u32[]{:S(2)}, u32[]{:S(2)}) collective-permute-start(f32[136,128]{1,0:T(8,128)S(1)} %add.30), channel_id=1, source_target_pairs={{0,6},{1,7},{2,0},{3,1},{4,2},{5,3},{6,4},{7,5},{8,14},{9,15},{10,... | collective-permute-start | bytes 208904 | tf_op jit(solution)/shard_map/ppermute | solution.py:358
  156.8 5.8 %collective-permute-start.10 = (f32[136,128]{1,0:T(8,128)S(1)}, f32[136,128]{1,0:T(8,128)S(1)}, u32[]{:S(2)}, u32[]{:S(2)}) collective-permute-start(f32[136,128]{1,0:T(8,128)S(1)} %add.30), channel_id=1, source_target_pairs={{0,4},{1,5},{2,6},{3,7},{4,0},{5,1},{6,2},{7,3},{8,12},{9,13},{10,... | collective-permute-start | bytes 208904 | tf_op jit(solution)/shard_map/ppermute | solution.py:358
  160.4 4.4 %collective-permute-start.9 = (f32[136,128]{1,0:T(8,128)S(1)}, f32[136,128]{1,0:T(8,128)S(1)}, u32[]{:S(2)}, u32[]{:S(2)}) collective-permute-start(f32[136,128]{1,0:T(8,128)S(1)} %add.30), channel_id=1, source_target_pairs={{0,2},{1,3},{2,4},{3,5},{4,6},{5,7},{6,0},{7,1},{8,10},{9,11},{10,... | collective-permute-start | bytes 208904 | tf_op jit(solution)/shard_map/ppermute | solution.py:358
  164.8 13.1 %collective-permute-start.14 = (f32[136,128]{1,0:T(8,128)S(1)}, f32[136,128]{1,0:T(8,128)S(1)}, u32[]{:S(2)}, u32[]{:S(2)}) collective-permute-start(f32[136,128]{1,0:T(8,128)S(1)} %add_add_fusion.2), channel_id=1, source_target_pairs={{0,24},{1,25},{2,26},{3,27},{4,28},{5,29},{6,30},{7,31},{8,0},{9,1... | collective-permute-start | bytes 208904 | tf_op jit(solution)/shard_map/ppermute | solution.py:358
  173.9 5.0 %collective-permute-start.13 = (f32[136,128]{1,0:T(8,128)S(1)}, f32[136,128]{1,0:T(8,128)S(1)}, u32[]{:S(2)}, u32[]{:S(2)}) collective-permute-start(f32[136,128]{1,0:T(8,128)S(1)} %add_add_fusion.2), channel_id=1, source_target_pairs={{0,16},{1,17},{2,18},{3,19},{4,20},{5,21},{6,22},{7,23},{8,24},{9,... | collective-permute-start | bytes 208904 | tf_op jit(solution)/shard_map/ppermute | solution.py:358
  177.1 4.4 %collective-permute-start.12 = (f32[136,128]{1,0:T(8,128)S(1)}, f32[136,128]{1,0:T(8,128)S(1)}, u32[]{:S(2)}, u32[]{:S(2)}) collective-permute-start(f32[136,128]{1,0:T(8,128)S(1)} %add_add_fusion.2), channel_id=1, source_target_pairs={{0,8},{1,9},{2,10},{3,11},{4,12},{5,13},{6,14},{7,15},{8,16},{9,17... | collective-permute-start | bytes 208904 | tf_op jit(solution)/shard_map/ppermute | solution.py:358
  181.5 8.1 %collective-permute-start.17 = (f32[136,128]{1,0:T(8,128)S(1)}, f32[136,128]{1,0:T(8,128)S(1)}, u32[]{:S(2)}, u32[]{:S(2)}) collective-permute-start(f32[136,128]{1,0:T(8,128)S(1)} %add_add_fusion.1), channel_id=1, source_target_pairs={{0,96},{1,97},{2,98},{3,99},{4,100},{5,101},{6,102},{7,103},{8,104... | collective-permute-start | bytes 208904 | tf_op jit(solution)/shard_map/ppermute | solution.py:358
  184.3 6.2 %collective-permute-start.16 = (f32[136,128]{1,0:T(8,128)S(1)}, f32[136,128]{1,0:T(8,128)S(1)}, u32[]{:S(2)}, u32[]{:S(2)}) collective-permute-start(f32[136,128]{1,0:T(8,128)S(1)} %add_add_fusion.1), channel_id=1, source_target_pairs={{0,64},{1,65},{2,66},{3,67},{4,68},{5,69},{6,70},{7,71},{8,72},{9,... | collective-permute-start | bytes 208904 | tf_op jit(solution)/shard_map/ppermute | solution.py:358
  188.9 4.8 %collective-permute-start.15 = (f32[136,128]{1,0:T(8,128)S(1)}, f32[136,128]{1,0:T(8,128)S(1)}, u32[]{:S(2)}, u32[]{:S(2)}) collective-permute-start(f32[136,128]{1,0:T(8,128)S(1)} %add_add_fusion.1), channel_id=1, source_target_pairs={{0,32},{1,33},{2,34},{3,35},{4,36},{5,37},{6,38},{7,39},{8,40},{9,... | collective-permute-start | bytes 208904 | tf_op jit(solution)/shard_map/ppermute | solution.py:358
  193.7 4.4 %copy-start.7 = (f32[136,128]{1,0:T(8,128)}, f32[136,128]{1,0:T(8,128)S(1)}, u32[]{:S(2)}) copy-start(f32[136,128]{1,0:T(8,128)S(1)} %add_add_fusion.mine) | copy-start | bytes 208900
  193.7 4.3 %collective-permute-start.18 = (f32[136,128]{1,0:T(8,128)S(1)}, f32[136,128]{1,0:T(8,128)S(1)}, u32[]{:S(2)}, u32[]{:S(2)}) collective-permute-start(f32[136,128]{1,0:T(8,128)S(1)} %add_add_fusion.mine), channel_id=1, source_target_pairs={{0,1},{1,0},{2,3},{3,2},{4,5},{5,4},{6,7},{7,6},{8,9},{9,8},{10,11... | collective-permute-start | bytes 208904 | tf_op jit(solution)/shard_map/ppermute | solution.py:358
  198.1 0.6 copy-start.8

commit v3 on v2

v3 whole, which is shorter than its diff:
```python
import functools

import jax
import jax.numpy as jnp
from jax import lax
from jax.experimental import pallas as pl
from jax.experimental.pallas import tpu as pltpu
from jax.sharding import PartitionSpec as P

CENTER = 0.5
HALF_WIDTH = 1.5
LANES = 128
ACCS = 4
UNROLL = 64
F32 = jnp.float32
SMEM = pl.BlockSpec(memory_space=pltpu.SMEM)
VMEM = pl.BlockSpec(memory_space=pltpu.VMEM)
HBM = pl.BlockSpec(memory_space=pl.ANY)
KEPT = object()


def passed_along(block, axis, distance):
    devices = range(lax.axis_size(axis))
    route = [(i - distance, i) for i in devices if i - distance in devices]
    return lax.ppermute(block, axis, route)


def pair(offset):
    return pl.ds(pl.multiple_of(offset, 2), 2)


def span(start, size):
    return pl.ds(pl.multiple_of(start, size), size)


def call(name, kernel, ins, outs, aliases=None, scratch=(), mib=8, flops=0):
    operands, in_specs = [], []
    for value, spec in ins:
        if spec is KEPT:
            value = pltpu.with_memory_space_constraint(value, pltpu.VMEM)
        elif spec is HBM:
            value = pltpu.with_memory_space_constraint(value, pltpu.HBM)
        operands.append(value)
        in_specs.append(VMEM if spec is KEPT else spec)
    return pl.pallas_call(
        kernel,
        out_shape=[
            pltpu.VMEM(shape, dtype) if spec is KEPT else jax.ShapeDtypeStruct(shape, dtype)
            for (shape, dtype), spec in outs
        ],
        in_specs=in_specs,
        out_specs=[VMEM if spec is KEPT else spec for _, spec in outs],
        input_output_aliases=aliases or {},
        scratch_shapes=list(scratch),
        compiler_params=pltpu.CompilerParams(vmem_limit_bytes=mib * 2**20),
        cost_estimate=pl.CostEstimate(flops=flops, bytes_accessed=flops, transcendentals=0),
        name=name,
    )(*operands)


def start_kernel(position, rows, mass_all, states_hbm, w, m, send, stage, picked, sems):
    count = mass_all.shape[0]
    total = count * LANES
    group = 8
    parts = count // group

    def load(part, h):
        at = span(part * group * LANES, group * LANES)
        return pltpu.make_async_copy(
            states_hbm.at[at, h * LANES : (h + 1) * LANES], stage.at[h, at, :], sems.at[part, h]
        )

    for part in range(parts):
        for h in range(2):
            load(part, h).start()
    for part in range(parts):
        for h in range(2):
            load(part, h).wait()

        def convert(i, carry):
            at = part * group + i
            mass = jnp.broadcast_to(mass_all[pl.ds(at, 1), :], (LANES, LANES)).T
            base = 2 * LANES * at
            for h in range(2):
                m[pl.ds(base + h, LANES, stride=2), :] = mass
                w[pl.ds(base + h, LANES, stride=2), :] = mass * stage[h, span(LANES * at, LANES), :]
            return carry

        lax.fori_loop(0, group, convert, 0)
    shared = picked.shape[0]
    take_rows(send.at[0 : 2 * shared, :], rows, shared, w)
    unroll = 32

    def pick(g, carry):
        some = rows.at[pl.ds(shared + g * unroll, unroll)]
        for k in range(unroll):
            picked[pl.ds(g * unroll + k, 1), :] = m[pl.ds(some[k], 1), :]
        return carry

    lax.fori_loop(0, shared // unroll, pick, 0)
    diagonal = lax.broadcasted_iota(jnp.int32, (LANES, LANES), 0) == lax.broadcasted_iota(
        jnp.int32, (LANES, LANES), 1
    )
    send[2 * shared : 2 * shared + 8, :] = jnp.zeros((8, LANES), F32)
    for i in range(shared // LANES):
        block = picked[i * LANES : (i + 1) * LANES, :]
        line = jnp.sum(jnp.where(diagonal, block, 0.0), axis=0, keepdims=True)
        send[2 * shared + i : 2 * shared + i + 1, :] = line


def clear_kernel(after, *accs):
    chunk = 512

    def clear(c, carry):
        for acc in accs:
            acc[span(c * chunk, chunk), :] = jnp.zeros((chunk, LANES), F32)
        return carry

    lax.fori_loop(0, accs[0].shape[0] // chunk, clear, 0)


def take_rows(out, rows, base, *sources):
    group = 32

    def step(g, carry):
        some = rows.at[pl.ds(base + g * group, group)]
        first = pl.multiple_of(2 * g * group, 2 * group)
        for k in range(group):
            at = pair(some[k])
            total = sources[0][at, :]
            for source in sources[1:]:
                total = total + source[at, :]
            out[pl.ds(first + 2 * k, 2), :] = total
        return carry

    lax.fori_loop(0, out.shape[0] // (2 * group), step, 0)


def add_rows(target, rows, base, source, m, scale):
    group = 16

    def step(g, carry):
        some = rows.at[pl.ds(base + g * group, group)]
        first = pl.multiple_of(2 * g * group, 2 * group)
        at = [pair(some[k]) for k in range(group)]
        new = []
        for k in range(group):
            mass = m[at[k], :]
            new.append(target[at[k], :] + scale * (mass * mass) * source[pl.ds(first + 2 * k, 2), :])
        for k in range(group):
            target[at[k], :] = new[k]
        return carry

    lax.fori_loop(0, source.shape[0] // (2 * group), step, 0)


def near_base(position, shared):
    return jnp.where(position % 2 == 0, shared, 0)


def ham_kernel(stage, *refs):
    count, position, nodes, rows = refs[:4]
    n_in = 1 if stage == 1 else 2
    received = refs[4 : 4 + n_in]
    refs = refs[4 + n_in :]
    n_field = 2 + ACCS
    blocks_hbm = refs[n_field]
    refs = refs[n_field + 1 :]
    w, m, *accs = refs[:n_field]
    send_near, send_far, picked, parts, lines, blocks, sems = refs[n_field:]

    shared = send_near.shape[0] // 2
    size = picked.shape[0] // 2
    live = count[0]
    near = near_base(position[0], shared)
    far = shared - near

    def load(e):
        return pltpu.make_async_copy(blocks_hbm.at[e], blocks.at[e % 2], sems.at[e % 2])

    load(0).start()

    if stage == 1:
        (owner,) = received

        @pl.when(position[0] > 0)
        def _():
            for i in range(shared // LANES):
                line = owner[2 * shared + i : 2 * shared + i + 1, :]
                lines[i * LANES : (i + 1) * LANES, :] = jnp.broadcast_to(line, (LANES, LANES)).T
            unroll = 16

            def patch(g, carry):
                some = rows.at[pl.ds(g * unroll, unroll)]
                first = pl.multiple_of(g * unroll, unroll)
                for k in range(unroll):
                    at = pair(some[k])
                    w[at, :] = owner[pl.ds(2 * first + 2 * k, 2), :]
                    m[at, :] = jnp.broadcast_to(lines[pl.ds(first + k, 1), :], (2, LANES))
                return carry

            lax.fori_loop(0, shared // unroll, patch, 0)
    else:
        scale = (1.0 if stage == 2 else 2.0) / HALF_WIDTH
        add_rows(w, rows, near, received[0], m, scale)
        add_rows(w, rows, far, received[1], m, scale)

    def product(e):
        load(e).wait()

        @pl.when(e + 1 < live)
        def _():
            load(e + 1).start()

        x = jnp.concatenate(
            [picked[pl.ds(h, size, stride=2), :].astype(jnp.bfloat16) for h in range(2)], axis=1
        )
        part = jnp.dot(blocks[e % 2], x, preferred_element_type=F32)
        for h in range(2):
            parts[pl.ds(h, size, stride=2), :] = part[:, h * LANES : (h + 1) * LANES]

    take_rows(picked, nodes, 0, w)
    product(0)

    def element(e, carry):
        later = jnp.minimum(e + 1, live - 1)

        def move(g, inner):
            here = nodes.at[pl.ds(e * size + g * UNROLL, UNROLL)]
            ahead = nodes.at[pl.ds(later * size + g * UNROLL, UNROLL)]
            first = pl.multiple_of(2 * g * UNROLL, 2 * UNROLL)
            for k in range(UNROLL):
                line = pl.ds(first + 2 * k, 2)
                picked[line, :] = w[pair(ahead[k]), :]
                at = pair(here[k])
                acc = accs[k % ACCS]
                acc[at, :] = acc[at, :] + parts[line, :]
            return inner

        lax.fori_loop(0, size // UNROLL, move, 0)

        @pl.when(e + 1 < live)
        def _():
            product(later)

        return carry

    lax.fori_loop(0, live, element, 0)
    take_rows(send_near, rows, near, *accs)
    take_rows(send_far, rows, far, *accs)


def combine_kernel(stage, *refs):
    n = 2 + ACCS + (stage > 1)
    w, m = refs[:2]
    accs = refs[n - ACCS : n]
    old = refs[2] if stage > 1 else None
    new, *emptied = refs[n:]
    factor = 1.0 if stage == 1 else 2.0
    scale_h = factor / HALF_WIDTH
    scale_w = -factor * CENTER / HALF_WIDTH
    chunk = 256

    def step(c, carry):
        at = span(c * chunk, chunk)
        total = accs[0][at, :]
        for acc in accs[1:]:
            total = total + acc[at, :]
        mass = m[at, :]
        rest = scale_w * w[at, :]
        if stage > 1:
            rest = rest - old[at, :]
        if stage < 3:
            new[at, :] = scale_h * (mass * mass) * total + rest
        else:
            new[at, :] = scale_h * mass * total + rest / mass
        for acc in emptied:
            acc[at, :] = jnp.zeros((chunk, LANES), F32)
        return carry

    lax.fori_loop(0, w.shape[0] // chunk, step, 0)


def high_low(x):
    high = x.astype(jnp.bfloat16)
    return high, (x - high.astype(F32)).astype(jnp.bfloat16)


def halves(ref, start, size):
    return jnp.concatenate([ref[pl.ds(start + h, size, stride=2), :] for h in range(2)], axis=1)


def add_square(gram, value, size):
    high, low = high_low(value)
    gram[...] += lax.dot_general(
        high,
        jnp.concatenate([high, low], axis=1),
        (((0,), (0,)), ((), ())),
        preferred_element_type=F32,
    )


def inner_kernel(counts, position, rows, f_in, f, saved, gram):
    shared = saved.shape[0] // 4
    take_rows(saved, rows, 0, f)
    unroll = 32

    def blank(g, carry):
        some = rows.at[pl.ds(g * unroll, unroll)]
        for k in range(unroll):
            f[pair(some[k]), :] = jnp.zeros((2, LANES), F32)
        return carry

    lax.fori_loop(0, 2 * shared // unroll, blank, 0)
    gram[...] = jnp.zeros_like(gram)
    limit = counts[position[0]]
    n = 256

    def add_chunk(c, carry):
        live = c * n + lax.broadcasted_iota(jnp.int32, (n, 2 * LANES), 0) < limit
        add_square(gram, jnp.where(live, halves(f, 2 * n * c, n), 0.0), n)
        return carry

    lax.fori_loop(0, pl.cdiv(limit, n), add_chunk, 0)


def finish_kernel(
    position, rows, near_in, far_in, m, saved_in, gram_in, f_in, f, keep, give, saved, gram
):
    shared = near_in.shape[0] // 2
    width = 2 * LANES
    near = near_base(position[0], shared)
    far = shared - near
    scale = 2.0 / HALF_WIDTH
    group = 16

    def step(g, carry):
        for base, source in ((near, near_in), (far, far_in)):
            some = rows.at[pl.ds(base + g * group, group)]
            first = pl.multiple_of(2 * g * group, 2 * group)
            for k in range(group):
                at = pair(some[k])
                line = pair(2 * base + first + 2 * k)
                value = saved_in[line, :] + scale * m[at, :] * source[pl.ds(first + 2 * k, 2), :]
                saved[line, :] = value
                f[at, :] = value
        return carry

    lax.fori_loop(0, shared // group, step, 0)
    gram[...] = gram_in[...]
    add_square(gram, halves(saved, 2 * shared, shared), shared)

    @pl.when(position[0] == 0)
    def _():
        add_square(gram, halves(saved, 0, shared), shared)

    cross = gram[:, width:]
    full = gram[:, :width] + (cross + cross.T)
    row = lax.broadcasted_iota(jnp.int32, (LANES, LANES), 0)
    lane = lax.broadcasted_iota(jnp.int32, (LANES, LANES), 1)
    last = full[LANES:, LANES:]
    both = jnp.where(row >= lane, full[:LANES, :LANES], last)
    diagonal = jnp.sum(jnp.where(row == lane, last, 0.0), axis=0, keepdims=True)
    pieces = (
        (both, jnp.broadcast_to(diagonal, (8, LANES))),
        (full[:LANES, LANES:], jnp.zeros((8, LANES), F32)),
    )
    for core in range(2):

        @pl.when(position[0] % 2 == core)
        def _():
            for out, (block, tail) in ((keep, pieces[core]), (give, pieces[1 - core])):
                out[0:LANES, :] = block
                out[LANES : LANES + 8, :] = tail


def shifted(value, stride, radix, by):
    route = []
    for i in range(lax.axis_size("mesh")):
        digit = i // stride % radix
        route.append((i, i + ((digit + by) % radix - digit) * stride))
    return lax.ppermute(value, "mesh", route)


def add_kernel(*refs):
    total = refs[0][...]
    for ref in refs[1:-1]:
        total = total + ref[...]
    refs[-1][...] = total


def added(*values):
    ins = [(value, VMEM) for value in values]
    return call("add", add_kernel, ins, [((values[0].shape, F32), VMEM)], mib=1)[0]


def sum_over_devices(keep, give):
    total = added(keep, shifted(give, 1, 2, 1))
    stride, devices = 2, lax.axis_size("mesh")
    while stride < devices:
        radix = min(4, devices // stride)
        got = [shifted(total, stride, radix, by) for by in range(1, radix)]
        total = added(total, *got)
        stride *= radix
    return total, shifted(total, 1, 2, 1)


def eliminate(block):
    n = block.shape[0]
    lane = lax.broadcasted_iota(jnp.int32, (8, n), 1)
    sub = lax.broadcasted_iota(jnp.int32, (8, n), 0)
    parts = [block[8 * i : 8 * i + 8, :] for i in range(n // 8)]
    for k in range(n):
        q, s = divmod(k, 8)
        row = parts[q][s : s + 1, :]
        rec = 1.0 / jnp.broadcast_to(row[:, k : k + 1], (1, n))
        row = jnp.broadcast_to(jnp.where(lane[:1] == k, 1.0, row) * rec, (8, n))
        for i in range(q, n // 8):
            col = jnp.broadcast_to(parts[i][:, k : k + 1], (8, n))
            new = jnp.where(lane == k, 0.0, parts[i]) - col * row
            parts[i] = jnp.where(sub > s, new, parts[i]) if i == q else new
    done = []
    for i in range(n // 8):
        here = sub + 8 * i
        pivot = jnp.sum(jnp.where(lane == here, parts[i], 0.0), axis=1, keepdims=True)
        unit = jnp.where(lane < here, parts[i], jnp.where(lane == here, 1.0, 0.0))
        done.append(unit * lax.rsqrt(pivot))
    return jnp.concatenate(done, axis=0)


def dot32(a, b, ca, cb):
    return lax.dot_general(
        a,
        b,
        (((ca,), (cb,)), ((), ())),
        precision=lax.Precision.HIGHEST,
        preferred_element_type=F32,
    )


def rotate_kernel(
    counts, position, mine, other, w, out_hbm, out, block, factors, basis, sems, *, total_of
):
    total = lax.fori_loop(0, counts.shape[0], lambda i, t: t + counts[i], jnp.int32(0))
    scale = 1.0 / (jnp.full((LANES, LANES), total_of(total), jnp.int32).astype(F32))
    core = jnp.full((LANES + 8, LANES), position[0] % 2, jnp.int32)
    first = jnp.where(core == 0, mine[...], other[...])
    second = jnp.where(core == 0, other[...], mine[...])
    row = lax.broadcasted_iota(jnp.int32, (LANES, LANES), 0)
    lane = lax.broadcasted_iota(jnp.int32, (LANES, LANES), 1)
    both = first[:LANES, :]
    turned = both.T
    block[...] = jnp.where(row >= lane, both, turned) * scale
    right = second[:LANES, :] * scale
    last = jnp.where(row < lane, both, turned)
    last = jnp.where(row == lane, jnp.broadcast_to(first[LANES : LANES + 1, :], (LANES, LANES)), last)
    factors[2] = last * scale

    def panel(p, carry):
        factors[p] = eliminate(block[...])

        @pl.when(p == 0)
        def _():
            side = dot32(factors[0], right, 1, 0)
            block[...] = factors[2] - dot32(side, side, 0, 0)
            factors[2] = side

        return carry

    lax.fori_loop(0, 2, panel, 0)
    n = 2 * LANES
    top = factors[0].T
    low_right = factors[1].T
    corner = -dot32(top, dot32(factors[2], low_right, 1, 0), 1, 0)
    inverse_t = jnp.concatenate(
        [
            jnp.concatenate([top, corner], axis=1),
            jnp.concatenate([jnp.zeros((LANES, LANES), F32), low_right], axis=1),
        ],
        axis=0,
    )
    basis[0:n, :], basis[n : 2 * n, :] = high_low(inverse_t)
    limit = counts[position[0]]
    size = 512

    def chunk(c, carry):
        at = span(c * size, size)
        high, low = high_low(halves(w, 2 * size * c, size))
        value = jnp.dot(high, basis[0:n, :], preferred_element_type=F32)
        value += jnp.dot(high, basis[n : 2 * n, :], preferred_element_type=F32)
        value += jnp.dot(low, basis[0:n, :], preferred_element_type=F32)
        live = c * size + lax.broadcasted_iota(jnp.int32, (size, n), 0) < limit
        out[at, :] = jnp.where(live, value, 0.0)
        pltpu.make_async_copy(out.at[at, :], out_hbm.at[at, :], sems.at[0]).start()
        return carry

    lax.fori_loop(0, out.shape[0] // size, chunk, 0)
    pltpu.make_async_copy(out, out_hbm, sems.at[0]).wait()


def exchanged(near, far):
    n = lax.axis_size("mesh")
    far = lax.ppermute(far, "mesh", [(i, i - 1 + 2 * (i % 2)) for i in range(1, n - 1)])
    near = lax.ppermute(near, "mesh", [(i, i ^ 1) for i in range(n)])
    return near, far


def body(
    states, inv_sqrt_mass, element_blocks, element_nodes, element_counts, node_counts, boundary_rows
):
    position = lax.axis_index("mesh").astype(jnp.int32).reshape(1)
    devices = lax.axis_size("mesh")
    row_total, width = states.shape
    shared = boundary_rows.shape[2]
    size = element_blocks.shape[1]
    rows = 2 * boundary_rows.reshape(-1)
    nodes = 2 * element_nodes.reshape(-1)
    tall = ((2 * row_total, LANES), F32)
    send = ((2 * shared, LANES), F32)
    mass_rows = inv_sqrt_mass.reshape(-1, LANES)

    w0, m, values = call(
        "start",
        start_kernel,
        [(position, SMEM), (rows, SMEM), (mass_rows, VMEM), (states, HBM)],
        [(tall, KEPT), (tall, KEPT), (((2 * shared + 8, LANES), F32), VMEM)],
        scratch=[
            pltpu.VMEM((2, row_total, LANES), F32),
            pltpu.VMEM((shared, LANES), F32),
            pltpu.SemaphoreType.DMA((mass_rows.shape[0] // 8, 2)),
        ],
        mib=12,
    )
    owner = passed_along(values, "mesh", 1)
    accs = call(
        "clear",
        clear_kernel,
        [(w0, KEPT)],
        [(tall, KEPT)] * ACCS,
        mib=1,
        flops=10 * row_total * width,
    )

    def ham(stage, received, w, m, accs):
        ins = [(element_counts, SMEM), (position, SMEM), (nodes, SMEM), (rows, SMEM)]
        ins += [(r, VMEM) for r in received]
        first = len(ins)
        ins += [(v, KEPT) for v in (w, m, *accs)] + [(element_blocks, HBM)]
        w, m, *accs, near, far = call(
            "ham%d" % stage,
            functools.partial(ham_kernel, stage),
            ins,
            [(tall, KEPT)] * (2 + ACCS) + [(send, VMEM)] * 2,
            aliases={first + i: i for i in range(2 + ACCS)},
            scratch=[
                pltpu.VMEM((2 * size, LANES), F32),
                pltpu.VMEM((2 * size, LANES), F32),
                pltpu.VMEM((shared, LANES), F32),
                pltpu.VMEM((2, *element_blocks.shape[1:]), element_blocks.dtype),
                pltpu.SemaphoreType.DMA((2,)),
            ],
            mib=4,
        )
        return w, m, accs, near, far

    def combine(stage, w, m, old, accs):
        ins = [(w, KEPT), (m, KEPT)] + ([(old, KEPT)] if stage > 1 else [])
        first = len(ins)
        ins += [(acc, KEPT) for acc in accs]
        aliases = {first + i: 1 + i for i in range(ACCS)}
        if stage > 1:
            aliases[2] = 0
        new, *accs = call(
            "combine%d" % stage,
            functools.partial(combine_kernel, stage),
            ins,
            [(tall, KEPT)] * (1 + ACCS),
            aliases=aliases,
            mib=1,
            flops=10 * row_total * width,
        )
        return new, accs

    w0, m, accs, near, far = ham(1, [owner], w0, m, accs)
    received = exchanged(near, far)
    w1, accs = combine(1, w0, m, None, accs)
    w1, m, accs, near, far = ham(2, received, w1, m, accs)
    received = exchanged(near, far)
    w2, accs = combine(2, w1, m, w0, accs)
    w2, m, accs, near, far = ham(3, received, w2, m, accs)
    received = exchanged(near, far)
    f, accs = combine(3, w2, m, w1, accs)
    wide = ((width, 2 * width), F32)
    pool = ((4 * shared, LANES), F32)
    f, saved, gram = call(
        "inner",
        inner_kernel,
        [(node_counts, SMEM), (position, SMEM), (rows, SMEM), (f, KEPT)],
        [(tall, KEPT), (pool, KEPT), (wide, KEPT)],
        aliases={3: 0},
        mib=4,
        flops=10 * row_total * width,
    )
    half = ((LANES + 8, LANES), F32)
    f, keep, give = call(
        "finish",
        finish_kernel,
        [(position, SMEM), (rows, SMEM), (received[0], VMEM), (received[1], VMEM)]
        + [(m, KEPT), (saved, KEPT), (gram, KEPT), (f, KEPT)],
        [(tall, KEPT), (half, VMEM), (half, VMEM)],
        aliases={7: 0},
        scratch=[pltpu.VMEM(*pool), pltpu.VMEM(*wide)],
        mib=4,
    )
    mine, other = sum_over_devices(keep, give)
    (rotated,) = call(
        "rotate",
        functools.partial(rotate_kernel, total_of=lambda t: t - shared * (devices - 1)),
        [(node_counts, SMEM), (position, SMEM), (mine, VMEM), (other, VMEM), (f, KEPT)],
        [((states.shape, F32), HBM)],
        scratch=[
            pltpu.VMEM(states.shape, F32),
            pltpu.VMEM((LANES, LANES), F32),
            pltpu.VMEM((3, LANES, LANES), F32),
            pltpu.VMEM((2 * width, width), jnp.bfloat16),
            pltpu.SemaphoreType.DMA((1,)),
        ],
        mib=24,
    )
    return rotated


def solution(mesh):
    in_specs = (
        P("mesh", None),
        P("mesh"),
        P("mesh", None, None),
        P("mesh", None),
        P("mesh"),
        P(),
        P("mesh", None, None),
    )
    out_specs = P("mesh", None)
    return jax.shard_map(body, mesh=mesh, in_specs=in_specs, out_specs=out_specs, check_vma=False)
```

time: 230 us -> 191 us (0.83)
  Pallas kernels: 138 us -> 87.6 us
  starting transfers between devices: 47.9 us -> 80.3 us
  waiting for transfers between devices: 35 us -> 19.1 us
  local copies, waits for them, and re-layouts: 4.87 us -> 0.77 us
    ppermute x0 -> x6, starting transfers between devices: none -> 54.2 us  [the longest x3 53.9 us: exchanged(): lax.ppermute(far, 'mesh', [(i, i - 1 + 2 * (i % 2)) for i in range(1, n -...]
    pallas_call x7 -> x15, Pallas kernels: 138 us -> 87.6 us  [call(): pl.pallas_call(kernel, out_shape=[pltpu.VMEM(shape, dtype) if spec is KEP...]
    ppermute x8 -> x1, waiting for transfers between devices: 20.6 us -> 2.4 us  [passed_along(): return lax.ppermute(block, axis, route)]
    ppermute x8 -> x1, starting transfers between devices: 19.5 us -> 4.51 us  [passed_along(): return lax.ppermute(block, axis, route)]
    ppermute x11, starting transfers between devices: 28.4 us -> 21.6 us  [shifted(): return lax.ppermute(value, 'mesh', route)]
    unnamed x23 -> x7, local copies, waits for them, and re-layouts: 4.27 us -> 0.76 us
  transfers between devices with their start and end apart: 19 -> 18, of which waited for: 15 -> 12; matrix products, arithmetic and copies ran while one was open for 0% -> 0% of each run, Pallas kernels for 4% -> 13%
where the time goes in v3:
time: 191 us; the launch traced here: 189 us
  Pallas kernels  87.6 us (46%)
  starting transfers between devices  80.3 us (42%)
  waiting for transfers between devices  19.1 us (10%)
    pallas_call x15, Pallas kernels, call(): pl.pallas_call(kernel, out_shape=[pltpu.VMEM(shape, dtype) if spec is KEP...  87.6 us
    ppermute x3, starting transfers between devices, exchanged(): lax.ppermute(far, 'mesh', [(i, i - 1 + 2 * (i % 2)) for i in range(1, n -...  53.9 us
    ppermute x11, starting transfers between devices, shifted(): return lax.ppermute(value, 'mesh', route)  21.6 us
    ppermute x11, waiting for transfers between devices, shifted(): return lax.ppermute(value, 'mesh', route)  15.1 us
    ppermute x1, starting transfers between devices, passed_along(): return lax.ppermute(block, axis, route)  4.51 us
  transfers between devices with their start and end apart: 18, of which 12 were waited for; matrix products, arithmetic and copies ran while one was open for 0% of the time, Pallas kernels for 13%

profile of v3, /device:TPU:1, one launch (start us, length us, event | category | flops | bytes accessed | tf_op | source)
XLA Modules:
  0.0 189.5 jit_solution(2062093474384211333)
XLA Ops:
  1.4 7.5 %start.1 = (f32[12288,128]{1,0:T(8,128)S(1)}, f32[12288,128]{1,0:T(8,128)S(1)}, f32[776,128]{1,0:T(8,128)S(1)}) custom-call(s32[1]{0:T(128)} %bitcast.position.refs_1_, s32[768]{0:T(1024)S(1)} %mul.18.rows.refs_3_, f32[48,128]{1,0:T(8,128)S(1)} %bitcast.8, f32[6144,256]{1,0:T(8,128)} %states_hbm.1), custom_call_target="tpu_custom_call" | custom-call | tf_op jit(solution)/shard_map/start/pallas_call | solution.py:45
  9.0 4.5 %collective-permute-start = (f32[776,128]{1,0:T(8,128)S(1)}, f32[776,128]{1,0:T(8,128)S(1)}, u32[]{:S(2)}, u32[]{:S(2)}) collective-permute-start(f32[776,128]{1,0:T(8,128)S(1)} %get-tuple-element.53), channel_id=1, source_target_pairs={{0,1},{1,2},{2,3},{3,4},{4,5},{5,6},{6,7},{7,8},{8,9},{9,10},{10,1... | collective-permute-start | bytes 1191944 | tf_op jit(solution)/shard_map/ppermute | solution.py:25
  14.2 1.6 clear.1
  15.8 2.4 %collective-permute-done.refs_4_ = f32[776,128]{1,0:T(8,128)S(1)} collective-permute-done((f32[776,128]{1,0:T(8,128)S(1)}, f32[776,128]{1,0:T(8,128)S(1)}, u32[]{:S(2)}, u32[]{:S(2)}) %collective-permute-start) | collective-permute-done | bytes 397344 | tf_op jit(solution)/shard_map/ppermute | solution.py:25
  18.2 7.3 %ham1.1 = (f32[12288,128]{1,0:T(8,128)S(1)}, f32[12288,128]{1,0:T(8,128)S(1)}, f32[12288,128]{1,0:T(8,128)S(1)}, f32[12288,128]{1,0:T(8,128)S(1)}, f32[12288,128...) custom-call(s32[1]{0:T(128)S(6)} %copy.77.refs_0_, ...), custom_call_target="tpu_custom_call", output_to_operand_aliasing={{0}: (5, {}), {1}: (6, {}), {2}: (7, {}), {3}: (8, {}), {4}... | custom-call | tf_op jit(solution)/shard_map/ham1/pallas_call | solution.py:45
  25.6 18.2 %collective-permute-start.2 = (f32[768,128]{1,0:T(8,128)S(1)}, f32[768,128]{1,0:T(8,128)S(1)}, u32[]{:S(2)}, u32[]{:S(2)}) collective-permute-start(f32[768,128]{1,0:T(8,128)S(1)} %get-tuple-element.61), channel_id=1, source_target_pairs={{1,2},{2,1},{3,4},{4,3},{5,6},{6,5},{7,8},{8,7},{9,10},{10,9},{11,... | collective-permute-start | bytes 1179656 | tf_op jit(solution)/shard_map/ppermute | solution.py:503
  43.8 4.5 %combine1.1 = (f32[12288,128]{1,0:T(8,128)S(1)}, f32[12288,128]{1,0:T(8,128)S(1)}, f32[12288,128]{1,0:T(8,128)S(1)}, f32[12288,128]{1,0:T(8,128)S(1)}, f32[12288,128]{1,0:T(8,128)S(1)}) custom-call(f32[12288,128]{1,0:T(8,128)S(1)} %get-tuple-element.62.refs_0_.refs_2_, ...), custom_call_target="tpu_custom_call", output_to_operand_aliasing={{1}: (2, {}), {2}: (3, {}), {3}: (4, {}), {4}: (5, {})} | custom-call | flops 15728640 | bytes 15728640 | tf_op jit(solution)/shard_map/combine1/pallas_call | solution.py:45
  48.4 0.9 collective-permute-done.2.refs_5_
  49.3 8.5 %ham2.1 = (f32[12288,128]{1,0:T(8,128)S(1)}, f32[12288,128]{1,0:T(8,128)S(1)}, f32[12288,128]{1,0:T(8,128)S(1)}, f32[12288,128]{1,0:T(8,128)S(1)}, f32[12288,128...) custom-call(s32[1]{0:T(128)S(6)} %copy.77.refs_0_, ...), custom_call_target="tpu_custom_call", output_to_operand_aliasing={{0}: (6, {}), {1}: (7, {}), {2}: (8, {}), {3}: (9, {}), {4}... | custom-call | tf_op jit(solution)/shard_map/ham2/pallas_call | solution.py:45
  57.9 17.9 %collective-permute-start.4 = (f32[768,128]{1,0:T(8,128)S(1)}, f32[768,128]{1,0:T(8,128)S(1)}, u32[]{:S(2)}, u32[]{:S(2)}) collective-permute-start(f32[768,128]{1,0:T(8,128)S(1)} %get-tuple-element.74), channel_id=1, source_target_pairs={{1,2},{2,1},{3,4},{4,3},{5,6},{6,5},{7,8},{8,7},{9,10},{10,9},{11,... | collective-permute-start | bytes 1179656 | tf_op jit(solution)/shard_map/ppermute | solution.py:503
  75.8 4.8 %combine2.1 = (f32[12288,128]{1,0:T(8,128)S(1)}, f32[12288,128]{1,0:T(8,128)S(1)}, f32[12288,128]{1,0:T(8,128)S(1)}, f32[12288,128]{1,0:T(8,128)S(1)}, f32[12288,128]{1,0:T(8,128)S(1)}) custom-call(f32[12288,128]{1,0:T(8,128)S(1)} %get-tuple-element.75.refs_0_.refs_2_, ...), custom_call_target="tpu_custom_call", output_to_operand_aliasing={{1}: (3, {}), {2}: (4, {}), {3}: (5, {}), {4}: (6, {}), {0}... | custom-call | flops 15728640 | bytes 15728640 | tf_op jit(solution)/shard_map/combine2/pallas_call | solution.py:45
  81.2 8.5 %ham3.1 = (f32[12288,128]{1,0:T(8,128)S(1)}, f32[12288,128]{1,0:T(8,128)S(1)}, f32[12288,128]{1,0:T(8,128)S(1)}, f32[12288,128]{1,0:T(8,128)S(1)}, f32[12288,128...) custom-call(s32[1]{0:T(128)S(6)} %copy.77.refs_0_, ...), custom_call_target="tpu_custom_call", output_to_operand_aliasing={{0}: (6, {}), {1}: (7, {}), {2}: (8, {}), {3}: (9, {}), {4}... | custom-call | tf_op jit(solution)/shard_map/ham3/pallas_call | solution.py:45
  89.8 17.9 %collective-permute-start.6 = (f32[768,128]{1,0:T(8,128)S(1)}, f32[768,128]{1,0:T(8,128)S(1)}, u32[]{:S(2)}, u32[]{:S(2)}) collective-permute-start(f32[768,128]{1,0:T(8,128)S(1)} %get-tuple-element.87), channel_id=1, source_target_pairs={{1,2},{2,1},{3,4},{4,3},{5,6},{6,5},{7,8},{8,7},{9,10},{10,9},{11,... | collective-permute-start | bytes 1179656 | tf_op jit(solution)/shard_map/ppermute | solution.py:503
  107.7 4.5 %combine3.1 = (f32[12288,128]{1,0:T(8,128)S(1)}, f32[12288,128]{1,0:T(8,128)S(1)}, f32[12288,128]{1,0:T(8,128)S(1)}, f32[12288,128]{1,0:T(8,128)S(1)}, f32[12288,128]{1,0:T(8,128)S(1)}) custom-call(f32[12288,128]{1,0:T(8,128)S(1)} %get-tuple-element.89.refs_0_, ...), custom_call_target="tpu_custom_call", output_to_operand_aliasing={{1}: (3, {}), {2}: (4, {}), {3}: (5, {}), {4}: (6, {}), {0}... | custom-call | flops 15728640 | bytes 15728640 | tf_op jit(solution)/shard_map/combine3/pallas_call | solution.py:45
  112.1 8.3 %inner.1 = (f32[12288,128]{1,0:T(8,128)S(1)}, f32[1536,128]{1,0:T(8,128)S(1)}, f32[256,512]{1,0:T(8,128)S(1)}) custom-call(s32[128]{0:T(128)S(1)} %copy-done.1, s32[1]{0:T(128)} %bitcast.position.refs_1_, s32[768]{0:T(1024)S(1)} %mul.18.rows.refs_3_, f32[12288,128]{1,0:T(8,128)S(1)} %get-tuple-element.94.f_in), custom_call_target="tpu_custom_call", output_to_operand_aliasing={{0}: (3, {})} | custom-call | flops 15728640 | bytes 15728640 | tf_op jit(solution)/shard_map/inner/pallas_call | solution.py:45
  120.5 2.6 %finish.1 = (f32[12288,128]{1,0:T(8,128)S(1)}, f32[136,128]{1,0:T(8,128)S(1)}, f32[136,128]{1,0:T(8,128)S(1)}) custom-call(s32[1]{0:T(128)} %bitcast.position.refs_1_, s32[768]{0:T(1024)S(1)} %mul.18.rows.refs_3_, f32[768,128]{1,0:T(8,128)S(1)} %collective-permute-done.5.near_in, ...), custom_call_target="tpu_custom_call", output_to_operand_aliasing={{0}: (7, {})} | custom-call | tf_op jit(solution)/shard_map/finish/pallas_call | solution.py:45
  123.2 1.2 collective-permute-done.7.refs_1_
  124.5 0.9 collective-permute-start.10
  125.4 1.2 collective-permute-start.9
  128.2 1.9 collective-permute-done.9.refs_2_
  130.1 2.1 %collective-permute-done.8.refs_1_ = f32[136,128]{1,0:T(8,128)S(1)} collective-permute-done((f32[136,128]{1,0:T(8,128)S(1)}, f32[136,128]{1,0:T(8,128)S(1)}, u32[]{:S(2)}, u32[]{:S(2)}) %collective-permute-start.8) | collective-permute-done | bytes 69664 | tf_op jit(solution)/shard_map/ppermute | solution.py:382
  132.2 2.0 %collective-permute-start.13 = (f32[136,128]{1,0:T(8,128)S(1)}, f32[136,128]{1,0:T(8,128)S(1)}, u32[]{:S(2)}, u32[]{:S(2)}) collective-permute-start(f32[136,128]{1,0:T(8,128)S(1)} %add.5.refs_0_), channel_id=1, source_target_pairs={{0,24},{1,25},{2,26},{3,27},{4,28},{5,29},{6,30},{7,31},{8,0},{9,1... | collective-permute-start | bytes 208904 | tf_op jit(solution)/shard_map/ppermute | solution.py:382
  134.2 2.9 %collective-permute-start.12 = (f32[136,128]{1,0:T(8,128)S(1)}, f32[136,128]{1,0:T(8,128)S(1)}, u32[]{:S(2)}, u32[]{:S(2)}) collective-permute-start(f32[136,128]{1,0:T(8,128)S(1)} %add.5.refs_0_), channel_id=1, source_target_pairs={{0,16},{1,17},{2,18},{3,19},{4,20},{5,21},{6,22},{7,23},{8,24},{9,... | collective-permute-start | bytes 208904 | tf_op jit(solution)/shard_map/ppermute | solution.py:382
  137.8 1.0 collective-permute-done.12.refs_2_
  138.8 3.4 %collective-permute-done.11.refs_1_ = f32[136,128]{1,0:T(8,128)S(1)} collective-permute-done((f32[136,128]{1,0:T(8,128)S(1)}, f32[136,128]{1,0:T(8,128)S(1)}, u32[]{:S(2)}, u32[]{:S(2)}) %collective-permute-start.11) | collective-permute-done | bytes 69664 | tf_op jit(solution)/shard_map/ppermute | solution.py:382
  142.2 1.0 collective-permute-start.16
  143.2 8.3 %collective-permute-start.15 = (f32[136,128]{1,0:T(8,128)S(1)}, f32[136,128]{1,0:T(8,128)S(1)}, u32[]{:S(2)}, u32[]{:S(2)}) collective-permute-start(f32[136,128]{1,0:T(8,128)S(1)} %add.6.refs_0_), channel_id=1, source_target_pairs={{0,64},{1,65},{2,66},{3,67},{4,68},{5,69},{6,70},{7,71},{8,72},{9,... | collective-permute-start | bytes 208904 | tf_op jit(solution)/shard_map/ppermute | solution.py:382
  152.3 0.9 collective-permute-done.15.refs_2_
  153.2 2.9 %collective-permute-done.14.refs_1_ = f32[136,128]{1,0:T(8,128)S(1)} collective-permute-done((f32[136,128]{1,0:T(8,128)S(1)}, f32[136,128]{1,0:T(8,128)S(1)}, u32[]{:S(2)}, u32[]{:S(2)}) %collective-permute-start.14) | collective-permute-done | bytes 69664 | tf_op jit(solution)/shard_map/ppermute | solution.py:382
  156.1 2.9 %collective-permute-start.17 = (f32[136,128]{1,0:T(8,128)S(1)}, f32[136,128]{1,0:T(8,128)S(1)}, u32[]{:S(2)}, u32[]{:S(2)}) collective-permute-start(f32[136,128]{1,0:T(8,128)S(1)} %add.7.mine), channel_id=1, source_target_pairs={{0,1},{1,0},{2,3},{3,2},{4,5},{5,4},{6,7},{7,6},{8,9},{9,8},{10,11... | collective-permute-start | bytes 208904 | tf_op jit(solution)/shard_map/ppermute | solution.py:382
  159.0 0.9 collective-permute-done.17.other
  159.9 29.4 %rotate.1 = f32[6144,256]{1,0:T(8,128)} custom-call(s32[128]{0:T(128)S(1)} %copy-done.1, s32[1]{0:T(128)} %bitcast.position.refs_1_, f32[136,128]{1,0:T(8,128)S(1)} %add.7.mine, f32[136,128]{1,0:T(8,128)S(1)} %collective-permute-done.17.other, f32[12288,128]{1,0:T(8,128)S(1)} %get-tuple-element.100.w), custom_call_target="tpu_custom_call" | custom-call | tf_op jit(solution)/shard_map/rotate/pallas_call | solution.py:45
  (29 shorter events, 5.7 us)
Async XLA Ops:
  0.7 0.7 copy-start
  1.4 12.7 %copy-start.2 = (s32[16,512]{1,0:T(8,128)S(1)}, s32[16,512]{1,0:T(8,128)}, u32[]{:S(2)}) copy-start(s32[16,512]{1,0:T(8,128)} %param.10) | copy-start | bytes 98308
  9.0 9.3 %collective-permute-start = (f32[776,128]{1,0:T(8,128)S(1)}, f32[776,128]{1,0:T(8,128)S(1)}, u32[]{:S(2)}, u32[]{:S(2)}) collective-permute-start(f32[776,128]{1,0:T(8,128)S(1)} %get-tuple-element.53), channel_id=1, source_target_pairs={{0,1},{1,2},{2,3},{3,4},{4,5},{5,6},{6,7},{7,8},{8,9},{9,10},{10,1... | collective-permute-start | bytes 1191944 | tf_op jit(solution)/shard_map/ppermute | solution.py:25
  25.6 22.8 %collective-permute-start.1 = (f32[768,128]{1,0:T(8,128)S(1)}, f32[768,128]{1,0:T(8,128)S(1)}, u32[]{:S(2)}, u32[]{:S(2)}) collective-permute-start(f32[768,128]{1,0:T(8,128)S(1)} %get-tuple-element.60), channel_id=1, source_target_pairs={{0,1},{1,0},{2,3},{3,2},{4,5},{5,4},{6,7},{7,6},{8,9},{9,8},{10,11... | collective-permute-start | bytes 1179656 | tf_op jit(solution)/shard_map/ppermute | solution.py:504
  25.6 23.6 %collective-permute-start.2 = (f32[768,128]{1,0:T(8,128)S(1)}, f32[768,128]{1,0:T(8,128)S(1)}, u32[]{:S(2)}, u32[]{:S(2)}) collective-permute-start(f32[768,128]{1,0:T(8,128)S(1)} %get-tuple-element.61), channel_id=1, source_target_pairs={{1,2},{2,1},{3,4},{4,3},{5,6},{6,5},{7,8},{8,7},{9,10},{10,9},{11,... | collective-permute-start | bytes 1179656 | tf_op jit(solution)/shard_map/ppermute | solution.py:503
  57.8 22.7 %collective-permute-start.3 = (f32[768,128]{1,0:T(8,128)S(1)}, f32[768,128]{1,0:T(8,128)S(1)}, u32[]{:S(2)}, u32[]{:S(2)}) collective-permute-start(f32[768,128]{1,0:T(8,128)S(1)} %get-tuple-element.73), channel_id=1, source_target_pairs={{0,1},{1,0},{2,3},{3,2},{4,5},{5,4},{6,7},{7,6},{8,9},{9,8},{10,11... | collective-permute-start | bytes 1179656 | tf_op jit(solution)/shard_map/ppermute | solution.py:504
  57.9 23.3 %collective-permute-start.4 = (f32[768,128]{1,0:T(8,128)S(1)}, f32[768,128]{1,0:T(8,128)S(1)}, u32[]{:S(2)}, u32[]{:S(2)}) collective-permute-start(f32[768,128]{1,0:T(8,128)S(1)} %get-tuple-element.74), channel_id=1, source_target_pairs={{1,2},{2,1},{3,4},{4,3},{5,6},{6,5},{7,8},{8,7},{9,10},{10,9},{11,... | collective-permute-start | bytes 1179656 | tf_op jit(solution)/shard_map/ppermute | solution.py:503
  89.7 30.8 %collective-permute-start.5 = (f32[768,128]{1,0:T(8,128)S(1)}, f32[768,128]{1,0:T(8,128)S(1)}, u32[]{:S(2)}, u32[]{:S(2)}) collective-permute-start(f32[768,128]{1,0:T(8,128)S(1)} %get-tuple-element.86), channel_id=1, source_target_pairs={{0,1},{1,0},{2,3},{3,2},{4,5},{5,4},{6,7},{7,6},{8,9},{9,8},{10,11... | collective-permute-start | bytes 1179656 | tf_op jit(solution)/shard_map/ppermute | solution.py:504
  89.8 30.7 %collective-permute-start.6 = (f32[768,128]{1,0:T(8,128)S(1)}, f32[768,128]{1,0:T(8,128)S(1)}, u32[]{:S(2)}, u32[]{:S(2)}) collective-permute-start(f32[768,128]{1,0:T(8,128)S(1)} %get-tuple-element.87), channel_id=1, source_target_pairs={{1,2},{2,1},{3,4},{4,3},{5,6},{6,5},{7,8},{8,7},{9,10},{10,9},{11,... | collective-permute-start | bytes 1179656 | tf_op jit(solution)/shard_map/ppermute | solution.py:503
  107.7 4.5 %copy-start.1 = (s32[128]{0:T(128)S(1)}, s32[128]{0:T(128)}, u32[]{:S(2)}) copy-start(s32[128]{0:T(128)} %counts.3) | copy-start | bytes 1540
  123.1 1.3 collective-permute-start.7
  124.5 3.7 %collective-permute-start.10 = (f32[136,128]{1,0:T(8,128)S(1)}, f32[136,128]{1,0:T(8,128)S(1)}, u32[]{:S(2)}, u32[]{:S(2)}) collective-permute-start(f32[136,128]{1,0:T(8,128)S(1)} %add.4.refs_0_), channel_id=1, source_target_pairs={{0,6},{1,7},{2,0},{3,1},{4,2},{5,3},{6,4},{7,5},{8,14},{9,15},{10,... | collective-permute-start | bytes 208904 | tf_op jit(solution)/shard_map/ppermute | solution.py:382
  125.4 4.7 %collective-permute-start.9 = (f32[136,128]{1,0:T(8,128)S(1)}, f32[136,128]{1,0:T(8,128)S(1)}, u32[]{:S(2)}, u32[]{:S(2)}) collective-permute-start(f32[136,128]{1,0:T(8,128)S(1)} %add.4.refs_0_), channel_id=1, source_target_pairs={{0,4},{1,5},{2,6},{3,7},{4,0},{5,1},{6,2},{7,3},{8,12},{9,13},{10,... | collective-permute-start | bytes 208904 | tf_op jit(solution)/shard_map/ppermute | solution.py:382
  126.5 5.6 %collective-permute-start.8 = (f32[136,128]{1,0:T(8,128)S(1)}, f32[136,128]{1,0:T(8,128)S(1)}, u32[]{:S(2)}, u32[]{:S(2)}) collective-permute-start(f32[136,128]{1,0:T(8,128)S(1)} %add.4.refs_0_), channel_id=1, source_target_pairs={{0,2},{1,3},{2,4},{3,5},{4,6},{5,7},{6,0},{7,1},{8,10},{9,11},{10,... | collective-permute-start | bytes 208904 | tf_op jit(solution)/shard_map/ppermute | solution.py:382
  132.2 5.7 %collective-permute-start.13 = (f32[136,128]{1,0:T(8,128)S(1)}, f32[136,128]{1,0:T(8,128)S(1)}, u32[]{:S(2)}, u32[]{:S(2)}) collective-permute-start(f32[136,128]{1,0:T(8,128)S(1)} %add.5.refs_0_), channel_id=1, source_target_pairs={{0,24},{1,25},{2,26},{3,27},{4,28},{5,29},{6,30},{7,31},{8,0},{9,1... | collective-permute-start | bytes 208904 | tf_op jit(solution)/shard_map/ppermute | solution.py:382
  134.2 4.7 %collective-permute-start.12 = (f32[136,128]{1,0:T(8,128)S(1)}, f32[136,128]{1,0:T(8,128)S(1)}, u32[]{:S(2)}, u32[]{:S(2)}) collective-permute-start(f32[136,128]{1,0:T(8,128)S(1)} %add.5.refs_0_), channel_id=1, source_target_pairs={{0,16},{1,17},{2,18},{3,19},{4,20},{5,21},{6,22},{7,23},{8,24},{9,... | collective-permute-start | bytes 208904 | tf_op jit(solution)/shard_map/ppermute | solution.py:382
  137.1 5.1 %collective-permute-start.11 = (f32[136,128]{1,0:T(8,128)S(1)}, f32[136,128]{1,0:T(8,128)S(1)}, u32[]{:S(2)}, u32[]{:S(2)}) collective-permute-start(f32[136,128]{1,0:T(8,128)S(1)} %add.5.refs_0_), channel_id=1, source_target_pairs={{0,8},{1,9},{2,10},{3,11},{4,12},{5,13},{6,14},{7,15},{8,16},{9,17... | collective-permute-start | bytes 208904 | tf_op jit(solution)/shard_map/ppermute | solution.py:382
  142.2 10.0 %collective-permute-start.16 = (f32[136,128]{1,0:T(8,128)S(1)}, f32[136,128]{1,0:T(8,128)S(1)}, u32[]{:S(2)}, u32[]{:S(2)}) collective-permute-start(f32[136,128]{1,0:T(8,128)S(1)} %add.6.refs_0_), channel_id=1, source_target_pairs={{0,96},{1,97},{2,98},{3,99},{4,100},{5,101},{6,102},{7,103},{8,104... | collective-permute-start | bytes 208904 | tf_op jit(solution)/shard_map/ppermute | solution.py:382
  143.2 10.0 %collective-permute-start.15 = (f32[136,128]{1,0:T(8,128)S(1)}, f32[136,128]{1,0:T(8,128)S(1)}, u32[]{:S(2)}, u32[]{:S(2)}) collective-permute-start(f32[136,128]{1,0:T(8,128)S(1)} %add.6.refs_0_), channel_id=1, source_target_pairs={{0,64},{1,65},{2,66},{3,67},{4,68},{5,69},{6,70},{7,71},{8,72},{9,... | collective-permute-start | bytes 208904 | tf_op jit(solution)/shard_map/ppermute | solution.py:382
  151.5 4.6 %collective-permute-start.14 = (f32[136,128]{1,0:T(8,128)S(1)}, f32[136,128]{1,0:T(8,128)S(1)}, u32[]{:S(2)}, u32[]{:S(2)}) collective-permute-start(f32[136,128]{1,0:T(8,128)S(1)} %add.6.refs_0_), channel_id=1, source_target_pairs={{0,32},{1,33},{2,34},{3,35},{4,36},{5,37},{6,38},{7,39},{8,40},{9,... | collective-permute-start | bytes 208904 | tf_op jit(solution)/shard_map/ppermute | solution.py:382
  156.1 3.8 %collective-permute-start.17 = (f32[136,128]{1,0:T(8,128)S(1)}, f32[136,128]{1,0:T(8,128)S(1)}, u32[]{:S(2)}, u32[]{:S(2)}) collective-permute-start(f32[136,128]{1,0:T(8,128)S(1)} %add.7.mine), channel_id=1, source_target_pairs={{0,1},{1,0},{2,3},{3,2},{4,5},{5,4},{6,7},{7,6},{8,9},{9,8},{10,11... | collective-permute-start | bytes 208904 | tf_op jit(solution)/shard_map/ppermute | solution.py:382

commit v4 on v3

--- a/solution.py
+++ b/solution.py
@@ -11,7 +11,7 @@
 HALF_WIDTH = 1.5
 LANES = 128
 ACCS = 4
-UNROLL = 64
+UNROLL = 256
 F32 = jnp.float32
 SMEM = pl.BlockSpec(memory_space=pltpu.SMEM)
 VMEM = pl.BlockSpec(memory_space=pltpu.VMEM)
@@ -58,65 +58,74 @@
     )(*operands)
 
 
-def start_kernel(position, rows, mass_all, states_hbm, w, m, send, stage, picked, sems):
+def start_kernel(position, rows, mass, states_hbm, stage, send, lines, sems):
+    shared = lines.shape[0]
+    total = mass.shape[0]
+    loads = [
+        pltpu.make_async_copy(
+            states_hbm.at[:, h * LANES : (h + 1) * LANES],
+            stage.at[h * total : (h + 1) * total, :],
+            sems.at[h],
+        )
+        for h in range(2)
+    ]
+    for load in loads:
+        load.start()
+    unroll = 32
+
+    def spread(g, carry):
+        some = rows.at[pl.ds(shared + g * unroll, unroll)]
+        for k in range(unroll):
+            lines[pl.ds(g * unroll + k, 1), :] = jnp.full((1, LANES), mass[some[k] // 2], F32)
+        return carry
+
+    lax.fori_loop(0, shared // unroll, spread, 0)
+    diagonal = lax.broadcasted_iota(jnp.int32, (LANES, LANES), 0) == lax.broadcasted_iota(
+        jnp.int32, (LANES, LANES), 1
+    )
+    send[2 * shared : 2 * shared + 8, :] = jnp.zeros((8, LANES), F32)
+    for i in range(shared // LANES):
+        block = lines[i * LANES : (i + 1) * LANES, :]
+        line = jnp.sum(jnp.where(diagonal, block, 0.0), axis=0, keepdims=True)
+        send[2 * shared + i : 2 * shared + i + 1, :] = line
+    for load in loads:
+        load.wait()
+
+    def pick(g, carry):
+        some = rows.at[pl.ds(shared + g * unroll, unroll)]
+        first = pl.multiple_of(g * unroll, unroll)
+        for k in range(unroll):
+            row = some[k] // 2
+            line = lines[pl.ds(first + k, 1), :]
+            for h in range(2):
+                value = stage[pl.ds(h * total + row, 1), :]
+                send[pl.ds(2 * first + 2 * k + h, 1), :] = line * value
+        return carry
+
+    lax.fori_loop(0, shared // unroll, pick, 0)
+
+
+def convert_kernel(mass_all, stage, w, m, *accs):
     count = mass_all.shape[0]
     total = count * LANES
-    group = 8
-    parts = count // group
-
-    def load(part, h):
-        at = span(part * group * LANES, group * LANES)
-        return pltpu.make_async_copy(
-            states_hbm.at[at, h * LANES : (h + 1) * LANES], stage.at[h, at, :], sems.at[part, h]
-        )
-
-    for part in range(parts):
+
+    def convert(i, carry):
+        mass = jnp.broadcast_to(mass_all[pl.ds(i, 1), :], (LANES, LANES)).T
+        base = 2 * LANES * i
         for h in range(2):
-            load(part, h).start()
-    for part in range(parts):
-        for h in range(2):
-            load(part, h).wait()
-
-        def convert(i, carry):
-            at = part * group + i
-            mass = jnp.broadcast_to(mass_all[pl.ds(at, 1), :], (LANES, LANES)).T
-            base = 2 * LANES * at
-            for h in range(2):
-                m[pl.ds(base + h, LANES, stride=2), :] = mass
-                w[pl.ds(base + h, LANES, stride=2), :] = mass * stage[h, span(LANES * at, LANES), :]
-            return carry
-
-        lax.fori_loop(0, group, convert, 0)
-    shared = picked.shape[0]
-    take_rows(send.at[0 : 2 * shared, :], rows, shared, w)
-    unroll = 32
-
-    def pick(g, carry):
-        some = rows.at[pl.ds(shared + g * unroll, unroll)]
-        for k in range(unroll):
-            picked[pl.ds(g * unroll + k, 1), :] = m[pl.ds(some[k], 1), :]
-        return carry
-
-    lax.fori_loop(0, shared // unroll, pick, 0)
-    diagonal = lax.broadcasted_iota(jnp.int32, (LANES, LANES), 0) == lax.broadcasted_iota(
-        jnp.int32, (LANES, LANES), 1
-    )
-    send[2 * shared : 2 * shared + 8, :] = jnp.zeros((8, LANES), F32)
-    for i in range(shared // LANES):
-        block = picked[i * LANES : (i + 1) * LANES, :]
-        line = jnp.sum(jnp.where(diagonal, block, 0.0), axis=0, keepdims=True)
-        send[2 * shared + i : 2 * shared + i + 1, :] = line
-
-
-def clear_kernel(after, *accs):
-    chunk = 512
-
-    def clear(c, carry):
-        for acc in accs:
-            acc[span(c * chunk, chunk), :] = jnp.zeros((chunk, LANES), F32)
-        return carry
-
-    lax.fori_loop(0, accs[0].shape[0] // chunk, clear, 0)
+            m[pl.ds(base + h, LANES, stride=2), :] = mass
+            w[pl.ds(base + h, LANES, stride=2), :] = mass * stage[span(h * total + LANES * i, LANES), :]
+        for acc in accs[:-1]:
+            acc[span(base, 2 * LANES), :] = jnp.zeros((2 * LANES, LANES), F32)
+        return carry
+
+    lax.fori_loop(0, count, convert, 0)
+
+    def clear(i, carry):
+        accs[-1][span(2 * LANES * i, 2 * LANES), :] = jnp.zeros((2 * LANES, LANES), F32)
+        return carry
+
+    lax.fori_loop(0, count, clear, 0)
 
 
 def take_rows(out, rows, base, *sources):
@@ -167,7 +176,8 @@
     blocks_hbm = refs[n_field]
     refs = refs[n_field + 1 :]
     w, m, *accs = refs[:n_field]
-    send_near, send_far, picked, parts, lines, blocks, sems = refs[n_field:]
+    send_near, send_far, picked, x, *parts_pair, lines, block_a, block_b, sems = refs[n_field:]
+    block_pair = (block_a, block_b)
 
     shared = send_near.shape[0] // 2
     size = picked.shape[0] // 2
@@ -175,10 +185,14 @@
     near = near_base(position[0], shared)
     far = shared - near
 
-    def load(e):
-        return pltpu.make_async_copy(blocks_hbm.at[e], blocks.at[e % 2], sems.at[e % 2])
-
-    load(0).start()
+    def load(e, parity):
+        return pltpu.make_async_copy(blocks_hbm.at[e], block_pair[parity], sems.at[parity])
+
+    load(0, 0).start()
+
+    @pl.when(live > 1)
+    def _():
+        load(1, 1).start()
 
     if stage == 1:
         (owner,) = received
@@ -205,47 +219,68 @@
         add_rows(w, rows, near, received[0], m, scale)
         add_rows(w, rows, far, received[1], m, scale)
 
-    def product(e):
-        load(e).wait()
+    def convert():
+        for h in range(2):
+            x[:, h * LANES : (h + 1) * LANES] = picked[pl.ds(h, size, stride=2), :].astype(x.dtype)
+
+    def product(parity, g):
+        part = jnp.dot(
+            block_pair[parity][span(g * UNROLL, UNROLL), :], x[...], preferred_element_type=F32
+        )
+        for h in range(2):
+            at = pl.ds(2 * UNROLL * g + h, UNROLL, stride=2)
+            parts_pair[parity][at, :] = part[:, h * LANES : (h + 1) * LANES]
+
+    take_rows(picked, nodes, 0, w)
+    convert()
+    load(0, 0).wait()
+
+    def first_product(g, carry):
+        product(0, g)
+        return carry
+
+    lax.fori_loop(0, size // UNROLL, first_product, 0)
+    take_rows(picked, nodes, jnp.minimum(1, live - 1) * size, w)
+    convert()
+
+    def element(e, parity):
+        other = 1 - parity
+        last = live - 1
+
+        @pl.when(e + 2 < live)
+        def _():
+            load(e + 2, parity).start()
 
         @pl.when(e + 1 < live)
         def _():
-            load(e + 1).start()
-
-        x = jnp.concatenate(
-            [picked[pl.ds(h, size, stride=2), :].astype(jnp.bfloat16) for h in range(2)], axis=1
-        )
-        part = jnp.dot(blocks[e % 2], x, preferred_element_type=F32)
-        for h in range(2):
-            parts[pl.ds(h, size, stride=2), :] = part[:, h * LANES : (h + 1) * LANES]
-
-    take_rows(picked, nodes, 0, w)
-    product(0)
-
-    def element(e, carry):
-        later = jnp.minimum(e + 1, live - 1)
+            load(e + 1, other).wait()
 
         def move(g, inner):
+            product(other, g)
             here = nodes.at[pl.ds(e * size + g * UNROLL, UNROLL)]
-            ahead = nodes.at[pl.ds(later * size + g * UNROLL, UNROLL)]
+            ahead = nodes.at[pl.ds(jnp.minimum(e + 2, last) * size + g * UNROLL, UNROLL)]
             first = pl.multiple_of(2 * g * UNROLL, 2 * UNROLL)
             for k in range(UNROLL):
                 line = pl.ds(first + 2 * k, 2)
                 picked[line, :] = w[pair(ahead[k]), :]
                 at = pair(here[k])
                 acc = accs[k % ACCS]
-                acc[at, :] = acc[at, :] + parts[line, :]
+                acc[at, :] = acc[at, :] + parts_pair[parity][line, :]
             return inner
 
         lax.fori_loop(0, size // UNROLL, move, 0)
-
-        @pl.when(e + 1 < live)
+        convert()
+
+    def two(t, carry):
+        element(2 * t, 0)
+
+        @pl.when(2 * t + 1 < live)
         def _():
-            product(later)
-
-        return carry
-
-    lax.fori_loop(0, live, element, 0)
+            element(2 * t + 1, 1)
+
+        return carry
+
+    lax.fori_loop(0, pl.cdiv(live, 2), two, 0)
     take_rows(send_near, rows, near, *accs)
     take_rows(send_far, rows, far, *accs)
 
@@ -259,7 +294,7 @@
     factor = 1.0 if stage == 1 else 2.0
     scale_h = factor / HALF_WIDTH
     scale_w = -factor * CENTER / HALF_WIDTH
-    chunk = 256
+    chunk = 64
 
     def step(c, carry):
         at = span(c * chunk, chunk)
@@ -314,7 +349,7 @@
     lax.fori_loop(0, 2 * shared // unroll, blank, 0)
     gram[...] = jnp.zeros_like(gram)
     limit = counts[position[0]]
-    n = 256
+    n = 512
 
     def add_chunk(c, carry):
         live = c * n + lax.broadcasted_iota(jnp.int32, (n, 2 * LANES), 0) < limit
@@ -407,25 +442,48 @@
 
 def eliminate(block):
     n = block.shape[0]
-    lane = lax.broadcasted_iota(jnp.int32, (8, n), 1)
-    sub = lax.broadcasted_iota(jnp.int32, (8, n), 0)
-    parts = [block[8 * i : 8 * i + 8, :] for i in range(n // 8)]
-    for k in range(n):
-        q, s = divmod(k, 8)
-        row = parts[q][s : s + 1, :]
-        rec = 1.0 / jnp.broadcast_to(row[:, k : k + 1], (1, n))
-        row = jnp.broadcast_to(jnp.where(lane[:1] == k, 1.0, row) * rec, (8, n))
-        for i in range(q, n // 8):
-            col = jnp.broadcast_to(parts[i][:, k : k + 1], (8, n))
-            new = jnp.where(lane == k, 0.0, parts[i]) - col * row
-            parts[i] = jnp.where(sub > s, new, parts[i]) if i == q else new
-    done = []
-    for i in range(n // 8):
-        here = sub + 8 * i
-        pivot = jnp.sum(jnp.where(lane == here, parts[i], 0.0), axis=1, keepdims=True)
-        unit = jnp.where(lane < here, parts[i], jnp.where(lane == here, 1.0, 0.0))
-        done.append(unit * lax.rsqrt(pivot))
-    return jnp.concatenate(done, axis=0)
+    b = 8
+    lane = lax.broadcasted_iota(jnp.int32, (b, n), 1)
+    sub = lax.broadcasted_iota(jnp.int32, (b, n), 0)
+
+    def line(value, s):
+        return jnp.broadcast_to(value[s : s + 1, :], (b, n))
+
+    def columns(value, first):
+        return [jnp.broadcast_to(value[:, first + c : first + c + 1], (b, n)) for c in range(b)]
+
+    parts = [block[b * i : b * i + b, :] for i in range(n // b)]
+    for q in range(n // b):
+        first = b * q
+        inside = (lane >= first) & (lane < first + b)
+        cols = columns(parts[q], first)
+        corner = [[line(cols[c], s) for c in range(s + 1)] for s in range(b)]
+        own = jnp.where(inside, jnp.where(lane - first == sub, 1.0, 0.0), parts[q])
+        rows = [line(own, s) for s in range(b)]
+        recs, low = [], [[None] * b for _ in range(b)]
+        for c in range(b):
+            recs.append(1.0 / corner[c][c])
+            for s in range(c + 1, b):
+                low[s][c] = corner[s][c] * recs[c]
+            for s in range(c + 1, b):
+                for t in range(c + 1, s + 1):
+                    corner[s][t] = corner[s][t] - low[s][c] * corner[t][c]
+                rows[s] = rows[s] - low[s][c] * rows[c]
+        done = jnp.zeros((b, n), F32)
+        for s in range(b):
+            done = jnp.where(sub == s, rows[s] * lax.rsqrt(corner[s][s]), done)
+        solved = [rows[s] * recs[s] for s in range(b)]
+        for s in reversed(range(b)):
+            for c in range(s):
+                solved[c] = solved[c] - low[s][c] * solved[s]
+        for i in range(q + 1, n // b):
+            cols = columns(parts[i], first)
+            terms = [cols[c] * solved[c] for c in range(b)]
+            while len(terms) > 1:
+                terms = [terms[k] + terms[k + 1] for k in range(0, len(terms), 2)]
+            parts[i] = jnp.where(inside, 0.0, parts[i]) - terms[0]
+        parts[q] = jnp.where(lane < first + b, done, 0.0)
+    return jnp.concatenate(parts, axis=0)
 
 
 def dot32(a, b, ca, cb):
@@ -519,25 +577,22 @@
     send = ((2 * shared, LANES), F32)
     mass_rows = inv_sqrt_mass.reshape(-1, LANES)
 
-    w0, m, values = call(
+    stage, values = call(
         "start",
         start_kernel,
-        [(position, SMEM), (rows, SMEM), (mass_rows, VMEM), (states, HBM)],
-        [(tall, KEPT), (tall, KEPT), (((2 * shared + 8, LANES), F32), VMEM)],
-        scratch=[
-            pltpu.VMEM((2, row_total, LANES), F32),
-            pltpu.VMEM((shared, LANES), F32),
-            pltpu.SemaphoreType.DMA((mass_rows.shape[0] // 8, 2)),
-        ],
-        mib=12,
+        [(position, SMEM), (rows, SMEM), (inv_sqrt_mass, SMEM), (states, HBM)],
+        [(tall, KEPT), (((2 * shared + 8, LANES), F32), VMEM)],
+        scratch=[pltpu.VMEM((shared, LANES), F32), pltpu.SemaphoreType.DMA((2,))],
+        mib=2,
     )
     owner = passed_along(values, "mesh", 1)
-    accs = call(
-        "clear",
-        clear_kernel,
-        [(w0, KEPT)],
-        [(tall, KEPT)] * ACCS,
-        mib=1,
+    w0, m, *accs = call(
+        "convert",
+        convert_kernel,
+        [(mass_rows, VMEM), (stage, KEPT)],
+        [(tall, KEPT)] * (2 + ACCS),
+        aliases={1: 1 + ACCS},
+        mib=2,
         flops=10 * row_total * width,
     )
 
@@ -554,9 +609,12 @@
             aliases={first + i: i for i in range(2 + ACCS)},
             scratch=[
                 pltpu.VMEM((2 * size, LANES), F32),
+                pltpu.VMEM((size, width), jnp.bfloat16),
+                pltpu.VMEM((2 * size, LANES), F32),
                 pltpu.VMEM((2 * size, LANES), F32),
                 pltpu.VMEM((shared, LANES), F32),
-                pltpu.VMEM((2, *element_blocks.shape[1:]), element_blocks.dtype),
+                pltpu.VMEM(element_blocks.shape[1:], element_blocks.dtype),
+                pltpu.VMEM(element_blocks.shape[1:], element_blocks.dtype),
                 pltpu.SemaphoreType.DMA((2,)),
             ],
             mib=4,
@@ -567,14 +625,14 @@
         ins = [(w, KEPT), (m, KEPT)] + ([(old, KEPT)] if stage > 1 else [])
         first = len(ins)
         ins += [(acc, KEPT) for acc in accs]
-        aliases = {first + i: 1 + i for i in range(ACCS)}
+        aliases = {first + i: 1 + i for i in range(ACCS * (stage < 3))}
         if stage > 1:
             aliases[2] = 0
         new, *accs = call(
             "combine%d" % stage,
             functools.partial(combine_kernel, stage),
             ins,
-            [(tall, KEPT)] * (1 + ACCS),
+            [(tall, KEPT)] * (1 + ACCS * (stage < 3)),
             aliases=aliases,
             mib=1,
             flops=10 * row_total * width,

time: 191 us -> 175 us (0.916); the launches traced: 189 us -> 176 us
  Pallas kernels: 87.6 us -> 75.9 us
  starting transfers between devices: 80.3 us -> 76.4 us
    ppermute x3, starting transfers between devices: 53.9 us -> 19.9 us  [exchanged(): lax.ppermute(far, 'mesh', [(i, i - 1 + 2 * (i % 2)) for i in range(1, n -...]
    ppermute x11, starting transfers between devices: 21.6 us -> 49.8 us  [shifted(): return lax.ppermute(value, 'mesh', route)]
    pallas_call x15, Pallas kernels: 87.6 us -> 75.9 us  [call(): pl.pallas_call(kernel, out_shape=[pltpu.VMEM(shape, dtype) if spec is KEP...]
    ppermute x3, waiting for transfers between devices: 1.58 us -> 4 us  [exchanged(): lax.ppermute(far, 'mesh', [(i, i - 1 + 2 * (i % 2)) for i in range(1, n -...]
    ppermute x1, waiting for transfers between devices: 2.4 us -> 0.01 us  [passed_along(): return lax.ppermute(block, axis, route)]
    ppermute x3, starting transfers between devices: 0.26 us -> 2.19 us  [exchanged(): near = lax.ppermute(near, 'mesh', [(i, i ^ 1) for i in range(n)])]
  transfers between devices with their start and end apart: 18 -> 18, of which waited for: 12 -> 11; matrix products, arithmetic and copies ran while one was open for 0% -> 0% of each run, Pallas kernels for 13% -> 12%
where the time goes in v4:
time: 175 us; the launch traced here: 176 us
  starting transfers between devices  76.4 us (44%)
  Pallas kernels  75.9 us (43%)
  waiting for transfers between devices  21 us (12%)
    pallas_call x15, Pallas kernels, call(): pl.pallas_call(kernel, out_shape=[pltpu.VMEM(shape, dtype) if spec is KEP...  75.9 us
    ppermute x11, starting transfers between devices, shifted(): return lax.ppermute(value, 'mesh', route)  49.8 us
    ppermute x3, starting transfers between devices, exchanged(): lax.ppermute(far, 'mesh', [(i, i - 1 + 2 * (i % 2)) for i in range(1, n -...  19.9 us
    ppermute x11, waiting for transfers between devices, shifted(): return lax.ppermute(value, 'mesh', route)  17 us
    ppermute x1, starting transfers between devices, passed_along(): return lax.ppermute(block, axis, route)  4.51 us
    ppermute x3, waiting for transfers between devices, exchanged(): lax.ppermute(far, 'mesh', [(i, i - 1 + 2 * (i % 2)) for i in range(1, n -...  4 us
  transfers between devices with their start and end apart: 18, of which 11 were waited for; matrix products, arithmetic and copies ran while one was open for 0% of the time, Pallas kernels for 12%

profile of v4, /device:TPU:1, one launch (start us, length us, event | category | flops | bytes accessed | tf_op | source)
XLA Modules:
  0.0 175.8 jit_solution(10187568319721435768)
XLA Ops:
  1.4 5.9 %start.1 = (f32[12288,128]{1,0:T(8,128)S(1)}, f32[776,128]{1,0:T(8,128)S(1)}) custom-call(s32[1]{0:T(128)} %bitcast.position.refs_1_, s32[768]{0:T(1024)S(1)} %mul.18.rows.refs_3_, f32[6144]{0:T(1024)S(1)} %copy-done.2, f32[6144,256]{1,0:T(8,128)} %states_hbm.1), custom_call_target="tpu_custom_call" | custom-call | tf_op jit(solution)/shard_map/start/pallas_call | solution.py:45
  7.3 4.5 %collective-permute-start = (f32[776,128]{1,0:T(8,128)S(1)}, f32[776,128]{1,0:T(8,128)S(1)}, u32[]{:S(2)}, u32[]{:S(2)}) collective-permute-start(f32[776,128]{1,0:T(8,128)S(1)} %get-tuple-element.53), channel_id=1, source_target_pairs={{0,1},{1,2},{2,3},{3,4},{4,5},{5,6},{6,7},{7,8},{8,9},{9,10},{10,1... | collective-permute-start | bytes 1191944 | tf_op jit(solution)/shard_map/ppermute | solution.py:25
  12.5 5.3 %convert.1 = (f32[12288,128]{1,0:T(8,128)S(1)}, f32[12288,128]{1,0:T(8,128)S(1)}, f32[12288,128]{1,0:T(8,128)S(1)}, f32[12288,128]{1,0:T(8,128)S(1)}, f32[12288,...) custom-call(f32[48,128]{1,0:T(8,128)S(1)} %bitcast.8, ...), custom_call_target="tpu_custom_call", output_to_operand_aliasing={{5}: (1, {})} | custom-call | flops 15728640 | bytes 15728640 | tf_op jit(solution)/shard_map/convert/pallas_call | solution.py:45
  17.9 8.9 %ham1.1 = (f32[12288,128]{1,0:T(8,128)S(1)}, f32[12288,128]{1,0:T(8,128)S(1)}, f32[12288,128]{1,0:T(8,128)S(1)}, f32[12288,128]{1,0:T(8,128)S(1)}, f32[12288,128...) custom-call(s32[1]{0:T(128)S(6)} %copy.71.refs_0_, ...), custom_call_target="tpu_custom_call", output_to_operand_aliasing={{0}: (5, {}), {1}: (6, {}), {2}: (7, {}), {3}: (8, {}), {4}... | custom-call | tf_op jit(solution)/shard_map/ham1/pallas_call | solution.py:45
  26.8 2.0 %collective-permute-start.1 = (f32[768,128]{1,0:T(8,128)S(1)}, f32[768,128]{1,0:T(8,128)S(1)}, u32[]{:S(2)}, u32[]{:S(2)}) collective-permute-start(f32[768,128]{1,0:T(8,128)S(1)} %get-tuple-element.61), channel_id=1, source_target_pairs={{0,1},{1,0},{2,3},{3,2},{4,5},{5,4},{6,7},{7,6},{8,9},{9,8},{10,11... | collective-permute-start | bytes 1179656 | tf_op jit(solution)/shard_map/ppermute | solution.py:562
  28.8 3.1 %collective-permute-start.2 = (f32[768,128]{1,0:T(8,128)S(1)}, f32[768,128]{1,0:T(8,128)S(1)}, u32[]{:S(2)}, u32[]{:S(2)}) collective-permute-start(f32[768,128]{1,0:T(8,128)S(1)} %get-tuple-element.62), channel_id=1, source_target_pairs={{1,2},{2,1},{3,4},{4,3},{5,6},{6,5},{7,8},{8,7},{9,10},{10,9},{11,... | collective-permute-start | bytes 1179656 | tf_op jit(solution)/shard_map/ppermute | solution.py:561
  31.9 3.7 %combine1.1 = (f32[12288,128]{1,0:T(8,128)S(1)}, f32[12288,128]{1,0:T(8,128)S(1)}, f32[12288,128]{1,0:T(8,128)S(1)}, f32[12288,128]{1,0:T(8,128)S(1)}, f32[12288,128]{1,0:T(8,128)S(1)}) custom-call(f32[12288,128]{1,0:T(8,128)S(1)} %get-tuple-element.63.refs_0_.refs_2_, ...), custom_call_target="tpu_custom_call", output_to_operand_aliasing={{1}: (2, {}), {2}: (3, {}), {3}: (4, {}), {4}: (5, {})} | custom-call | flops 15728640 | bytes 15728640 | tf_op jit(solution)/shard_map/combine1/pallas_call | solution.py:45
  35.7 2.2 %collective-permute-done.2.refs_5_ = f32[768,128]{1,0:T(8,128)S(1)} collective-permute-done((f32[768,128]{1,0:T(8,128)S(1)}, f32[768,128]{1,0:T(8,128)S(1)}, u32[]{:S(2)}, u32[]{:S(2)}) %collective-permute-start.2) | collective-permute-done | bytes 393248 | tf_op jit(solution)/shard_map/ppermute | solution.py:561
  37.9 9.9 %ham2.1 = (f32[12288,128]{1,0:T(8,128)S(1)}, f32[12288,128]{1,0:T(8,128)S(1)}, f32[12288,128]{1,0:T(8,128)S(1)}, f32[12288,128]{1,0:T(8,128)S(1)}, f32[12288,128...) custom-call(s32[1]{0:T(128)S(6)} %copy.71.refs_0_, ...), custom_call_target="tpu_custom_call", output_to_operand_aliasing={{0}: (6, {}), {1}: (7, {}), {2}: (8, {}), {3}: (9, {}), {4}... | custom-call | tf_op jit(solution)/shard_map/ham2/pallas_call | solution.py:45
  48.0 5.0 %collective-permute-start.4 = (f32[768,128]{1,0:T(8,128)S(1)}, f32[768,128]{1,0:T(8,128)S(1)}, u32[]{:S(2)}, u32[]{:S(2)}) collective-permute-start(f32[768,128]{1,0:T(8,128)S(1)} %get-tuple-element.75), channel_id=1, source_target_pairs={{1,2},{2,1},{3,4},{4,3},{5,6},{6,5},{7,8},{8,7},{9,10},{10,9},{11,... | collective-permute-start | bytes 1179656 | tf_op jit(solution)/shard_map/ppermute | solution.py:561
  53.0 3.6 %combine2.1 = (f32[12288,128]{1,0:T(8,128)S(1)}, f32[12288,128]{1,0:T(8,128)S(1)}, f32[12288,128]{1,0:T(8,128)S(1)}, f32[12288,128]{1,0:T(8,128)S(1)}, f32[12288,128]{1,0:T(8,128)S(1)}) custom-call(f32[12288,128]{1,0:T(8,128)S(1)} %get-tuple-element.76.refs_0_.refs_2_, ...), custom_call_target="tpu_custom_call", output_to_operand_aliasing={{1}: (3, {}), {2}: (4, {}), {3}: (5, {}), {4}: (6, {}), {0}... | custom-call | flops 15728640 | bytes 15728640 | tf_op jit(solution)/shard_map/combine2/pallas_call | solution.py:45
  56.7 1.8 %collective-permute-done.4.refs_5_ = f32[768,128]{1,0:T(8,128)S(1)} collective-permute-done((f32[768,128]{1,0:T(8,128)S(1)}, f32[768,128]{1,0:T(8,128)S(1)}, u32[]{:S(2)}, u32[]{:S(2)}) %collective-permute-start.4) | collective-permute-done | bytes 393248 | tf_op jit(solution)/shard_map/ppermute | solution.py:561
  58.5 9.9 %ham3.1 = (f32[12288,128]{1,0:T(8,128)S(1)}, f32[12288,128]{1,0:T(8,128)S(1)}, f32[12288,128]{1,0:T(8,128)S(1)}, f32[12288,128]{1,0:T(8,128)S(1)}, f32[12288,128...) custom-call(s32[1]{0:T(128)S(6)} %copy.71.refs_0_, ...), custom_call_target="tpu_custom_call", output_to_operand_aliasing={{0}: (6, {}), {1}: (7, {}), {2}: (8, {}), {3}: (9, {}), {4}... | custom-call | tf_op jit(solution)/shard_map/ham3/pallas_call | solution.py:45
  68.5 11.8 %collective-permute-start.6 = (f32[768,128]{1,0:T(8,128)S(1)}, f32[768,128]{1,0:T(8,128)S(1)}, u32[]{:S(2)}, u32[]{:S(2)}) collective-permute-start(f32[768,128]{1,0:T(8,128)S(1)} %get-tuple-element.88), channel_id=1, source_target_pairs={{1,2},{2,1},{3,4},{4,3},{5,6},{6,5},{7,8},{8,7},{9,10},{10,9},{11,... | collective-permute-start | bytes 1179656 | tf_op jit(solution)/shard_map/ppermute | solution.py:561
  80.3 3.5 %combine3.1.f_in = f32[12288,128]{1,0:T(8,128)S(1)} custom-call(f32[12288,128]{1,0:T(8,128)S(1)} %get-tuple-element.90.refs_0_, f32[12288,128]{1,0:T(8,128)S(1)} %get-tuple-element.89.refs_1_.m, f32[12288,128]{1,0:T(8,128)S(1)} %get-tuple-element.76.refs_0_.refs_2_, f32[12288,128]{1,0:T(8,128)S(1)} %get-tuple-element.91.refs_3_, ...), custom_call_target="tpu_custom_call", output_to_operand_aliasing={{}: (2, {})} | custom-call | flops 15728640 | bytes 15728640 | tf_op jit(solution)/shard_map/combine3/pallas_call | solution.py:45
  83.9 5.5 %inner.1 = (f32[12288,128]{1,0:T(8,128)S(1)}, f32[1536,128]{1,0:T(8,128)S(1)}, f32[256,512]{1,0:T(8,128)S(1)}) custom-call(s32[128]{0:T(128)S(1)} %copy-done.3, s32[1]{0:T(128)} %bitcast.position.refs_1_, s32[768]{0:T(1024)S(1)} %mul.18.rows.refs_3_, f32[12288,128]{1,0:T(8,128)S(1)} %combine3.1.f_in), custom_call_target="tpu_custom_call", output_to_operand_aliasing={{0}: (3, {})} | custom-call | flops 15728640 | bytes 15728640 | tf_op jit(solution)/shard_map/inner/pallas_call | solution.py:45
  89.4 2.6 %finish.1 = (f32[12288,128]{1,0:T(8,128)S(1)}, f32[136,128]{1,0:T(8,128)S(1)}, f32[136,128]{1,0:T(8,128)S(1)}) custom-call(s32[1]{0:T(128)} %bitcast.position.refs_1_, s32[768]{0:T(1024)S(1)} %mul.18.rows.refs_3_, f32[768,128]{1,0:T(8,128)S(1)} %collective-permute-done.5.near_in, ...), custom_call_target="tpu_custom_call", output_to_operand_aliasing={{0}: (7, {})} | custom-call | tf_op jit(solution)/shard_map/finish/pallas_call | solution.py:45
  92.1 1.2 collective-permute-done.7.refs_1_
  93.3 26.8 %collective-permute-start.10 = (f32[136,128]{1,0:T(8,128)S(1)}, f32[136,128]{1,0:T(8,128)S(1)}, u32[]{:S(2)}, u32[]{:S(2)}) collective-permute-start(f32[136,128]{1,0:T(8,128)S(1)} %add.4.refs_0_), channel_id=1, source_target_pairs={{0,6},{1,7},{2,0},{3,1},{4,2},{5,3},{6,4},{7,5},{8,14},{9,15},{10,... | collective-permute-start | bytes 208904 | tf_op jit(solution)/shard_map/ppermute | solution.py:417
  120.8 2.2 %collective-permute-done.10.refs_3_ = f32[136,128]{1,0:T(8,128)S(1)} collective-permute-done((f32[136,128]{1,0:T(8,128)S(1)}, f32[136,128]{1,0:T(8,128)S(1)}, u32[]{:S(2)}, u32[]{:S(2)}) %collective-permute-start.10) | collective-permute-done | bytes 69664 | tf_op jit(solution)/shard_map/ppermute | solution.py:417
  123.0 1.9 %collective-permute-done.9.refs_2_ = f32[136,128]{1,0:T(8,128)S(1)} collective-permute-done((f32[136,128]{1,0:T(8,128)S(1)}, f32[136,128]{1,0:T(8,128)S(1)}, u32[]{:S(2)}, u32[]{:S(2)}) %collective-permute-start.9) | collective-permute-done | bytes 69664 | tf_op jit(solution)/shard_map/ppermute | solution.py:417
  124.9 1.8 %collective-permute-done.8.refs_1_ = f32[136,128]{1,0:T(8,128)S(1)} collective-permute-done((f32[136,128]{1,0:T(8,128)S(1)}, f32[136,128]{1,0:T(8,128)S(1)}, u32[]{:S(2)}, u32[]{:S(2)}) %collective-permute-start.8) | collective-permute-done | bytes 69664 | tf_op jit(solution)/shard_map/ppermute | solution.py:417
  127.2 3.6 %collective-permute-start.12 = (f32[136,128]{1,0:T(8,128)S(1)}, f32[136,128]{1,0:T(8,128)S(1)}, u32[]{:S(2)}, u32[]{:S(2)}) collective-permute-start(f32[136,128]{1,0:T(8,128)S(1)} %add.5.refs_0_), channel_id=1, source_target_pairs={{0,16},{1,17},{2,18},{3,19},{4,20},{5,21},{6,22},{7,23},{8,24},{9,... | collective-permute-start | bytes 208904 | tf_op jit(solution)/shard_map/ppermute | solution.py:417
  131.6 0.9 collective-permute-done.12.refs_2_
  132.5 2.9 %collective-permute-done.11.refs_1_ = f32[136,128]{1,0:T(8,128)S(1)} collective-permute-done((f32[136,128]{1,0:T(8,128)S(1)}, f32[136,128]{1,0:T(8,128)S(1)}, u32[]{:S(2)}, u32[]{:S(2)}) %collective-permute-start.11) | collective-permute-done | bytes 69664 | tf_op jit(solution)/shard_map/ppermute | solution.py:417
  135.4 9.5 %collective-permute-start.16 = (f32[136,128]{1,0:T(8,128)S(1)}, f32[136,128]{1,0:T(8,128)S(1)}, u32[]{:S(2)}, u32[]{:S(2)}) collective-permute-start(f32[136,128]{1,0:T(8,128)S(1)} %add.6.refs_0_), channel_id=1, source_target_pairs={{0,96},{1,97},{2,98},{3,99},{4,100},{5,101},{6,102},{7,103},{8,104... | collective-permute-start | bytes 208904 | tf_op jit(solution)/shard_map/ppermute | solution.py:417
  144.9 4.4 %collective-permute-start.15 = (f32[136,128]{1,0:T(8,128)S(1)}, f32[136,128]{1,0:T(8,128)S(1)}, u32[]{:S(2)}, u32[]{:S(2)}) collective-permute-start(f32[136,128]{1,0:T(8,128)S(1)} %add.6.refs_0_), channel_id=1, source_target_pairs={{0,64},{1,65},{2,66},{3,67},{4,68},{5,69},{6,70},{7,71},{8,72},{9,... | collective-permute-start | bytes 208904 | tf_op jit(solution)/shard_map/ppermute | solution.py:417
  149.3 1.7 collective-permute-done.15.refs_2_
  151.0 3.4 %collective-permute-done.14.refs_1_ = f32[136,128]{1,0:T(8,128)S(1)} collective-permute-done((f32[136,128]{1,0:T(8,128)S(1)}, f32[136,128]{1,0:T(8,128)S(1)}, u32[]{:S(2)}, u32[]{:S(2)}) %collective-permute-start.14) | collective-permute-done | bytes 69664 | tf_op jit(solution)/shard_map/ppermute | solution.py:417
  154.5 3.4 %collective-permute-start.17 = (f32[136,128]{1,0:T(8,128)S(1)}, f32[136,128]{1,0:T(8,128)S(1)}, u32[]{:S(2)}, u32[]{:S(2)}) collective-permute-start(f32[136,128]{1,0:T(8,128)S(1)} %add.7.mine), channel_id=1, source_target_pairs={{0,1},{1,0},{2,3},{3,2},{4,5},{5,4},{6,7},{7,6},{8,9},{9,8},{10,11... | collective-permute-start | bytes 208904 | tf_op jit(solution)/shard_map/ppermute | solution.py:417
  157.9 0.9 collective-permute-done.17.other
  158.8 16.8 %rotate.1 = f32[6144,256]{1,0:T(8,128)} custom-call(s32[128]{0:T(128)S(1)} %copy-done.3, s32[1]{0:T(128)} %bitcast.position.refs_1_, f32[136,128]{1,0:T(8,128)S(1)} %add.7.mine, f32[136,128]{1,0:T(8,128)S(1)} %collective-permute-done.17.other, f32[12288,128]{1,0:T(8,128)S(1)} %get-tuple-element.100.w), custom_call_target="tpu_custom_call" | custom-call | tf_op jit(solution)/shard_map/rotate/pallas_call | solution.py:45
  (33 shorter events, 3.8 us)
Async XLA Ops:
  0.7 0.7 copy-start.2
  1.4 11.0 %copy-start.4 = (s32[16,512]{1,0:T(8,128)S(1)}, s32[16,512]{1,0:T(8,128)}, u32[]{:S(2)}) copy-start(s32[16,512]{1,0:T(8,128)} %param.10) | copy-start | bytes 98308
  7.3 10.5 %collective-permute-start = (f32[776,128]{1,0:T(8,128)S(1)}, f32[776,128]{1,0:T(8,128)S(1)}, u32[]{:S(2)}, u32[]{:S(2)}) collective-permute-start(f32[776,128]{1,0:T(8,128)S(1)} %get-tuple-element.53), channel_id=1, source_target_pairs={{0,1},{1,2},{2,3},{3,4},{4,5},{5,6},{6,7},{7,8},{8,9},{9,10},{10,1... | collective-permute-start | bytes 1191944 | tf_op jit(solution)/shard_map/ppermute | solution.py:25
  26.8 8.9 %copy-start = (f32[12288,128]{1,0:T(8,128)}, f32[12288,128]{1,0:T(8,128)S(1)}, u32[]{:S(2)}) copy-start(f32[12288,128]{1,0:T(8,128)S(1)} %get-tuple-element.63.refs_0_.refs_2_) | copy-start | bytes 18874372
  26.8 8.9 %collective-permute-start.1 = (f32[768,128]{1,0:T(8,128)S(1)}, f32[768,128]{1,0:T(8,128)S(1)}, u32[]{:S(2)}, u32[]{:S(2)}) collective-permute-start(f32[768,128]{1,0:T(8,128)S(1)} %get-tuple-element.61), channel_id=1, source_target_pairs={{0,1},{1,0},{2,3},{3,2},{4,5},{5,4},{6,7},{7,6},{8,9},{9,8},{10,11... | collective-permute-start | bytes 1179656 | tf_op jit(solution)/shard_map/ppermute | solution.py:562
  28.8 9.1 %collective-permute-start.2 = (f32[768,128]{1,0:T(8,128)S(1)}, f32[768,128]{1,0:T(8,128)S(1)}, u32[]{:S(2)}, u32[]{:S(2)}) collective-permute-start(f32[768,128]{1,0:T(8,128)S(1)} %get-tuple-element.62), channel_id=1, source_target_pairs={{1,2},{2,1},{3,4},{4,3},{5,6},{6,5},{7,8},{8,7},{9,10},{10,9},{11,... | collective-permute-start | bytes 1179656 | tf_op jit(solution)/shard_map/ppermute | solution.py:561
  37.9 15.1 %copy-start.1 = (f32[12288,128]{1,0:T(8,128)S(1)}, f32[12288,128]{1,0:T(8,128)}, u32[]{:S(2)}) copy-start(f32[12288,128]{1,0:T(8,128)} %copy-done) | copy-start | bytes 18874372
  47.9 8.8 %collective-permute-start.3 = (f32[768,128]{1,0:T(8,128)S(1)}, f32[768,128]{1,0:T(8,128)S(1)}, u32[]{:S(2)}, u32[]{:S(2)}) collective-permute-start(f32[768,128]{1,0:T(8,128)S(1)} %get-tuple-element.74), channel_id=1, source_target_pairs={{0,1},{1,0},{2,3},{3,2},{4,5},{5,4},{6,7},{7,6},{8,9},{9,8},{10,11... | collective-permute-start | bytes 1179656 | tf_op jit(solution)/shard_map/ppermute | solution.py:562
  48.0 10.5 %collective-permute-start.4 = (f32[768,128]{1,0:T(8,128)S(1)}, f32[768,128]{1,0:T(8,128)S(1)}, u32[]{:S(2)}, u32[]{:S(2)}) collective-permute-start(f32[768,128]{1,0:T(8,128)S(1)} %get-tuple-element.75), channel_id=1, source_target_pairs={{1,2},{2,1},{3,4},{4,3},{5,6},{6,5},{7,8},{8,7},{9,10},{10,9},{11,... | collective-permute-start | bytes 1179656 | tf_op jit(solution)/shard_map/ppermute | solution.py:561
  68.4 20.9 %collective-permute-start.5 = (f32[768,128]{1,0:T(8,128)S(1)}, f32[768,128]{1,0:T(8,128)S(1)}, u32[]{:S(2)}, u32[]{:S(2)}) collective-permute-start(f32[768,128]{1,0:T(8,128)S(1)} %get-tuple-element.87), channel_id=1, source_target_pairs={{0,1},{1,0},{2,3},{3,2},{4,5},{5,4},{6,7},{7,6},{8,9},{9,8},{10,11... | collective-permute-start | bytes 1179656 | tf_op jit(solution)/shard_map/ppermute | solution.py:562
  68.5 20.9 %collective-permute-start.6 = (f32[768,128]{1,0:T(8,128)S(1)}, f32[768,128]{1,0:T(8,128)S(1)}, u32[]{:S(2)}, u32[]{:S(2)}) collective-permute-start(f32[768,128]{1,0:T(8,128)S(1)} %get-tuple-element.88), channel_id=1, source_target_pairs={{1,2},{2,1},{3,4},{4,3},{5,6},{6,5},{7,8},{8,7},{9,10},{10,9},{11,... | collective-permute-start | bytes 1179656 | tf_op jit(solution)/shard_map/ppermute | solution.py:561
  80.3 3.6 %copy-start.3 = (s32[128]{0:T(128)S(1)}, s32[128]{0:T(128)}, u32[]{:S(2)}) copy-start(s32[128]{0:T(128)} %counts.3) | copy-start | bytes 1540
  92.0 1.3 collective-permute-start.7
  93.3 29.7 %collective-permute-start.10 = (f32[136,128]{1,0:T(8,128)S(1)}, f32[136,128]{1,0:T(8,128)S(1)}, u32[]{:S(2)}, u32[]{:S(2)}) collective-permute-start(f32[136,128]{1,0:T(8,128)S(1)} %add.4.refs_0_), channel_id=1, source_target_pairs={{0,6},{1,7},{2,0},{3,1},{4,2},{5,3},{6,4},{7,5},{8,14},{9,15},{10,... | collective-permute-start | bytes 208904 | tf_op jit(solution)/shard_map/ppermute | solution.py:417
  120.1 4.8 %collective-permute-start.9 = (f32[136,128]{1,0:T(8,128)S(1)}, f32[136,128]{1,0:T(8,128)S(1)}, u32[]{:S(2)}, u32[]{:S(2)}) collective-permute-start(f32[136,128]{1,0:T(8,128)S(1)} %add.4.refs_0_), channel_id=1, source_target_pairs={{0,4},{1,5},{2,6},{3,7},{4,0},{5,1},{6,2},{7,3},{8,12},{9,13},{10,... | collective-permute-start | bytes 208904 | tf_op jit(solution)/shard_map/ppermute | solution.py:417
  120.1 6.5 %collective-permute-start.8 = (f32[136,128]{1,0:T(8,128)S(1)}, f32[136,128]{1,0:T(8,128)S(1)}, u32[]{:S(2)}, u32[]{:S(2)}) collective-permute-start(f32[136,128]{1,0:T(8,128)S(1)} %add.4.refs_0_), channel_id=1, source_target_pairs={{0,2},{1,3},{2,4},{3,5},{4,6},{5,7},{6,0},{7,1},{8,10},{9,11},{10,... | collective-permute-start | bytes 208904 | tf_op jit(solution)/shard_map/ppermute | solution.py:417
  126.6 4.9 %collective-permute-start.13 = (f32[136,128]{1,0:T(8,128)S(1)}, f32[136,128]{1,0:T(8,128)S(1)}, u32[]{:S(2)}, u32[]{:S(2)}) collective-permute-start(f32[136,128]{1,0:T(8,128)S(1)} %add.5.refs_0_), channel_id=1, source_target_pairs={{0,24},{1,25},{2,26},{3,27},{4,28},{5,29},{6,30},{7,31},{8,0},{9,1... | collective-permute-start | bytes 208904 | tf_op jit(solution)/shard_map/ppermute | solution.py:417
  127.2 5.3 %collective-permute-start.12 = (f32[136,128]{1,0:T(8,128)S(1)}, f32[136,128]{1,0:T(8,128)S(1)}, u32[]{:S(2)}, u32[]{:S(2)}) collective-permute-start(f32[136,128]{1,0:T(8,128)S(1)} %add.5.refs_0_), channel_id=1, source_target_pairs={{0,16},{1,17},{2,18},{3,19},{4,20},{5,21},{6,22},{7,23},{8,24},{9,... | collective-permute-start | bytes 208904 | tf_op jit(solution)/shard_map/ppermute | solution.py:417
  130.8 4.6 %collective-permute-start.11 = (f32[136,128]{1,0:T(8,128)S(1)}, f32[136,128]{1,0:T(8,128)S(1)}, u32[]{:S(2)}, u32[]{:S(2)}) collective-permute-start(f32[136,128]{1,0:T(8,128)S(1)} %add.5.refs_0_), channel_id=1, source_target_pairs={{0,8},{1,9},{2,10},{3,11},{4,12},{5,13},{6,14},{7,15},{8,16},{9,17... | collective-permute-start | bytes 208904 | tf_op jit(solution)/shard_map/ppermute | solution.py:417
  135.4 13.9 %collective-permute-start.16 = (f32[136,128]{1,0:T(8,128)S(1)}, f32[136,128]{1,0:T(8,128)S(1)}, u32[]{:S(2)}, u32[]{:S(2)}) collective-permute-start(f32[136,128]{1,0:T(8,128)S(1)} %add.6.refs_0_), channel_id=1, source_target_pairs={{0,96},{1,97},{2,98},{3,99},{4,100},{5,101},{6,102},{7,103},{8,104... | collective-permute-start | bytes 208904 | tf_op jit(solution)/shard_map/ppermute | solution.py:417
  144.9 6.1 %collective-permute-start.15 = (f32[136,128]{1,0:T(8,128)S(1)}, f32[136,128]{1,0:T(8,128)S(1)}, u32[]{:S(2)}, u32[]{:S(2)}) collective-permute-start(f32[136,128]{1,0:T(8,128)S(1)} %add.6.refs_0_), channel_id=1, source_target_pairs={{0,64},{1,65},{2,66},{3,67},{4,68},{5,69},{6,70},{7,71},{8,72},{9,... | collective-permute-start | bytes 208904 | tf_op jit(solution)/shard_map/ppermute | solution.py:417
  149.3 5.1 %collective-permute-start.14 = (f32[136,128]{1,0:T(8,128)S(1)}, f32[136,128]{1,0:T(8,128)S(1)}, u32[]{:S(2)}, u32[]{:S(2)}) collective-permute-start(f32[136,128]{1,0:T(8,128)S(1)} %add.6.refs_0_), channel_id=1, source_target_pairs={{0,32},{1,33},{2,34},{3,35},{4,36},{5,37},{6,38},{7,39},{8,40},{9,... | collective-permute-start | bytes 208904 | tf_op jit(solution)/shard_map/ppermute | solution.py:417
  154.5 4.3 %collective-permute-start.17 = (f32[136,128]{1,0:T(8,128)S(1)}, f32[136,128]{1,0:T(8,128)S(1)}, u32[]{:S(2)}, u32[]{:S(2)}) collective-permute-start(f32[136,128]{1,0:T(8,128)S(1)} %add.7.mine), channel_id=1, source_target_pairs={{0,1},{1,0},{2,3},{3,2},{4,5},{5,4},{6,7},{7,6},{8,9},{9,8},{10,11... | collective-permute-start | bytes 208904 | tf_op jit(solution)/shard_map/ppermute | solution.py:417

commit v5 on v4

--- a/solution.py
+++ b/solution.py
@@ -76,7 +76,7 @@
     def spread(g, carry):
         some = rows.at[pl.ds(shared + g * unroll, unroll)]
         for k in range(unroll):
-            lines[pl.ds(g * unroll + k, 1), :] = jnp.full((1, LANES), mass[some[k] // 2], F32)
+            lines[pl.ds(g * unroll + k, 1), :] = jnp.full((1, LANES), mass[some[k] >> 1], F32)
         return carry
 
     lax.fori_loop(0, shared // unroll, spread, 0)
@@ -95,7 +95,7 @@
         some = rows.at[pl.ds(shared + g * unroll, unroll)]
         first = pl.multiple_of(g * unroll, unroll)
         for k in range(unroll):
-            row = some[k] // 2
+            row = some[k] >> 1
             line = lines[pl.ds(first + k, 1), :]
             for h in range(2):
                 value = stage[pl.ds(h * total + row, 1), :]
@@ -169,9 +169,8 @@
 
 def ham_kernel(stage, *refs):
     count, position, nodes, rows = refs[:4]
-    n_in = 1 if stage == 1 else 2
-    received = refs[4 : 4 + n_in]
-    refs = refs[4 + n_in :]
+    received = refs[4]
+    refs = refs[5:]
     n_field = 2 + ACCS
     blocks_hbm = refs[n_field]
     refs = refs[n_field + 1 :]
@@ -179,7 +178,7 @@
     send_near, send_far, picked, x, *parts_pair, lines, block_a, block_b, sems = refs[n_field:]
     block_pair = (block_a, block_b)
 
-    shared = send_near.shape[0] // 2
+    shared = send_far.shape[0] // 2
     size = picked.shape[0] // 2
     live = count[0]
     near = near_base(position[0], shared)
@@ -195,7 +194,7 @@
         load(1, 1).start()
 
     if stage == 1:
-        (owner,) = received
+        owner = received
 
         @pl.when(position[0] > 0)
         def _():
@@ -215,9 +214,7 @@
 
             lax.fori_loop(0, shared // unroll, patch, 0)
     else:
-        scale = (1.0 if stage == 2 else 2.0) / HALF_WIDTH
-        add_rows(w, rows, near, received[0], m, scale)
-        add_rows(w, rows, far, received[1], m, scale)
+        add_rows(w, rows, far, received, m, (1.0 if stage == 2 else 2.0) / HALF_WIDTH)
 
     def convert():
         for h in range(2):
@@ -283,6 +280,10 @@
     lax.fori_loop(0, pl.cdiv(live, 2), two, 0)
     take_rows(send_near, rows, near, *accs)
     take_rows(send_far, rows, far, *accs)
+
+
+def patch_kernel(scale, position, rows, received, m, w_in, w):
+    add_rows(w, rows, near_base(position[0], received.shape[0] // 2), received, m, scale)
 
 
 def combine_kernel(stage, *refs):
@@ -556,11 +557,13 @@
     pltpu.make_async_copy(out, out_hbm, sems.at[0]).wait()
 
 
-def exchanged(near, far):
+def far_swapped(value):
     n = lax.axis_size("mesh")
-    far = lax.ppermute(far, "mesh", [(i, i - 1 + 2 * (i % 2)) for i in range(1, n - 1)])
-    near = lax.ppermute(near, "mesh", [(i, i ^ 1) for i in range(n)])
-    return near, far
+    return lax.ppermute(value, "mesh", [(i, i - 1 + 2 * (i % 2)) for i in range(1, n - 1)])
+
+
+def near_swapped(value):
+    return lax.ppermute(value, "mesh", [(i, i ^ 1) for i in range(lax.axis_size("mesh"))])
 
 
 def body(
@@ -598,7 +601,7 @@
 
     def ham(stage, received, w, m, accs):
         ins = [(element_counts, SMEM), (position, SMEM), (nodes, SMEM), (rows, SMEM)]
-        ins += [(r, VMEM) for r in received]
+        ins += [(received, VMEM)]
         first = len(ins)
         ins += [(v, KEPT) for v in (w, m, *accs)] + [(element_blocks, HBM)]
         w, m, *accs, near, far = call(
@@ -619,7 +622,19 @@
             ],
             mib=4,
         )
+        far, near = far_swapped(far), near_swapped(near)
         return w, m, accs, near, far
+
+    def patched(stage, w, m, near):
+        return call(
+            "patch%d" % stage,
+            functools.partial(patch_kernel, (1.0 if stage == 1 else 2.0) / HALF_WIDTH),
+            [(position, SMEM), (rows, SMEM), (near, VMEM), (m, KEPT), (w, KEPT)],
+            [(tall, KEPT)],
+            aliases={4: 0},
+            mib=1,
+            flops=shared * width,
+        )[0]
 
     def combine(stage, w, m, old, accs):
         ins = [(w, KEPT), (m, KEPT)] + ([(old, KEPT)] if stage > 1 else [])
@@ -639,14 +654,13 @@
         )
         return new, accs
 
-    w0, m, accs, near, far = ham(1, [owner], w0, m, accs)
-    received = exchanged(near, far)
+    w0, m, accs, near, far = ham(1, owner, w0, m, accs)
     w1, accs = combine(1, w0, m, None, accs)
-    w1, m, accs, near, far = ham(2, received, w1, m, accs)
-    received = exchanged(near, far)
+    w1 = patched(1, w1, m, near)
+    w1, m, accs, near, far = ham(2, far, w1, m, accs)
     w2, accs = combine(2, w1, m, w0, accs)
-    w2, m, accs, near, far = ham(3, received, w2, m, accs)
-    received = exchanged(near, far)
+    w2 = patched(2, w2, m, near)
+    w2, m, accs, near, far = ham(3, far, w2, m, accs)
     f, accs = combine(3, w2, m, w1, accs)
     wide = ((width, 2 * width), F32)
     pool = ((4 * shared, LANES), F32)
@@ -663,7 +677,7 @@
     f, keep, give = call(
         "finish",
         finish_kernel,
-        [(position, SMEM), (rows, SMEM), (received[0], VMEM), (received[1], VMEM)]
+        [(position, SMEM), (rows, SMEM), (near, VMEM), (far, VMEM)]
         + [(m, KEPT), (saved, KEPT), (gram, KEPT), (f, KEPT)],
         [(tall, KEPT), (half, VMEM), (half, VMEM)],
         aliases={7: 0},

time: 175 us -> 169 us (0.966); the launches traced: 176 us -> 172 us
  waiting for transfers between devices: 21 us -> 14.6 us
  Pallas kernels: 75.9 us -> 79 us
    ppermute x11, starting transfers between devices: 49.8 us -> 28.3 us  [shifted(): return lax.ppermute(value, 'mesh', route)]
    ppermute x6, starting transfers between devices: 22.1 us -> 43 us  [the longest x3 41.9 us: far_swapped(): lax.ppermute(value, 'mesh', [(i, i - 1 + 2 * (i % 2)) for i in range(1, n...]
    ppermute x6, waiting for transfers between devices: 4 us -> 0.56 us  [the longest x3 0.56 us: far_swapped(): lax.ppermute(value, 'mesh', [(i, i - 1 + 2 * (i % 2)) for i in range(1, n...]
    pallas_call x15 -> x17, Pallas kernels: 75.9 us -> 79 us  [call(): pl.pallas_call(kernel, out_shape=[pltpu.VMEM(shape, dtype) if spec is KEP...]
    ppermute x11, waiting for transfers between devices: 17 us -> 14 us  [shifted(): return lax.ppermute(value, 'mesh', route)]
  transfers between devices with their start and end apart: 18 -> 18, of which waited for: 11 -> 11; matrix products, arithmetic and copies ran while one was open for 0% -> 0% of each run, Pallas kernels for 12% -> 14%
where the time goes in v5:
time: 169 us; the launch traced here: 172 us
  Pallas kernels  79 us (47%)
  starting transfers between devices  75.9 us (45%)
  waiting for transfers between devices  14.6 us (9%)
    pallas_call x17, Pallas kernels, call(): pl.pallas_call(kernel, out_shape=[pltpu.VMEM(shape, dtype) if spec is KEP...  79 us
    ppermute x3, starting transfers between devices, far_swapped(): lax.ppermute(value, 'mesh', [(i, i - 1 + 2 * (i % 2)) for i in range(1, n...  41.9 us
    ppermute x11, starting transfers between devices, shifted(): return lax.ppermute(value, 'mesh', route)  28.3 us
    ppermute x11, waiting for transfers between devices, shifted(): return lax.ppermute(value, 'mesh', route)  14 us
    ppermute x1, starting transfers between devices, passed_along(): return lax.ppermute(block, axis, route)  4.51 us
  transfers between devices with their start and end apart: 18, of which 11 were waited for; matrix products, arithmetic and copies ran while one was open for 0% of the time, Pallas kernels for 14%

profile of v5, /device:TPU:1, one launch (start us, length us, event | category | flops | bytes accessed | tf_op | source)
XLA Modules:
  0.0 172.0 jit_solution(6360760065717932939)
XLA Ops:
  1.4 4.3 %start.1 = (f32[12288,128]{1,0:T(8,128)S(1)}, f32[776,128]{1,0:T(8,128)S(1)}) custom-call(s32[1]{0:T(128)} %bitcast.position.refs_1_, s32[768]{0:T(1024)S(1)} %mul.18.rows.refs_3_, f32[6144]{0:T(1024)S(1)} %copy-done.1, f32[6144,256]{1,0:T(8,128)} %states_hbm.1), custom_call_target="tpu_custom_call" | custom-call | tf_op jit(solution)/shard_map/start/pallas_call | solution.py:45
  5.8 4.5 %collective-permute-start = (f32[776,128]{1,0:T(8,128)S(1)}, f32[776,128]{1,0:T(8,128)S(1)}, u32[]{:S(2)}, u32[]{:S(2)}) collective-permute-start(f32[776,128]{1,0:T(8,128)S(1)} %get-tuple-element.53), channel_id=1, source_target_pairs={{0,1},{1,2},{2,3},{3,4},{4,5},{5,6},{6,7},{7,8},{8,9},{9,10},{10,1... | collective-permute-start | bytes 1191944 | tf_op jit(solution)/shard_map/ppermute | solution.py:25
  11.0 5.3 %convert.1 = (f32[12288,128]{1,0:T(8,128)S(1)}, f32[12288,128]{1,0:T(8,128)S(1)}, f32[12288,128]{1,0:T(8,128)S(1)}, f32[12288,128]{1,0:T(8,128)S(1)}, f32[12288,...) custom-call(f32[48,128]{1,0:T(8,128)S(1)} %bitcast.10, ...), custom_call_target="tpu_custom_call", output_to_operand_aliasing={{5}: (1, {})} | custom-call | flops 15728640 | bytes 15728640 | tf_op jit(solution)/shard_map/convert/pallas_call | solution.py:45
  16.3 10.0 %ham1.1 = (f32[12288,128]{1,0:T(8,128)S(1)}, f32[12288,128]{1,0:T(8,128)S(1)}, f32[12288,128]{1,0:T(8,128)S(1)}, f32[12288,128]{1,0:T(8,128)S(1)}, f32[12288,128...) custom-call(s32[1]{0:T(128)S(6)} %copy.75.refs_0_, ...), custom_call_target="tpu_custom_call", output_to_operand_aliasing={{0}: (5, {}), {1}: (6, {}), {2}: (7, {}), {3}: (8, {}), {4}... | custom-call | tf_op jit(solution)/shard_map/ham1/pallas_call | solution.py:45
  26.3 1.0 collective-permute-start.2
  27.3 13.2 %collective-permute-start.1 = (f32[768,128]{1,0:T(8,128)S(1)}, f32[768,128]{1,0:T(8,128)S(1)}, u32[]{:S(2)}, u32[]{:S(2)}) collective-permute-start(f32[768,128]{1,0:T(8,128)S(1)} %get-tuple-element.61), channel_id=1, source_target_pairs={{1,2},{2,1},{3,4},{4,3},{5,6},{6,5},{7,8},{8,7},{9,10},{10,9},{11,... | collective-permute-start | bytes 1179656 | tf_op jit(solution)/shard_map/ppermute | solution.py:562
  40.5 3.7 %combine1.1 = (f32[12288,128]{1,0:T(8,128)S(1)}, f32[12288,128]{1,0:T(8,128)S(1)}, f32[12288,128]{1,0:T(8,128)S(1)}, f32[12288,128]{1,0:T(8,128)S(1)}, f32[12288,128]{1,0:T(8,128)S(1)}) custom-call(f32[12288,128]{1,0:T(8,128)S(1)} %get-tuple-element.64.refs_0_.refs_2_, ...), custom_call_target="tpu_custom_call", output_to_operand_aliasing={{1}: (2, {}), {2}: (3, {}), {3}: (4, {}), {4}: (5, {})} | custom-call | flops 15728640 | bytes 15728640 | tf_op jit(solution)/shard_map/combine1/pallas_call | solution.py:45
  44.3 1.4 patch1.1.refs_5_
  46.0 10.1 %ham2.1 = (f32[12288,128]{1,0:T(8,128)S(1)}, f32[12288,128]{1,0:T(8,128)S(1)}, f32[12288,128]{1,0:T(8,128)S(1)}, f32[12288,128]{1,0:T(8,128)S(1)}, f32[12288,128...) custom-call(s32[1]{0:T(128)S(6)} %copy.75.refs_0_, ...), custom_call_target="tpu_custom_call", output_to_operand_aliasing={{0}: (5, {}), {1}: (6, {}), {2}: (7, {}), {3}: (8, {}), {4}... | custom-call | tf_op jit(solution)/shard_map/ham2/pallas_call | solution.py:45
  56.2 14.3 %collective-permute-start.3 = (f32[768,128]{1,0:T(8,128)S(1)}, f32[768,128]{1,0:T(8,128)S(1)}, u32[]{:S(2)}, u32[]{:S(2)}) collective-permute-start(f32[768,128]{1,0:T(8,128)S(1)} %get-tuple-element.74), channel_id=1, source_target_pairs={{1,2},{2,1},{3,4},{4,3},{5,6},{6,5},{7,8},{8,7},{9,10},{10,9},{11,... | collective-permute-start | bytes 1179656 | tf_op jit(solution)/shard_map/ppermute | solution.py:562
  70.6 3.6 %combine2.1 = (f32[12288,128]{1,0:T(8,128)S(1)}, f32[12288,128]{1,0:T(8,128)S(1)}, f32[12288,128]{1,0:T(8,128)S(1)}, f32[12288,128]{1,0:T(8,128)S(1)}, f32[12288,128]{1,0:T(8,128)S(1)}) custom-call(f32[12288,128]{1,0:T(8,128)S(1)} %get-tuple-element.77.refs_0_.refs_2_, ...), custom_call_target="tpu_custom_call", output_to_operand_aliasing={{1}: (3, {}), {2}: (4, {}), {3}: (5, {}), {4}: (6, {}), {0}... | custom-call | flops 15728640 | bytes 15728640 | tf_op jit(solution)/shard_map/combine2/pallas_call | solution.py:45
  74.2 1.4 patch2.1.refs_5_
  76.0 10.1 %ham3.1 = (f32[12288,128]{1,0:T(8,128)S(1)}, f32[12288,128]{1,0:T(8,128)S(1)}, f32[12288,128]{1,0:T(8,128)S(1)}, f32[12288,128]{1,0:T(8,128)S(1)}, f32[12288,128...) custom-call(s32[1]{0:T(128)S(6)} %copy.75.refs_0_, ...), custom_call_target="tpu_custom_call", output_to_operand_aliasing={{0}: (5, {}), {1}: (6, {}), {2}: (7, {}), {3}: (8, {}), {4}... | custom-call | tf_op jit(solution)/shard_map/ham3/pallas_call | solution.py:45
  86.2 14.3 %collective-permute-start.6 = (f32[768,128]{1,0:T(8,128)S(1)}, f32[768,128]{1,0:T(8,128)S(1)}, u32[]{:S(2)}, u32[]{:S(2)}) collective-permute-start(f32[768,128]{1,0:T(8,128)S(1)} %get-tuple-element.88), channel_id=1, source_target_pairs={{1,2},{2,1},{3,4},{4,3},{5,6},{6,5},{7,8},{8,7},{9,10},{10,9},{11,... | collective-permute-start | bytes 1179656 | tf_op jit(solution)/shard_map/ppermute | solution.py:562
  100.6 3.5 %combine3.1.f_in = f32[12288,128]{1,0:T(8,128)S(1)} custom-call(f32[12288,128]{1,0:T(8,128)S(1)} %get-tuple-element.90.refs_0_, f32[12288,128]{1,0:T(8,128)S(1)} %get-tuple-element.89.refs_1_.m, f32[12288,128]{1,0:T(8,128)S(1)} %get-tuple-element.77.refs_0_.refs_2_, f32[12288,128]{1,0:T(8,128)S(1)} %get-tuple-element.91.refs_3_, ...), custom_call_target="tpu_custom_call", output_to_operand_aliasing={{}: (2, {})} | custom-call | flops 15728640 | bytes 15728640 | tf_op jit(solution)/shard_map/combine3/pallas_call | solution.py:45
  104.2 5.8 %inner.1 = (f32[12288,128]{1,0:T(8,128)S(1)}, f32[1536,128]{1,0:T(8,128)S(1)}, f32[256,512]{1,0:T(8,128)S(1)}) custom-call(s32[128]{0:T(128)S(1)} %copy-done.2, s32[1]{0:T(128)} %bitcast.position.refs_1_, s32[768]{0:T(1024)S(1)} %mul.18.rows.refs_3_, f32[12288,128]{1,0:T(8,128)S(1)} %combine3.1.f_in), custom_call_target="tpu_custom_call", output_to_operand_aliasing={{0}: (3, {})} | custom-call | flops 15728640 | bytes 15728640 | tf_op jit(solution)/shard_map/inner/pallas_call | solution.py:45
  110.0 2.6 %finish.1 = (f32[12288,128]{1,0:T(8,128)S(1)}, f32[136,128]{1,0:T(8,128)S(1)}, f32[136,128]{1,0:T(8,128)S(1)}) custom-call(s32[1]{0:T(128)} %bitcast.position.refs_1_, s32[768]{0:T(1024)S(1)} %mul.18.rows.refs_3_, f32[768,128]{1,0:T(8,128)S(1)} %collective-permute-done.5.near_in, ...), custom_call_target="tpu_custom_call", output_to_operand_aliasing={{0}: (7, {})} | custom-call | tf_op jit(solution)/shard_map/finish/pallas_call | solution.py:45
  112.7 1.2 collective-permute-done.7.refs_1_
  114.0 1.9 %collective-permute-start.9 = (f32[136,128]{1,0:T(8,128)S(1)}, f32[136,128]{1,0:T(8,128)S(1)}, u32[]{:S(2)}, u32[]{:S(2)}) collective-permute-start(f32[136,128]{1,0:T(8,128)S(1)} %add.4.refs_0_), channel_id=1, source_target_pairs={{0,4},{1,5},{2,6},{3,7},{4,0},{5,1},{6,2},{7,3},{8,12},{9,13},{10,... | collective-permute-start | bytes 208904 | tf_op jit(solution)/shard_map/ppermute | solution.py:418
  116.6 1.0 collective-permute-done.10.refs_3_
  117.6 1.6 collective-permute-done.9.refs_2_
  119.2 1.0 collective-permute-done.8.refs_1_
  120.4 4.7 %collective-permute-start.12 = (f32[136,128]{1,0:T(8,128)S(1)}, f32[136,128]{1,0:T(8,128)S(1)}, u32[]{:S(2)}, u32[]{:S(2)}) collective-permute-start(f32[136,128]{1,0:T(8,128)S(1)} %add.5.refs_0_), channel_id=1, source_target_pairs={{0,16},{1,17},{2,18},{3,19},{4,20},{5,21},{6,22},{7,23},{8,24},{9,... | collective-permute-start | bytes 208904 | tf_op jit(solution)/shard_map/ppermute | solution.py:418
  125.5 1.2 collective-permute-done.12.refs_2_
  126.8 2.7 %collective-permute-done.11.refs_1_ = f32[136,128]{1,0:T(8,128)S(1)} collective-permute-done((f32[136,128]{1,0:T(8,128)S(1)}, f32[136,128]{1,0:T(8,128)S(1)}, u32[]{:S(2)}, u32[]{:S(2)}) %collective-permute-start.11) | collective-permute-done | bytes 69664 | tf_op jit(solution)/shard_map/ppermute | solution.py:418
  129.5 11.9 %collective-permute-start.16 = (f32[136,128]{1,0:T(8,128)S(1)}, f32[136,128]{1,0:T(8,128)S(1)}, u32[]{:S(2)}, u32[]{:S(2)}) collective-permute-start(f32[136,128]{1,0:T(8,128)S(1)} %add.6.refs_0_), channel_id=1, source_target_pairs={{0,96},{1,97},{2,98},{3,99},{4,100},{5,101},{6,102},{7,103},{8,104... | collective-permute-start | bytes 208904 | tf_op jit(solution)/shard_map/ppermute | solution.py:418
  141.4 4.4 %collective-permute-start.15 = (f32[136,128]{1,0:T(8,128)S(1)}, f32[136,128]{1,0:T(8,128)S(1)}, u32[]{:S(2)}, u32[]{:S(2)}) collective-permute-start(f32[136,128]{1,0:T(8,128)S(1)} %add.6.refs_0_), channel_id=1, source_target_pairs={{0,64},{1,65},{2,66},{3,67},{4,68},{5,69},{6,70},{7,71},{8,72},{9,... | collective-permute-start | bytes 208904 | tf_op jit(solution)/shard_map/ppermute | solution.py:418
  146.6 0.9 collective-permute-done.15.refs_2_
  147.5 3.4 %collective-permute-done.14.refs_1_ = f32[136,128]{1,0:T(8,128)S(1)} collective-permute-done((f32[136,128]{1,0:T(8,128)S(1)}, f32[136,128]{1,0:T(8,128)S(1)}, u32[]{:S(2)}, u32[]{:S(2)}) %collective-permute-start.14) | collective-permute-done | bytes 69664 | tf_op jit(solution)/shard_map/ppermute | solution.py:418
  150.9 3.2 %collective-permute-start.17 = (f32[136,128]{1,0:T(8,128)S(1)}, f32[136,128]{1,0:T(8,128)S(1)}, u32[]{:S(2)}, u32[]{:S(2)}) collective-permute-start(f32[136,128]{1,0:T(8,128)S(1)} %add.7.mine), channel_id=1, source_target_pairs={{0,1},{1,0},{2,3},{3,2},{4,5},{5,4},{6,7},{7,6},{8,9},{9,8},{10,11... | collective-permute-start | bytes 208904 | tf_op jit(solution)/shard_map/ppermute | solution.py:418
  154.1 0.9 collective-permute-done.17.other
  155.0 16.8 %rotate.1 = f32[6144,256]{1,0:T(8,128)} custom-call(s32[128]{0:T(128)S(1)} %copy-done.2, s32[1]{0:T(128)} %bitcast.position.refs_1_, f32[136,128]{1,0:T(8,128)S(1)} %add.7.mine, f32[136,128]{1,0:T(8,128)S(1)} %collective-permute-done.17.other, f32[12288,128]{1,0:T(8,128)S(1)} %get-tuple-element.100.w), custom_call_target="tpu_custom_call" | custom-call | tf_op jit(solution)/shard_map/rotate/pallas_call | solution.py:45
  (38 shorter events, 4.5 us)
Async XLA Ops:
  0.7 0.7 copy-start.1
  1.4 9.5 %copy-start.3 = (s32[16,512]{1,0:T(8,128)S(1)}, s32[16,512]{1,0:T(8,128)}, u32[]{:S(2)}) copy-start(s32[16,512]{1,0:T(8,128)} %param.10) | copy-start | bytes 98308
  5.8 10.5 %collective-permute-start = (f32[776,128]{1,0:T(8,128)S(1)}, f32[776,128]{1,0:T(8,128)S(1)}, u32[]{:S(2)}, u32[]{:S(2)}) collective-permute-start(f32[776,128]{1,0:T(8,128)S(1)} %get-tuple-element.53), channel_id=1, source_target_pairs={{0,1},{1,2},{2,3},{3,4},{4,5},{5,6},{6,7},{7,8},{8,9},{9,10},{10,1... | collective-permute-start | bytes 1191944 | tf_op jit(solution)/shard_map/ppermute | solution.py:25
  26.3 18.0 %copy-start = (f32[12288,128]{1,0:T(8,128)}, f32[12288,128]{1,0:T(8,128)S(1)}, u32[]{:S(2)}) copy-start(f32[12288,128]{1,0:T(8,128)S(1)} %get-tuple-element.64.refs_0_.refs_2_) | copy-start | bytes 18874372
  26.3 18.0 %collective-permute-start.2 = (f32[768,128]{1,0:T(8,128)S(1)}, f32[768,128]{1,0:T(8,128)S(1)}, u32[]{:S(2)}, u32[]{:S(2)}) collective-permute-start(f32[768,128]{1,0:T(8,128)S(1)} %get-tuple-element.62), channel_id=1, source_target_pairs={{0,1},{1,0},{2,3},{3,2},{4,5},{5,4},{6,7},{7,6},{8,9},{9,8},{10,11... | collective-permute-start | bytes 1179656 | tf_op jit(solution)/shard_map/ppermute | solution.py:566
  27.3 18.6 %collective-permute-start.1 = (f32[768,128]{1,0:T(8,128)S(1)}, f32[768,128]{1,0:T(8,128)S(1)}, u32[]{:S(2)}, u32[]{:S(2)}) collective-permute-start(f32[768,128]{1,0:T(8,128)S(1)} %get-tuple-element.61), channel_id=1, source_target_pairs={{1,2},{2,1},{3,4},{4,3},{5,6},{6,5},{7,8},{8,7},{9,10},{10,9},{11,... | collective-permute-start | bytes 1179656 | tf_op jit(solution)/shard_map/ppermute | solution.py:562
  44.3 26.3 %slice-start = ((s8[6291456]{0:T(1024)(128)(4,1)}), s8[4194304]{0:T(1024)(128)(4,1)S(1)}, s32[]{:S(2)}) async-start(s8[6291456]{0:T(1024)(128)(4,1)} %bitcast.5), calls=%async_computation | async-start | bytes 8388608
  46.0 24.6 %slice-start.1 = ((s8[6291456]{0:T(1024)(128)(4,1)}), s8[2097152]{0:T(1024)(128)(4,1)S(1)}, s32[]{:S(2)}) async-start(s8[6291456]{0:T(1024)(128)(4,1)} %bitcast.5), calls=%async_computation.1 | async-start | bytes 4194304
  56.1 18.1 %collective-permute-start.4 = (f32[768,128]{1,0:T(8,128)S(1)}, f32[768,128]{1,0:T(8,128)S(1)}, u32[]{:S(2)}, u32[]{:S(2)}) collective-permute-start(f32[768,128]{1,0:T(8,128)S(1)} %get-tuple-element.75), channel_id=1, source_target_pairs={{0,1},{1,0},{2,3},{3,2},{4,5},{5,4},{6,7},{7,6},{8,9},{9,8},{10,11... | collective-permute-start | bytes 1179656 | tf_op jit(solution)/shard_map/ppermute | solution.py:566
  56.2 19.8 %collective-permute-start.3 = (f32[768,128]{1,0:T(8,128)S(1)}, f32[768,128]{1,0:T(8,128)S(1)}, u32[]{:S(2)}, u32[]{:S(2)}) collective-permute-start(f32[768,128]{1,0:T(8,128)S(1)} %get-tuple-element.74), channel_id=1, source_target_pairs={{1,2},{2,1},{3,4},{4,3},{5,6},{6,5},{7,8},{8,7},{9,10},{10,9},{11,... | collective-permute-start | bytes 1179656 | tf_op jit(solution)/shard_map/ppermute | solution.py:562
  86.2 23.8 %collective-permute-start.5 = (f32[768,128]{1,0:T(8,128)S(1)}, f32[768,128]{1,0:T(8,128)S(1)}, u32[]{:S(2)}, u32[]{:S(2)}) collective-permute-start(f32[768,128]{1,0:T(8,128)S(1)} %get-tuple-element.87), channel_id=1, source_target_pairs={{0,1},{1,0},{2,3},{3,2},{4,5},{5,4},{6,7},{7,6},{8,9},{9,8},{10,11... | collective-permute-start | bytes 1179656 | tf_op jit(solution)/shard_map/ppermute | solution.py:566
  86.2 23.7 %collective-permute-start.6 = (f32[768,128]{1,0:T(8,128)S(1)}, f32[768,128]{1,0:T(8,128)S(1)}, u32[]{:S(2)}, u32[]{:S(2)}) collective-permute-start(f32[768,128]{1,0:T(8,128)S(1)} %get-tuple-element.88), channel_id=1, source_target_pairs={{1,2},{2,1},{3,4},{4,3},{5,6},{6,5},{7,8},{8,7},{9,10},{10,9},{11,... | collective-permute-start | bytes 1179656 | tf_op jit(solution)/shard_map/ppermute | solution.py:562
  100.6 3.6 %copy-start.2 = (s32[128]{0:T(128)S(1)}, s32[128]{0:T(128)}, u32[]{:S(2)}) copy-start(s32[128]{0:T(128)} %counts.3) | copy-start | bytes 1540
  112.6 1.3 collective-permute-start.7
  113.9 3.7 %collective-permute-start.10 = (f32[136,128]{1,0:T(8,128)S(1)}, f32[136,128]{1,0:T(8,128)S(1)}, u32[]{:S(2)}, u32[]{:S(2)}) collective-permute-start(f32[136,128]{1,0:T(8,128)S(1)} %add.4.refs_0_), channel_id=1, source_target_pairs={{0,6},{1,7},{2,0},{3,1},{4,2},{5,3},{6,4},{7,5},{8,14},{9,15},{10,... | collective-permute-start | bytes 208904 | tf_op jit(solution)/shard_map/ppermute | solution.py:418
  114.0 5.2 %collective-permute-start.9 = (f32[136,128]{1,0:T(8,128)S(1)}, f32[136,128]{1,0:T(8,128)S(1)}, u32[]{:S(2)}, u32[]{:S(2)}) collective-permute-start(f32[136,128]{1,0:T(8,128)S(1)} %add.4.refs_0_), channel_id=1, source_target_pairs={{0,4},{1,5},{2,6},{3,7},{4,0},{5,1},{6,2},{7,3},{8,12},{9,13},{10,... | collective-permute-start | bytes 208904 | tf_op jit(solution)/shard_map/ppermute | solution.py:418
  115.9 4.4 %collective-permute-start.8 = (f32[136,128]{1,0:T(8,128)S(1)}, f32[136,128]{1,0:T(8,128)S(1)}, u32[]{:S(2)}, u32[]{:S(2)}) collective-permute-start(f32[136,128]{1,0:T(8,128)S(1)} %add.4.refs_0_), channel_id=1, source_target_pairs={{0,2},{1,3},{2,4},{3,5},{4,6},{5,7},{6,0},{7,1},{8,10},{9,11},{10,... | collective-permute-start | bytes 208904 | tf_op jit(solution)/shard_map/ppermute | solution.py:418
  120.3 5.3 %collective-permute-start.13 = (f32[136,128]{1,0:T(8,128)S(1)}, f32[136,128]{1,0:T(8,128)S(1)}, u32[]{:S(2)}, u32[]{:S(2)}) collective-permute-start(f32[136,128]{1,0:T(8,128)S(1)} %add.5.refs_0_), channel_id=1, source_target_pairs={{0,24},{1,25},{2,26},{3,27},{4,28},{5,29},{6,30},{7,31},{8,0},{9,1... | collective-permute-start | bytes 208904 | tf_op jit(solution)/shard_map/ppermute | solution.py:418
  120.4 6.4 %collective-permute-start.12 = (f32[136,128]{1,0:T(8,128)S(1)}, f32[136,128]{1,0:T(8,128)S(1)}, u32[]{:S(2)}, u32[]{:S(2)}) collective-permute-start(f32[136,128]{1,0:T(8,128)S(1)} %add.5.refs_0_), channel_id=1, source_target_pairs={{0,16},{1,17},{2,18},{3,19},{4,20},{5,21},{6,22},{7,23},{8,24},{9,... | collective-permute-start | bytes 208904 | tf_op jit(solution)/shard_map/ppermute | solution.py:418
  125.1 4.4 %collective-permute-start.11 = (f32[136,128]{1,0:T(8,128)S(1)}, f32[136,128]{1,0:T(8,128)S(1)}, u32[]{:S(2)}, u32[]{:S(2)}) collective-permute-start(f32[136,128]{1,0:T(8,128)S(1)} %add.5.refs_0_), channel_id=1, source_target_pairs={{0,8},{1,9},{2,10},{3,11},{4,12},{5,13},{6,14},{7,15},{8,16},{9,17... | collective-permute-start | bytes 208904 | tf_op jit(solution)/shard_map/ppermute | solution.py:418
  129.5 17.1 %collective-permute-start.16 = (f32[136,128]{1,0:T(8,128)S(1)}, f32[136,128]{1,0:T(8,128)S(1)}, u32[]{:S(2)}, u32[]{:S(2)}) collective-permute-start(f32[136,128]{1,0:T(8,128)S(1)} %add.6.refs_0_), channel_id=1, source_target_pairs={{0,96},{1,97},{2,98},{3,99},{4,100},{5,101},{6,102},{7,103},{8,104... | collective-permute-start | bytes 208904 | tf_op jit(solution)/shard_map/ppermute | solution.py:418
  141.4 6.1 %collective-permute-start.15 = (f32[136,128]{1,0:T(8,128)S(1)}, f32[136,128]{1,0:T(8,128)S(1)}, u32[]{:S(2)}, u32[]{:S(2)}) collective-permute-start(f32[136,128]{1,0:T(8,128)S(1)} %add.6.refs_0_), channel_id=1, source_target_pairs={{0,64},{1,65},{2,66},{3,67},{4,68},{5,69},{6,70},{7,71},{8,72},{9,... | collective-permute-start | bytes 208904 | tf_op jit(solution)/shard_map/ppermute | solution.py:418
  145.8 5.1 %collective-permute-start.14 = (f32[136,128]{1,0:T(8,128)S(1)}, f32[136,128]{1,0:T(8,128)S(1)}, u32[]{:S(2)}, u32[]{:S(2)}) collective-permute-start(f32[136,128]{1,0:T(8,128)S(1)} %add.6.refs_0_), channel_id=1, source_target_pairs={{0,32},{1,33},{2,34},{3,35},{4,36},{5,37},{6,38},{7,39},{8,40},{9,... | collective-permute-start | bytes 208904 | tf_op jit(solution)/shard_map/ppermute | solution.py:418
  150.9 4.1 %collective-permute-start.17 = (f32[136,128]{1,0:T(8,128)S(1)}, f32[136,128]{1,0:T(8,128)S(1)}, u32[]{:S(2)}, u32[]{:S(2)}) collective-permute-start(f32[136,128]{1,0:T(8,128)S(1)} %add.7.mine), channel_id=1, source_target_pairs={{0,1},{1,0},{2,3},{3,2},{4,5},{5,4},{6,7},{7,6},{8,9},{9,8},{10,11... | collective-permute-start | bytes 208904 | tf_op jit(solution)/shard_map/ppermute | solution.py:418

commit v6 on v5

--- a/solution.py
+++ b/solution.py
@@ -350,7 +350,7 @@
     lax.fori_loop(0, 2 * shared // unroll, blank, 0)
     gram[...] = jnp.zeros_like(gram)
     limit = counts[position[0]]
-    n = 512
+    n = 1024
 
     def add_chunk(c, carry):
         live = c * n + lax.broadcasted_iota(jnp.int32, (n, 2 * LANES), 0) < limit
@@ -540,7 +540,7 @@
     )
     basis[0:n, :], basis[n : 2 * n, :] = high_low(inverse_t)
     limit = counts[position[0]]
-    size = 512
+    size = 1024
 
     def chunk(c, carry):
         at = span(c * size, size)

time: 169 us -> 170 us (level); the launches traced: 172 us -> 168 us
  starting transfers between devices: 75.9 us -> 64.7 us
  Pallas kernels: 79 us -> 83.1 us
  waiting for transfers between devices: 14.6 us -> 17.7 us
    ppermute x3, starting transfers between devices: 41.9 us -> 28.8 us  [far_swapped(): lax.ppermute(value, 'mesh', [(i, i - 1 + 2 * (i % 2)) for i in range(1, n...]
    pallas_call x17, Pallas kernels: 79 us -> 83.1 us  [call(): pl.pallas_call(kernel, out_shape=[pltpu.VMEM(shape, dtype) if spec is KEP...]
    ppermute x11, waiting for transfers between devices: 14 us -> 17.1 us  [shifted(): return lax.ppermute(value, 'mesh', route)]
    ppermute x11, starting transfers between devices: 28.3 us -> 31.2 us  [shifted(): return lax.ppermute(value, 'mesh', route)]
  transfers between devices with their start and end apart: 18 -> 18, of which waited for: 11 -> 12; matrix products, arithmetic and copies ran while one was open for 0% -> 0% of each run, Pallas kernels for 14% -> 14%
where the time goes in v6:
time: 170 us; the launch traced here: 168 us
  Pallas kernels  83.1 us (49%)
  starting transfers between devices  64.7 us (38%)
  waiting for transfers between devices  17.7 us (10%)
    pallas_call x17, Pallas kernels, call(): pl.pallas_call(kernel, out_shape=[pltpu.VMEM(shape, dtype) if spec is KEP...  83.1 us
    ppermute x11, starting transfers between devices, shifted(): return lax.ppermute(value, 'mesh', route)  31.2 us
    ppermute x3, starting transfers between devices, far_swapped(): lax.ppermute(value, 'mesh', [(i, i - 1 + 2 * (i % 2)) for i in range(1, n...  28.8 us
    ppermute x11, waiting for transfers between devices, shifted(): return lax.ppermute(value, 'mesh', route)  17.1 us
    ppermute x1, starting transfers between devices, passed_along(): return lax.ppermute(block, axis, route)  4.51 us
  transfers between devices with their start and end apart: 18, of which 12 were waited for; matrix products, arithmetic and copies ran while one was open for 0% of the time, Pallas kernels for 14%

profile of v6, /device:TPU:1, one launch (start us, length us, event | category | flops | bytes accessed | tf_op | source)
XLA Modules:
  0.0 168.1 jit_solution(13848740409638871343)
XLA Ops:
  0.7 0.7 copy-done.1
  1.4 4.3 %start.1 = (f32[12288,128]{1,0:T(8,128)S(1)}, f32[776,128]{1,0:T(8,128)S(1)}) custom-call(s32[1]{0:T(128)} %bitcast.position.refs_1_, s32[768]{0:T(1024)S(1)} %mul.18.rows.refs_3_, f32[6144]{0:T(1024)S(1)} %copy-done.1, f32[6144,256]{1,0:T(8,128)} %states_hbm.1), custom_call_target="tpu_custom_call" | custom-call | tf_op jit(solution)/shard_map/start/pallas_call | solution.py:45
  5.8 4.5 %collective-permute-start = (f32[776,128]{1,0:T(8,128)S(1)}, f32[776,128]{1,0:T(8,128)S(1)}, u32[]{:S(2)}, u32[]{:S(2)}) collective-permute-start(f32[776,128]{1,0:T(8,128)S(1)} %get-tuple-element.53), channel_id=1, source_target_pairs={{0,1},{1,2},{2,3},{3,4},{4,5},{5,6},{6,7},{7,8},{8,9},{9,10},{10,1... | collective-permute-start | bytes 1191944 | tf_op jit(solution)/shard_map/ppermute | solution.py:25
  11.0 5.3 %convert.1 = (f32[12288,128]{1,0:T(8,128)S(1)}, f32[12288,128]{1,0:T(8,128)S(1)}, f32[12288,128]{1,0:T(8,128)S(1)}, f32[12288,128]{1,0:T(8,128)S(1)}, f32[12288,...) custom-call(f32[48,128]{1,0:T(8,128)S(1)} %bitcast.10, ...), custom_call_target="tpu_custom_call", output_to_operand_aliasing={{5}: (1, {})} | custom-call | flops 15728640 | bytes 15728640 | tf_op jit(solution)/shard_map/convert/pallas_call | solution.py:45
  16.3 11.9 %ham1.1 = (f32[12288,128]{1,0:T(8,128)S(1)}, f32[12288,128]{1,0:T(8,128)S(1)}, f32[12288,128]{1,0:T(8,128)S(1)}, f32[12288,128]{1,0:T(8,128)S(1)}, f32[12288,128...) custom-call(s32[1]{0:T(128)S(6)} %copy.75.refs_0_, ...), custom_call_target="tpu_custom_call", output_to_operand_aliasing={{0}: (5, {}), {1}: (6, {}), {2}: (7, {}), {3}: (8, {}), {4}... | custom-call | tf_op jit(solution)/shard_map/ham1/pallas_call | solution.py:45
  28.3 4.4 %collective-permute-start.1 = (f32[768,128]{1,0:T(8,128)S(1)}, f32[768,128]{1,0:T(8,128)S(1)}, u32[]{:S(2)}, u32[]{:S(2)}) collective-permute-start(f32[768,128]{1,0:T(8,128)S(1)} %get-tuple-element.61), channel_id=1, source_target_pairs={{1,2},{2,1},{3,4},{4,3},{5,6},{6,5},{7,8},{8,7},{9,10},{10,9},{11,... | collective-permute-start | bytes 1179656 | tf_op jit(solution)/shard_map/ppermute | solution.py:562
  32.8 3.7 %combine1.1 = (f32[12288,128]{1,0:T(8,128)S(1)}, f32[12288,128]{1,0:T(8,128)S(1)}, f32[12288,128]{1,0:T(8,128)S(1)}, f32[12288,128]{1,0:T(8,128)S(1)}, f32[12288,128]{1,0:T(8,128)S(1)}) custom-call(f32[12288,128]{1,0:T(8,128)S(1)} %get-tuple-element.64.refs_0_.refs_2_, ...), custom_call_target="tpu_custom_call", output_to_operand_aliasing={{1}: (2, {}), {2}: (3, {}), {3}: (4, {}), {4}: (5, {})} | custom-call | flops 15728640 | bytes 15728640 | tf_op jit(solution)/shard_map/combine1/pallas_call | solution.py:45
  36.5 1.4 patch1.1.refs_5_
  38.2 12.1 %ham2.1 = (f32[12288,128]{1,0:T(8,128)S(1)}, f32[12288,128]{1,0:T(8,128)S(1)}, f32[12288,128]{1,0:T(8,128)S(1)}, f32[12288,128]{1,0:T(8,128)S(1)}, f32[12288,128...) custom-call(s32[1]{0:T(128)S(6)} %copy.75.refs_0_, ...), custom_call_target="tpu_custom_call", output_to_operand_aliasing={{0}: (5, {}), {1}: (6, {}), {2}: (7, {}), {3}: (8, {}), {4}... | custom-call | tf_op jit(solution)/shard_map/ham2/pallas_call | solution.py:45
  50.4 11.9 %collective-permute-start.3 = (f32[768,128]{1,0:T(8,128)S(1)}, f32[768,128]{1,0:T(8,128)S(1)}, u32[]{:S(2)}, u32[]{:S(2)}) collective-permute-start(f32[768,128]{1,0:T(8,128)S(1)} %get-tuple-element.74), channel_id=1, source_target_pairs={{1,2},{2,1},{3,4},{4,3},{5,6},{6,5},{7,8},{8,7},{9,10},{10,9},{11,... | collective-permute-start | bytes 1179656 | tf_op jit(solution)/shard_map/ppermute | solution.py:562
  62.3 3.6 %combine2.1 = (f32[12288,128]{1,0:T(8,128)S(1)}, f32[12288,128]{1,0:T(8,128)S(1)}, f32[12288,128]{1,0:T(8,128)S(1)}, f32[12288,128]{1,0:T(8,128)S(1)}, f32[12288,128]{1,0:T(8,128)S(1)}) custom-call(f32[12288,128]{1,0:T(8,128)S(1)} %get-tuple-element.77.refs_0_.refs_2_, ...), custom_call_target="tpu_custom_call", output_to_operand_aliasing={{1}: (3, {}), {2}: (4, {}), {3}: (5, {}), {4}: (6, {}), {0}... | custom-call | flops 15728640 | bytes 15728640 | tf_op jit(solution)/shard_map/combine2/pallas_call | solution.py:45
  66.0 1.4 patch2.1.refs_5_
  67.7 12.1 %ham3.1 = (f32[12288,128]{1,0:T(8,128)S(1)}, f32[12288,128]{1,0:T(8,128)S(1)}, f32[12288,128]{1,0:T(8,128)S(1)}, f32[12288,128]{1,0:T(8,128)S(1)}, f32[12288,128...) custom-call(s32[1]{0:T(128)S(6)} %copy.75.refs_0_, ...), custom_call_target="tpu_custom_call", output_to_operand_aliasing={{0}: (5, {}), {1}: (6, {}), {2}: (7, {}), {3}: (8, {}), {4}... | custom-call | tf_op jit(solution)/shard_map/ham3/pallas_call | solution.py:45
  79.9 12.5 %collective-permute-start.6 = (f32[768,128]{1,0:T(8,128)S(1)}, f32[768,128]{1,0:T(8,128)S(1)}, u32[]{:S(2)}, u32[]{:S(2)}) collective-permute-start(f32[768,128]{1,0:T(8,128)S(1)} %get-tuple-element.88), channel_id=1, source_target_pairs={{1,2},{2,1},{3,4},{4,3},{5,6},{6,5},{7,8},{8,7},{9,10},{10,9},{11,... | collective-permute-start | bytes 1179656 | tf_op jit(solution)/shard_map/ppermute | solution.py:562
  92.4 3.5 %combine3.1.f_in = f32[12288,128]{1,0:T(8,128)S(1)} custom-call(f32[12288,128]{1,0:T(8,128)S(1)} %get-tuple-element.90.refs_0_, f32[12288,128]{1,0:T(8,128)S(1)} %get-tuple-element.89.refs_1_.m, f32[12288,128]{1,0:T(8,128)S(1)} %get-tuple-element.77.refs_0_.refs_2_, f32[12288,128]{1,0:T(8,128)S(1)} %get-tuple-element.91.refs_3_, ...), custom_call_target="tpu_custom_call", output_to_operand_aliasing={{}: (2, {})} | custom-call | flops 15728640 | bytes 15728640 | tf_op jit(solution)/shard_map/combine3/pallas_call | solution.py:45
  96.0 5.0 %inner.1 = (f32[12288,128]{1,0:T(8,128)S(1)}, f32[1536,128]{1,0:T(8,128)S(1)}, f32[256,512]{1,0:T(8,128)S(1)}) custom-call(s32[128]{0:T(128)S(1)} %copy-done.2, s32[1]{0:T(128)} %bitcast.position.refs_1_, s32[768]{0:T(1024)S(1)} %mul.18.rows.refs_3_, f32[12288,128]{1,0:T(8,128)S(1)} %combine3.1.f_in), custom_call_target="tpu_custom_call", output_to_operand_aliasing={{0}: (3, {})} | custom-call | flops 15728640 | bytes 15728640 | tf_op jit(solution)/shard_map/inner/pallas_call | solution.py:45
  101.0 2.6 %finish.1 = (f32[12288,128]{1,0:T(8,128)S(1)}, f32[136,128]{1,0:T(8,128)S(1)}, f32[136,128]{1,0:T(8,128)S(1)}) custom-call(s32[1]{0:T(128)} %bitcast.position.refs_1_, s32[768]{0:T(1024)S(1)} %mul.18.rows.refs_3_, f32[768,128]{1,0:T(8,128)S(1)} %collective-permute-done.5.near_in, ...), custom_call_target="tpu_custom_call", output_to_operand_aliasing={{0}: (7, {})} | custom-call | tf_op jit(solution)/shard_map/finish/pallas_call | solution.py:45
  103.6 1.2 collective-permute-done.7.refs_1_
  104.9 14.2 %collective-permute-start.10 = (f32[136,128]{1,0:T(8,128)S(1)}, f32[136,128]{1,0:T(8,128)S(1)}, u32[]{:S(2)}, u32[]{:S(2)}) collective-permute-start(f32[136,128]{1,0:T(8,128)S(1)} %add.4.refs_0_), channel_id=1, source_target_pairs={{0,6},{1,7},{2,0},{3,1},{4,2},{5,3},{6,4},{7,5},{8,14},{9,15},{10,... | collective-permute-start | bytes 208904 | tf_op jit(solution)/shard_map/ppermute | solution.py:418
  119.6 0.8 collective-permute-start.8
  120.5 3.4 %collective-permute-done.9.refs_2_ = f32[136,128]{1,0:T(8,128)S(1)} collective-permute-done((f32[136,128]{1,0:T(8,128)S(1)}, f32[136,128]{1,0:T(8,128)S(1)}, u32[]{:S(2)}, u32[]{:S(2)}) %collective-permute-start.9) | collective-permute-done | bytes 69664 | tf_op jit(solution)/shard_map/ppermute | solution.py:418
  123.8 2.3 %collective-permute-done.8.refs_1_ = f32[136,128]{1,0:T(8,128)S(1)} collective-permute-done((f32[136,128]{1,0:T(8,128)S(1)}, f32[136,128]{1,0:T(8,128)S(1)}, u32[]{:S(2)}, u32[]{:S(2)}) %collective-permute-start.8) | collective-permute-done | bytes 69664 | tf_op jit(solution)/shard_map/ppermute | solution.py:418
  126.1 2.8 %collective-permute-start.13 = (f32[136,128]{1,0:T(8,128)S(1)}, f32[136,128]{1,0:T(8,128)S(1)}, u32[]{:S(2)}, u32[]{:S(2)}) collective-permute-start(f32[136,128]{1,0:T(8,128)S(1)} %add.5.refs_0_), channel_id=1, source_target_pairs={{0,24},{1,25},{2,26},{3,27},{4,28},{5,29},{6,30},{7,31},{8,0},{9,1... | collective-permute-start | bytes 208904 | tf_op jit(solution)/shard_map/ppermute | solution.py:418
  129.4 0.8 collective-permute-start.11
  130.3 3.3 %collective-permute-done.12.refs_2_ = f32[136,128]{1,0:T(8,128)S(1)} collective-permute-done((f32[136,128]{1,0:T(8,128)S(1)}, f32[136,128]{1,0:T(8,128)S(1)}, u32[]{:S(2)}, u32[]{:S(2)}) %collective-permute-start.12) | collective-permute-done | bytes 69664 | tf_op jit(solution)/shard_map/ppermute | solution.py:418
  133.6 0.7 collective-permute-done.11.refs_1_
  134.4 8.1 %collective-permute-start.15 = (f32[136,128]{1,0:T(8,128)S(1)}, f32[136,128]{1,0:T(8,128)S(1)}, u32[]{:S(2)}, u32[]{:S(2)}) collective-permute-start(f32[136,128]{1,0:T(8,128)S(1)} %add.6.refs_0_), channel_id=1, source_target_pairs={{0,64},{1,65},{2,66},{3,67},{4,68},{5,69},{6,70},{7,71},{8,72},{9,... | collective-permute-start | bytes 208904 | tf_op jit(solution)/shard_map/ppermute | solution.py:418
  142.5 1.7 %collective-permute-done.15.refs_2_ = f32[136,128]{1,0:T(8,128)S(1)} collective-permute-done((f32[136,128]{1,0:T(8,128)S(1)}, f32[136,128]{1,0:T(8,128)S(1)}, u32[]{:S(2)}, u32[]{:S(2)}) %collective-permute-start.15) | collective-permute-done | bytes 69664 | tf_op jit(solution)/shard_map/ppermute | solution.py:418
  144.2 3.4 %collective-permute-done.14.refs_1_ = f32[136,128]{1,0:T(8,128)S(1)} collective-permute-done((f32[136,128]{1,0:T(8,128)S(1)}, f32[136,128]{1,0:T(8,128)S(1)}, u32[]{:S(2)}, u32[]{:S(2)}) %collective-permute-start.14) | collective-permute-done | bytes 69664 | tf_op jit(solution)/shard_map/ppermute | solution.py:418
  147.6 3.4 %collective-permute-start.17 = (f32[136,128]{1,0:T(8,128)S(1)}, f32[136,128]{1,0:T(8,128)S(1)}, u32[]{:S(2)}, u32[]{:S(2)}) collective-permute-start(f32[136,128]{1,0:T(8,128)S(1)} %add.7.mine), channel_id=1, source_target_pairs={{0,1},{1,0},{2,3},{3,2},{4,5},{5,4},{6,7},{7,6},{8,9},{9,8},{10,11... | collective-permute-start | bytes 208904 | tf_op jit(solution)/shard_map/ppermute | solution.py:418
  151.0 0.9 collective-permute-done.17.other
  152.0 16.0 %rotate.1 = f32[6144,256]{1,0:T(8,128)} custom-call(s32[128]{0:T(128)S(1)} %copy-done.2, s32[1]{0:T(128)} %bitcast.position.refs_1_, f32[136,128]{1,0:T(8,128)S(1)} %add.7.mine, f32[136,128]{1,0:T(8,128)S(1)} %collective-permute-done.17.other, f32[12288,128]{1,0:T(8,128)S(1)} %get-tuple-element.100.w), custom_call_target="tpu_custom_call" | custom-call | tf_op jit(solution)/shard_map/rotate/pallas_call | solution.py:45
  (38 shorter events, 3.0 us)
Async XLA Ops:
  0.7 0.7 copy-start.1
  1.4 9.5 %copy-start.3 = (s32[16,512]{1,0:T(8,128)S(1)}, s32[16,512]{1,0:T(8,128)}, u32[]{:S(2)}) copy-start(s32[16,512]{1,0:T(8,128)} %param.10) | copy-start | bytes 98308
  5.8 10.5 %collective-permute-start = (f32[776,128]{1,0:T(8,128)S(1)}, f32[776,128]{1,0:T(8,128)S(1)}, u32[]{:S(2)}, u32[]{:S(2)}) collective-permute-start(f32[776,128]{1,0:T(8,128)S(1)} %get-tuple-element.53), channel_id=1, source_target_pairs={{0,1},{1,2},{2,3},{3,4},{4,5},{5,6},{6,7},{7,8},{8,9},{9,10},{10,1... | collective-permute-start | bytes 1191944 | tf_op jit(solution)/shard_map/ppermute | solution.py:25
  28.2 8.3 %copy-start = (f32[12288,128]{1,0:T(8,128)}, f32[12288,128]{1,0:T(8,128)S(1)}, u32[]{:S(2)}) copy-start(f32[12288,128]{1,0:T(8,128)S(1)} %get-tuple-element.64.refs_0_.refs_2_) | copy-start | bytes 18874372
  28.3 8.3 %collective-permute-start.2 = (f32[768,128]{1,0:T(8,128)S(1)}, f32[768,128]{1,0:T(8,128)S(1)}, u32[]{:S(2)}, u32[]{:S(2)}) collective-permute-start(f32[768,128]{1,0:T(8,128)S(1)} %get-tuple-element.62), channel_id=1, source_target_pairs={{0,1},{1,0},{2,3},{3,2},{4,5},{5,4},{6,7},{7,6},{8,9},{9,8},{10,11... | collective-permute-start | bytes 1179656 | tf_op jit(solution)/shard_map/ppermute | solution.py:566
  28.3 9.9 %collective-permute-start.1 = (f32[768,128]{1,0:T(8,128)S(1)}, f32[768,128]{1,0:T(8,128)S(1)}, u32[]{:S(2)}, u32[]{:S(2)}) collective-permute-start(f32[768,128]{1,0:T(8,128)S(1)} %get-tuple-element.61), channel_id=1, source_target_pairs={{1,2},{2,1},{3,4},{4,3},{5,6},{6,5},{7,8},{8,7},{9,10},{10,9},{11,... | collective-permute-start | bytes 1179656 | tf_op jit(solution)/shard_map/ppermute | solution.py:562
  36.5 25.7 %slice-start = ((s8[6291456]{0:T(1024)(128)(4,1)}), s8[4194304]{0:T(1024)(128)(4,1)S(1)}, s32[]{:S(2)}) async-start(s8[6291456]{0:T(1024)(128)(4,1)} %bitcast.5), calls=%async_computation | async-start | bytes 8388608
  38.2 24.1 %slice-start.1 = ((s8[6291456]{0:T(1024)(128)(4,1)}), s8[2097152]{0:T(1024)(128)(4,1)S(1)}, s32[]{:S(2)}) async-start(s8[6291456]{0:T(1024)(128)(4,1)} %bitcast.5), calls=%async_computation.1 | async-start | bytes 4194304
  50.3 15.6 %collective-permute-start.4 = (f32[768,128]{1,0:T(8,128)S(1)}, f32[768,128]{1,0:T(8,128)S(1)}, u32[]{:S(2)}, u32[]{:S(2)}) collective-permute-start(f32[768,128]{1,0:T(8,128)S(1)} %get-tuple-element.75), channel_id=1, source_target_pairs={{0,1},{1,0},{2,3},{3,2},{4,5},{5,4},{6,7},{7,6},{8,9},{9,8},{10,11... | collective-permute-start | bytes 1179656 | tf_op jit(solution)/shard_map/ppermute | solution.py:566
  50.4 17.3 %collective-permute-start.3 = (f32[768,128]{1,0:T(8,128)S(1)}, f32[768,128]{1,0:T(8,128)S(1)}, u32[]{:S(2)}, u32[]{:S(2)}) collective-permute-start(f32[768,128]{1,0:T(8,128)S(1)} %get-tuple-element.74), channel_id=1, source_target_pairs={{1,2},{2,1},{3,4},{4,3},{5,6},{6,5},{7,8},{8,7},{9,10},{10,9},{11,... | collective-permute-start | bytes 1179656 | tf_op jit(solution)/shard_map/ppermute | solution.py:562
  79.8 21.1 %collective-permute-start.5 = (f32[768,128]{1,0:T(8,128)S(1)}, f32[768,128]{1,0:T(8,128)S(1)}, u32[]{:S(2)}, u32[]{:S(2)}) collective-permute-start(f32[768,128]{1,0:T(8,128)S(1)} %get-tuple-element.87), channel_id=1, source_target_pairs={{0,1},{1,0},{2,3},{3,2},{4,5},{5,4},{6,7},{7,6},{8,9},{9,8},{10,11... | collective-permute-start | bytes 1179656 | tf_op jit(solution)/shard_map/ppermute | solution.py:566
  79.9 21.1 %collective-permute-start.6 = (f32[768,128]{1,0:T(8,128)S(1)}, f32[768,128]{1,0:T(8,128)S(1)}, u32[]{:S(2)}, u32[]{:S(2)}) collective-permute-start(f32[768,128]{1,0:T(8,128)S(1)} %get-tuple-element.88), channel_id=1, source_target_pairs={{1,2},{2,1},{3,4},{4,3},{5,6},{6,5},{7,8},{8,7},{9,10},{10,9},{11,... | collective-permute-start | bytes 1179656 | tf_op jit(solution)/shard_map/ppermute | solution.py:562
  92.4 3.6 %copy-start.2 = (s32[128]{0:T(128)S(1)}, s32[128]{0:T(128)}, u32[]{:S(2)}) copy-start(s32[128]{0:T(128)} %counts.3) | copy-start | bytes 1540
  103.5 1.3 collective-permute-start.7
  104.9 15.6 %collective-permute-start.10 = (f32[136,128]{1,0:T(8,128)S(1)}, f32[136,128]{1,0:T(8,128)S(1)}, u32[]{:S(2)}, u32[]{:S(2)}) collective-permute-start(f32[136,128]{1,0:T(8,128)S(1)} %add.4.refs_0_), channel_id=1, source_target_pairs={{0,6},{1,7},{2,0},{3,1},{4,2},{5,3},{6,4},{7,5},{8,14},{9,15},{10,... | collective-permute-start | bytes 208904 | tf_op jit(solution)/shard_map/ppermute | solution.py:418
  119.1 4.7 %collective-permute-start.9 = (f32[136,128]{1,0:T(8,128)S(1)}, f32[136,128]{1,0:T(8,128)S(1)}, u32[]{:S(2)}, u32[]{:S(2)}) collective-permute-start(f32[136,128]{1,0:T(8,128)S(1)} %add.4.refs_0_), channel_id=1, source_target_pairs={{0,4},{1,5},{2,6},{3,7},{4,0},{5,1},{6,2},{7,3},{8,12},{9,13},{10,... | collective-permute-start | bytes 208904 | tf_op jit(solution)/shard_map/ppermute | solution.py:418
  119.6 6.5 %collective-permute-start.8 = (f32[136,128]{1,0:T(8,128)S(1)}, f32[136,128]{1,0:T(8,128)S(1)}, u32[]{:S(2)}, u32[]{:S(2)}) collective-permute-start(f32[136,128]{1,0:T(8,128)S(1)} %add.4.refs_0_), channel_id=1, source_target_pairs={{0,2},{1,3},{2,4},{3,5},{4,6},{5,7},{6,0},{7,1},{8,10},{9,11},{10,... | collective-permute-start | bytes 208904 | tf_op jit(solution)/shard_map/ppermute | solution.py:418
  126.1 4.1 %collective-permute-start.13 = (f32[136,128]{1,0:T(8,128)S(1)}, f32[136,128]{1,0:T(8,128)S(1)}, u32[]{:S(2)}, u32[]{:S(2)}) collective-permute-start(f32[136,128]{1,0:T(8,128)S(1)} %add.5.refs_0_), channel_id=1, source_target_pairs={{0,24},{1,25},{2,26},{3,27},{4,28},{5,29},{6,30},{7,31},{8,0},{9,1... | collective-permute-start | bytes 208904 | tf_op jit(solution)/shard_map/ppermute | solution.py:418
  128.9 4.7 %collective-permute-start.12 = (f32[136,128]{1,0:T(8,128)S(1)}, f32[136,128]{1,0:T(8,128)S(1)}, u32[]{:S(2)}, u32[]{:S(2)}) collective-permute-start(f32[136,128]{1,0:T(8,128)S(1)} %add.5.refs_0_), channel_id=1, source_target_pairs={{0,16},{1,17},{2,18},{3,19},{4,20},{5,21},{6,22},{7,23},{8,24},{9,... | collective-permute-start | bytes 208904 | tf_op jit(solution)/shard_map/ppermute | solution.py:418
  129.4 4.9 %collective-permute-start.11 = (f32[136,128]{1,0:T(8,128)S(1)}, f32[136,128]{1,0:T(8,128)S(1)}, u32[]{:S(2)}, u32[]{:S(2)}) collective-permute-start(f32[136,128]{1,0:T(8,128)S(1)} %add.5.refs_0_), channel_id=1, source_target_pairs={{0,8},{1,9},{2,10},{3,11},{4,12},{5,13},{6,14},{7,15},{8,16},{9,17... | collective-permute-start | bytes 208904 | tf_op jit(solution)/shard_map/ppermute | solution.py:418
  134.3 8.2 %collective-permute-start.16 = (f32[136,128]{1,0:T(8,128)S(1)}, f32[136,128]{1,0:T(8,128)S(1)}, u32[]{:S(2)}, u32[]{:S(2)}) collective-permute-start(f32[136,128]{1,0:T(8,128)S(1)} %add.6.refs_0_), channel_id=1, source_target_pairs={{0,96},{1,97},{2,98},{3,99},{4,100},{5,101},{6,102},{7,103},{8,104... | collective-permute-start | bytes 208904 | tf_op jit(solution)/shard_map/ppermute | solution.py:418
  134.4 9.8 %collective-permute-start.15 = (f32[136,128]{1,0:T(8,128)S(1)}, f32[136,128]{1,0:T(8,128)S(1)}, u32[]{:S(2)}, u32[]{:S(2)}) collective-permute-start(f32[136,128]{1,0:T(8,128)S(1)} %add.6.refs_0_), channel_id=1, source_target_pairs={{0,64},{1,65},{2,66},{3,67},{4,68},{5,69},{6,70},{7,71},{8,72},{9,... | collective-permute-start | bytes 208904 | tf_op jit(solution)/shard_map/ppermute | solution.py:418
  142.5 5.1 %collective-permute-start.14 = (f32[136,128]{1,0:T(8,128)S(1)}, f32[136,128]{1,0:T(8,128)S(1)}, u32[]{:S(2)}, u32[]{:S(2)}) collective-permute-start(f32[136,128]{1,0:T(8,128)S(1)} %add.6.refs_0_), channel_id=1, source_target_pairs={{0,32},{1,33},{2,34},{3,35},{4,36},{5,37},{6,38},{7,39},{8,40},{9,... | collective-permute-start | bytes 208904 | tf_op jit(solution)/shard_map/ppermute | solution.py:418
  147.6 4.3 %collective-permute-start.17 = (f32[136,128]{1,0:T(8,128)S(1)}, f32[136,128]{1,0:T(8,128)S(1)}, u32[]{:S(2)}, u32[]{:S(2)}) collective-permute-start(f32[136,128]{1,0:T(8,128)S(1)} %add.7.mine), channel_id=1, source_target_pairs={{0,1},{1,0},{2,3},{3,2},{4,5},{5,4},{6,7},{7,6},{8,9},{9,8},{10,11... | collective-permute-start | bytes 208904 | tf_op jit(solution)/shard_map/ppermute | solution.py:418
